TPU v7x, 32 devices: a whole 2x2x4 slice. The times are simulated.
32 devices in a mesh: seq: 2 (over x), fsdp: 16 (over z, y, core).
Axes of the slice: x: 2, y: 2, z: 4, core: 2. Of those that a mesh axis runs over, the one named last changes fastest.
Arguments:
- inputs: bfloat16 [16, 1024, 1024], P('fsdp', 'seq'), may hold values from -6 to 6
- ln_gain: bfloat16 [1024], P('fsdp'), may hold values from 0.5 to 1.5
- ln_shift: bfloat16 [1024], P('fsdp'), may hold values from -1.75 to 1.75
- w_query: bfloat16 [1024, 1024], P('fsdp'), may hold values from -0.1875 to 0.1875
- w_key: bfloat16 [1024, 1024], P('fsdp'), may hold values from -0.1875 to 0.1875
- w_value: bfloat16 [1024, 1024], P('fsdp'), may hold values from -0.1875 to 0.1875
- w_output: bfloat16 [1024, 1024], P('fsdp'), may hold values from -0.75 to 0.75
- exp_gain1: bfloat16 [16, 512], P('fsdp'), may hold values from 0.5 to 1.5
- exp_shift1: bfloat16 [16, 512], P('fsdp'), may hold values from -1.75 to 1.75
- w_in1: bfloat16 [16, 2048, 1024], P('fsdp', 'seq'), may hold values from -0.1875 to 0.1875
- b_in1: bfloat16 [16, 2048], P('fsdp'), may hold values from -1.75 to 1.75
- w_out1: bfloat16 [16, 2048, 1024], P('fsdp', 'seq'), may hold values from -0.1875 to 0.1875
- b_out1: bfloat16 [16, 512], P('fsdp'), may hold values from -1.75 to 1.75
- exp_gain2: bfloat16 [16, 512], P('fsdp'), may hold values from 0.5 to 1.5
- exp_shift2: bfloat16 [16, 512], P('fsdp'), may hold values from -1.75 to 1.75
- w_in2: bfloat16 [16, 2048, 1024], P('fsdp', 'seq'), may hold values from -0.1875 to 0.1875
- b_in2: bfloat16 [16, 2048], P('fsdp'), may hold values from -1.75 to 1.75
- w_out2: bfloat16 [16, 2048, 1024], P('fsdp', 'seq'), may hold values from -0.1875 to 0.1875
- b_out2: bfloat16 [16, 512], P('fsdp'), may hold values from -1.75 to 1.75
- centroid: bfloat16 [16, 512], P('fsdp'), may hold values from -0.125 to 0.125
- order: int32 [16, 1024], P('fsdp', 'seq'), may hold values from 0 to 511, as said below
- inverse: int32 [16, 1024], P('fsdp', 'seq'), may hold values from 0 to 511, as said below
- cotangent: bfloat16 [16, 1024, 1024], P('fsdp', 'seq'), may hold values from -6 to 6
Outputs:
- layer_out: bfloat16 [16, 1024, 1024], P('fsdp', 'seq')
- grad_inputs: float32 [16, 1024, 1024], P('fsdp', 'seq')
- grad_ln_gain: float32 [1024], P('fsdp')
- grad_ln_shift: float32 [1024], P('fsdp')
- grad_w_query: float32 [1024, 1024], P('fsdp')
- grad_w_key: float32 [1024, 1024], P('fsdp')
- grad_w_value: float32 [1024, 1024], P('fsdp')
- grad_w_output: float32 [1024, 1024], P('fsdp')
- grad_exp_gain1: float32 [16, 512], P('fsdp')
- grad_exp_shift1: float32 [16, 512], P('fsdp')
- grad_w_in1: float32 [16, 2048, 1024], P('fsdp', 'seq')
- grad_b_in1: float32 [16, 2048], P('fsdp')
- grad_w_out1: float32 [16, 2048, 1024], P('fsdp', 'seq')
- grad_b_out1: float32 [16, 512], P('fsdp')
- grad_exp_gain2: float32 [16, 512], P('fsdp')
- grad_exp_shift2: float32 [16, 512], P('fsdp')
- grad_w_in2: float32 [16, 2048, 1024], P('fsdp', 'seq')
- grad_b_in2: float32 [16, 2048], P('fsdp')
- grad_w_out2: float32 [16, 2048, 1024], P('fsdp', 'seq')
- grad_b_out2: float32 [16, 512], P('fsdp')
- grad_centroid: float32 [16, 512], P('fsdp')
Inputs may be any that keep to these rules, and one draw needn't show every extreme that they name: `order`: within each row, every aligned block of 512 places holds each of 0 to 511 once, so every expert receives exactly 64 tokens of every block and 2048 in all. Within each aligned block of 512 places, the inverse of order: order[b, inverse[b, p]] = p.
All inputs are finite; a program needn't handle non-finite values.
Results may differ from a plain program's by a relative error of at most 0.018.
Values may be sent and summed in bfloat16 or wider, within the bound.
A program may use at most 384 MiB of HBM per device.

v0:
```python
import jax
import jax.numpy as jnp
from jax import lax
from jax.sharding import PartitionSpec as P

HEADS = 16


epsilon = 1e-05
masked = -1e30


def swapped(value, axis, bit):
    mask = 2**bit
    pairs = [(source, source ^ mask) for source in range(lax.axis_size(axis))]
    return lax.ppermute(value, axis, pairs)


def layer_norm(values, gain_row, shift_row):
    row_mean = jnp.mean(values, axis=-1, keepdims=True)
    centred = values - row_mean
    spread = jnp.mean(centred * centred, axis=-1, keepdims=True)
    return centred * lax.rsqrt(spread + epsilon) * gain_row + shift_row


def exact_gelu(values):
    return jax.nn.gelu(values, approximate=False)


def attention_scores(query_heads, key_heads, first_place):
    scale = query_heads.shape[2] ** (-0.5)
    scores = (
        jnp.einsum("qhd,khd->hqk", query_heads, key_heads, preferred_element_type=jnp.float32)
        * scale
    )
    query_places = first_place + lax.iota(jnp.int32, query_heads.shape[0])
    key_places = lax.iota(jnp.int32, key_heads.shape[0])
    causal = key_places[None, :] <= query_places[:, None]
    return jnp.where(causal[None], scores, masked)


def holders_gather(stack):
    partner_piece = swapped(stack, "fsdp", 0)
    paired = jnp.concatenate([stack, partner_piece], axis=1)
    return lax.all_gather(paired, "seq", axis=1, tiled=True)


def holders_sum(stack):
    seq_share = lax.psum_scatter(
        stack.astype(jnp.bfloat16), "seq", scatter_dimension=1, tiled=True
    ).astype(jnp.float32)
    half = seq_share.shape[1] // 2
    incoming = swapped(seq_share[:, half:].astype(jnp.bfloat16), "fsdp", 0).astype(jnp.float32)
    return seq_share[:, :half] + incoming


def contract_last(left, right):
    return lax.dot_general(
        left, right, (((1,), (1,)), ((), ())), preferred_element_type=jnp.float32
    )


def contract_first(left, right):
    return lax.dot_general(
        left, right, (((0,), (0,)), ((), ())), preferred_element_type=jnp.float32
    )


def sublayer_forward(
    token_rows, gain_row, shift_row, in_rows, in_bias, out_rows, out_bias, spread, merge
):
    normed, norm_pull = jax.vjp(layer_norm, token_rows, gain_row, shift_row)
    normed_low = spread(normed.astype(jnp.bfloat16))
    inner_sum = contract_last(normed_low, in_rows) + in_bias
    active, gelu_pull = jax.vjp(exact_gelu, inner_sum)
    active_low = active.astype(jnp.bfloat16)
    output = merge(jnp.dot(active_low, out_rows, preferred_element_type=jnp.float32)) + out_bias
    return (output, (norm_pull, normed_low, gelu_pull, active_low))


def sublayer_backward(grad_low, kept, in_rows, out_rows, spread, merge):
    norm_pull, normed_low, gelu_pull, active_low = kept
    grad_all = spread(grad_low)
    grad_w_out = contract_first(active_low, grad_all)
    grad_active = contract_last(grad_all, out_rows)
    grad_inner = gelu_pull(grad_active)[0].astype(jnp.bfloat16)
    grad_bias = jnp.sum(grad_inner.astype(jnp.float32), axis=0)
    grad_w_in = contract_first(grad_inner, normed_low)
    grad_normed = merge(jnp.dot(grad_inner, in_rows, preferred_element_type=jnp.float32))
    grad_rows, grad_gain, grad_shift = norm_pull(grad_normed)
    return (grad_rows, grad_gain, grad_shift, grad_bias, grad_w_in, grad_w_out)


def pair_order(table, peer, partner, seq_count):
    own_row = lax.dynamic_slice_in_dim(table, peer, 1, 0)[0].reshape(seq_count, 1, -1)
    other_row = lax.dynamic_slice_in_dim(table, partner, 1, 0)[0].reshape(seq_count, 1, -1)
    return jnp.concatenate([own_row, other_row], axis=1).reshape(-1).astype(jnp.float32)


def vector_table(vector, count, pair_base):
    empty = jnp.zeros((count, vector.shape[0] // 2), jnp.float32)
    return lax.dynamic_update_slice(empty, vector.reshape(2, -1), (pair_base, 0))


def bias_table(own_row, other_row, count, peer, partner):
    empty = jnp.zeros((count, own_row.shape[0]), jnp.float32)
    filled = lax.dynamic_update_slice(empty, own_row[None], (peer, 0))
    return lax.dynamic_update_slice(filled, other_row[None], (partner, 0))


def body(
    inputs,
    ln_gain,
    ln_shift,
    w_query,
    w_key,
    w_value,
    w_output,
    exp_gain1,
    exp_shift1,
    w_in1,
    b_in1,
    w_out1,
    b_out1,
    exp_gain2,
    exp_shift2,
    w_in2,
    b_in2,
    w_out2,
    b_out2,
    centroid,
    order,
    inverse,
    cotangent,
):
    params = (
        lax.all_gather(ln_gain, "fsdp", axis=0, tiled=True),
        lax.all_gather(ln_shift, "fsdp", axis=0, tiled=True),
        lax.all_gather(w_query, "fsdp", axis=0, tiled=True),
        lax.all_gather(w_key, "fsdp", axis=0, tiled=True),
        lax.all_gather(w_value, "fsdp", axis=0, tiled=True),
        lax.all_gather(w_output, "fsdp", axis=0, tiled=True),
        lax.all_gather(exp_gain1, "fsdp", axis=0, tiled=True),
        lax.all_gather(exp_shift1, "fsdp", axis=0, tiled=True),
        lax.all_gather(b_in1, "fsdp", axis=0, tiled=True),
        lax.all_gather(b_out1, "fsdp", axis=0, tiled=True),
        lax.all_gather(exp_gain2, "fsdp", axis=0, tiled=True),
        lax.all_gather(exp_shift2, "fsdp", axis=0, tiled=True),
        lax.all_gather(b_in2, "fsdp", axis=0, tiled=True),
        lax.all_gather(b_out2, "fsdp", axis=0, tiled=True),
        lax.all_gather(centroid, "fsdp", axis=0, tiled=True),
    )
    gain_all, shift_all, query_full, key_full, value_full, output_full = (
        params[0],
        params[1],
        params[2],
        params[3],
        params[4],
        params[5],
    )
    token_rows = inputs[0].astype(jnp.float32)
    tokens = token_rows.shape[0]
    feature_count = token_rows.shape[1]
    head_count = HEADS
    head_size = feature_count // head_count
    scale = head_size ** (-0.5)
    normed, norm_pull = jax.vjp(
        layer_norm, token_rows, gain_all.astype(jnp.float32), shift_all.astype(jnp.float32)
    )
    normed_low = normed.astype(jnp.bfloat16)
    query_low = jnp.dot(normed_low, query_full, preferred_element_type=jnp.float32).astype(
        jnp.bfloat16
    )
    keys_local = jnp.dot(normed_low, key_full, preferred_element_type=jnp.float32).astype(
        jnp.bfloat16
    )
    values_local = jnp.dot(normed_low, value_full, preferred_element_type=jnp.float32).astype(
        jnp.bfloat16
    )
    keys_all, values_all = (
        lax.all_gather(keys_local, "seq", axis=0, tiled=True),
        lax.all_gather(values_local, "seq", axis=0, tiled=True),
    )
    first_place = lax.axis_index("seq") * tokens
    query_heads = query_low.reshape(tokens, head_count, head_size)
    key_heads = keys_all.reshape(-1, head_count, head_size)
    value_heads = values_all.reshape(-1, head_count, head_size)
    scores = attention_scores(query_heads, key_heads, first_place)
    row_peak = jnp.max(scores, axis=-1, keepdims=True)
    exponent = jnp.exp(scores - row_peak)
    row_total = jnp.sum(exponent, axis=-1, keepdims=True)
    log_total = row_peak + jnp.log(row_total)
    attention_low = (exponent / row_total).astype(jnp.bfloat16)
    mixed_heads = jnp.einsum(
        "hqk,khd->qhd", attention_low, value_heads, preferred_element_type=jnp.float32
    )
    mixed_low = mixed_heads.reshape(tokens, feature_count).astype(jnp.bfloat16)
    middle = token_rows + jnp.dot(mixed_low, output_full, preferred_element_type=jnp.float32)
    peer_count = lax.axis_size("fsdp")
    seq_count = lax.axis_size("seq")
    per_peer = tokens // peer_count
    peer = lax.axis_index("fsdp")
    partner = jnp.bitwise_xor(peer, 1)
    pair_base = peer - peer % 2
    quarter = w_in1.shape[1]

    def expert_vector(table):
        return lax.dynamic_slice_in_dim(table, pair_base, 2, 0).reshape(-1).astype(jnp.float32)

    gain_one = expert_vector(params[6])
    shift_one = expert_vector(params[7])
    out_bias_one = expert_vector(params[9])
    gain_two = expert_vector(params[10])
    shift_two = expert_vector(params[11])
    out_bias_two = expert_vector(params[13])
    centre = expert_vector(params[14])
    full = holders_gather(jnp.stack([w_in1[0], w_out1[0], w_in2[0], w_out2[0]]))
    in_one, out_one, in_two, out_two = (full[0], full[1], full[2], full[3])
    bias_one = pair_order(params[8], peer, partner, seq_count)
    bias_two = pair_order(params[12], peer, partner, seq_count)

    def spread(values):
        return values

    def merge(values):
        return values

    sent_rows = middle.astype(jnp.bfloat16)
    slot_rows = jnp.take(sent_rows, order[0], axis=0).reshape(peer_count, per_peer, feature_count)
    back_slots = jnp.take(cotangent[0], order[0], axis=0).reshape(
        peer_count, per_peer, feature_count
    )
    arrived, arrived_grads = (
        lax.all_to_all(slot_rows, "fsdp", split_axis=0, concat_axis=0, tiled=True),
        lax.all_to_all(back_slots, "fsdp", split_axis=0, concat_axis=0, tiled=True),
    )
    arrived_wide = arrived.reshape(tokens, feature_count).astype(jnp.float32)
    grad_gated = arrived_grads.reshape(tokens, feature_count).astype(jnp.float32)
    first, kept_one = sublayer_forward(
        arrived_wide, gain_one, shift_one, in_one, bias_one, out_one, out_bias_one, spread, merge
    )
    second, kept_two = sublayer_forward(
        arrived_wide + first,
        gain_two,
        shift_two,
        in_two,
        bias_two,
        out_two,
        out_bias_two,
        spread,
        merge,
    )
    branch = first + second
    gate_value = jax.nn.sigmoid(jnp.sum(arrived_wide * centre, axis=-1, keepdims=True))
    gated_rows = (gate_value * branch).astype(jnp.bfloat16)
    returned = lax.all_to_all(
        gated_rows.reshape(peer_count, per_peer, feature_count),
        "fsdp",
        split_axis=0,
        concat_axis=0,
        tiled=True,
    )
    home_rows = jnp.take(returned.reshape(tokens, feature_count), inverse[0], axis=0)
    result = middle + home_rows.astype(jnp.float32)
    grad_gate = jnp.sum(grad_gated * branch, axis=-1, keepdims=True)
    grad_second_low = (gate_value * grad_gated).astype(jnp.bfloat16)
    back_two = sublayer_backward(grad_second_low, kept_two, in_two, out_two, spread, merge)
    grad_bout_two = jnp.sum(grad_second_low.astype(jnp.float32), axis=0)
    grad_second_in = back_two[0]
    grad_first_low = (gate_value * grad_gated + grad_second_in).astype(jnp.bfloat16)
    back_one = sublayer_backward(grad_first_low, kept_one, in_one, out_one, spread, merge)
    grad_bout_one = jnp.sum(grad_first_low.astype(jnp.float32), axis=0)
    grad_score = grad_gate * gate_value * (1.0 - gate_value)
    grad_centre = jnp.sum(grad_score * arrived_wide, axis=0)
    grad_sent = (grad_second_in + back_one[0] + grad_score * centre).astype(jnp.bfloat16)
    coming = lax.all_to_all(
        grad_sent.reshape(peer_count, per_peer, feature_count),
        "fsdp",
        split_axis=0,
        concat_axis=0,
        tiled=True,
    )
    upstream = cotangent[0].astype(jnp.float32)
    grad_middle = upstream + jnp.take(
        coming.reshape(tokens, feature_count), inverse[0], axis=0
    ).astype(jnp.float32)
    reduced = holders_sum(jnp.stack([back_one[4], back_one[5], back_two[4], back_two[5]]))
    grad_win_one, grad_wout_one, grad_win_two, grad_wout_two = (
        reduced[0],
        reduced[1],
        reduced[2],
        reduced[3],
    )
    split_one = back_one[3].reshape(seq_count, 2, quarter)
    split_two = back_two[3].reshape(seq_count, 2, quarter)
    bias_rows_one = (split_one[:, 0].reshape(-1), split_one[:, 1].reshape(-1))
    bias_rows_two = (split_two[:, 0].reshape(-1), split_two[:, 1].reshape(-1))
    grad_attn = grad_middle.astype(jnp.bfloat16)
    grad_wo = jnp.dot(mixed_low.T, grad_attn, preferred_element_type=jnp.float32)
    grad_mixed = jnp.dot(grad_attn, output_full.T, preferred_element_type=jnp.float32).astype(
        jnp.bfloat16
    )
    grad_mixed = grad_mixed.reshape(tokens, head_count, head_size)
    scores_again = attention_scores(query_heads, key_heads, first_place)
    attention_full = jnp.exp(scores_again - log_total)
    grad_probs = jnp.einsum(
        "qhd,khd->hqk", grad_mixed, value_heads, preferred_element_type=jnp.float32
    )
    row_inner = jnp.sum(grad_probs * attention_full, axis=-1, keepdims=True)
    grad_scores = (attention_full * (grad_probs - row_inner)).astype(jnp.bfloat16)
    grad_query = (
        jnp.einsum("hqk,khd->qhd", grad_scores, key_heads, preferred_element_type=jnp.float32)
        * scale
    )
    grad_query = grad_query.reshape(tokens, feature_count).astype(jnp.bfloat16)
    keys_part = (
        jnp.einsum("hqk,qhd->khd", grad_scores, query_heads, preferred_element_type=jnp.float32)
        * scale
    )
    values_part = jnp.einsum(
        "hqk,qhd->khd", attention_low, grad_mixed, preferred_element_type=jnp.float32
    )
    grad_keys, grad_values = (
        lax.psum_scatter(
            keys_part.reshape(-1, feature_count).astype(jnp.bfloat16),
            "seq",
            scatter_dimension=0,
            tiled=True,
        ).astype(jnp.float32),
        lax.psum_scatter(
            values_part.reshape(-1, feature_count).astype(jnp.bfloat16),
            "seq",
            scatter_dimension=0,
            tiled=True,
        ).astype(jnp.float32),
    )
    grad_keys = grad_keys.astype(jnp.bfloat16)
    grad_values = grad_values.astype(jnp.bfloat16)
    grad_wq = jnp.dot(normed_low.T, grad_query, preferred_element_type=jnp.float32)
    grad_wk = jnp.dot(normed_low.T, grad_keys, preferred_element_type=jnp.float32)
    grad_wv = jnp.dot(normed_low.T, grad_values, preferred_element_type=jnp.float32)
    grad_normed = jnp.dot(grad_query, query_full.T, preferred_element_type=jnp.float32)
    grad_normed = grad_normed + jnp.dot(grad_keys, key_full.T, preferred_element_type=jnp.float32)
    grad_normed = grad_normed + jnp.dot(
        grad_values, value_full.T, preferred_element_type=jnp.float32
    )
    grad_rows, grad_gain, grad_shift = norm_pull(grad_normed)
    grad_inputs = grad_middle + grad_rows
    shards = (
        lax.psum_scatter(grad_gain, "fsdp", scatter_dimension=0, tiled=True),
        lax.psum_scatter(grad_shift, "fsdp", scatter_dimension=0, tiled=True),
        lax.psum_scatter(grad_wq, "fsdp", scatter_dimension=0, tiled=True),
        lax.psum_scatter(grad_wk, "fsdp", scatter_dimension=0, tiled=True),
        lax.psum_scatter(grad_wv, "fsdp", scatter_dimension=0, tiled=True),
        lax.psum_scatter(grad_wo, "fsdp", scatter_dimension=0, tiled=True),
        lax.psum_scatter(
            vector_table(back_one[1], peer_count, pair_base),
            "fsdp",
            scatter_dimension=0,
            tiled=True,
        ),
        lax.psum_scatter(
            vector_table(back_one[2], peer_count, pair_base),
            "fsdp",
            scatter_dimension=0,
            tiled=True,
        ),
        lax.psum_scatter(
            bias_table(bias_rows_one[0], bias_rows_one[1], peer_count, peer, partner),
            "fsdp",
            scatter_dimension=0,
            tiled=True,
        ),
        lax.psum_scatter(
            vector_table(grad_bout_one, peer_count, pair_base),
            "fsdp",
            scatter_dimension=0,
            tiled=True,
        ),
        lax.psum_scatter(
            vector_table(back_two[1], peer_count, pair_base),
            "fsdp",
            scatter_dimension=0,
            tiled=True,
        ),
        lax.psum_scatter(
            vector_table(back_two[2], peer_count, pair_base),
            "fsdp",
            scatter_dimension=0,
            tiled=True,
        ),
        lax.psum_scatter(
            bias_table(bias_rows_two[0], bias_rows_two[1], peer_count, peer, partner),
            "fsdp",
            scatter_dimension=0,
            tiled=True,
        ),
        lax.psum_scatter(
            vector_table(grad_bout_two, peer_count, pair_base),
            "fsdp",
            scatter_dimension=0,
            tiled=True,
        ),
        lax.psum_scatter(
            vector_table(grad_centre, peer_count, pair_base),
            "fsdp",
            scatter_dimension=0,
            tiled=True,
        ),
    )
    summed = (
        lax.psum(shards[0].astype(jnp.bfloat16), "seq").astype(jnp.float32),
        lax.psum(shards[1].astype(jnp.bfloat16), "seq").astype(jnp.float32),
        lax.psum(shards[2].astype(jnp.bfloat16), "seq").astype(jnp.float32),
        lax.psum(shards[3].astype(jnp.bfloat16), "seq").astype(jnp.float32),
        lax.psum(shards[4].astype(jnp.bfloat16), "seq").astype(jnp.float32),
        lax.psum(shards[5].astype(jnp.bfloat16), "seq").astype(jnp.float32),
        lax.psum(shards[6].astype(jnp.bfloat16), "seq").astype(jnp.float32),
        lax.psum(shards[7].astype(jnp.bfloat16), "seq").astype(jnp.float32),
        lax.psum(shards[8].astype(jnp.bfloat16), "seq").astype(jnp.float32),
        lax.psum(shards[9].astype(jnp.bfloat16), "seq").astype(jnp.float32),
        lax.psum(shards[10].astype(jnp.bfloat16), "seq").astype(jnp.float32),
        lax.psum(shards[11].astype(jnp.bfloat16), "seq").astype(jnp.float32),
        lax.psum(shards[12].astype(jnp.bfloat16), "seq").astype(jnp.float32),
        lax.psum(shards[13].astype(jnp.bfloat16), "seq").astype(jnp.float32),
        lax.psum(shards[14].astype(jnp.bfloat16), "seq").astype(jnp.float32),
    )
    return (
        result.astype(jnp.bfloat16)[None],
        grad_inputs[None],
        summed[0],
        summed[1],
        summed[2],
        summed[3],
        summed[4],
        summed[5],
        summed[6],
        summed[7],
        grad_win_one[None],
        summed[8],
        grad_wout_one[None],
        summed[9],
        summed[10],
        summed[11],
        grad_win_two[None],
        summed[12],
        grad_wout_two[None],
        summed[13],
        summed[14],
    )


def solution(mesh):
    return jax.shard_map(
        body,
        mesh=mesh,
        in_specs=(
            P("fsdp", "seq", None),
            P("fsdp"),
            P("fsdp"),
            P("fsdp", None),
            P("fsdp", None),
            P("fsdp", None),
            P("fsdp", None),
            P("fsdp", None),
            P("fsdp", None),
            P("fsdp", "seq", None),
            P("fsdp", None),
            P("fsdp", "seq", None),
            P("fsdp", None),
            P("fsdp", None),
            P("fsdp", None),
            P("fsdp", "seq", None),
            P("fsdp", None),
            P("fsdp", "seq", None),
            P("fsdp", None),
            P("fsdp", None),
            P("fsdp", "seq"),
            P("fsdp", "seq"),
            P("fsdp", "seq", None),
        ),
        out_specs=(
            P("fsdp", "seq", None),
            P("fsdp", "seq", None),
            P("fsdp"),
            P("fsdp"),
            P("fsdp", None),
            P("fsdp", None),
            P("fsdp", None),
            P("fsdp", None),
            P("fsdp", None),
            P("fsdp", None),
            P("fsdp", "seq", None),
            P("fsdp", None),
            P("fsdp", "seq", None),
            P("fsdp", None),
            P("fsdp", None),
            P("fsdp", None),
            P("fsdp", "seq", None),
            P("fsdp", None),
            P("fsdp", "seq", None),
            P("fsdp", None),
            P("fsdp", None),
        ),
        check_vma=False,
    )
```

profile of v0, /device:TPU:0, one launch (start us, length us, event | category | flops | bytes accessed | tf_op | source)
XLA Modules:
  0.0 1680.6 jit_solution(18253575511281001507)
XLA Ops:
  21.1 39.2 %all-reduce.14 = (bf16[1024]{0:T(1024)(128)(2,1)S(1)}, bf16[1024]{0:T(1024)(128)(2,1)S(1)}) all-reduce(bf16[1024]{0:T(1024)(128)(2,1)S(1)} %dynamic-update-slice.1, bf16[1024]{0:T(1024)(128)(2,1)S(1)} %dynamic-update-slice), channel_id=1, replica_groups=mesh['seq'=2,'fsdp'=16] {'fsdp'}, use_global_device_ids=true, to_apply=%add.1 | all-reduce | flops 2048 | bytes 8192
  61.0 3.9 convolution_convert_fusion.5
  65.0 31.8 %all-gather.23.cloned.1.call-done = bf16[1024,1024]{1,0:T(8,128)(2,1)} async-done(((bf16[64,1024]{1,0:T(8,128)(2,1)}), bf16[1024,1024]{1,0:T(8,128)(2,1)}) %all-gather.23.cloned.1.call-update) | async-done | bytes 2097168 | tf_op jit(solution)/shard_map/all_gather | solution.py:140
  96.8 3.9 convolution_convert_fusion.3
  101.7 13.7 pad_maximum_fusion.1
  119.8 19.4 %all-gather.21.cloned.1.call-done = bf16[1024,1024]{1,0:T(8,128)(2,1)} async-done(((bf16[64,1024]{1,0:T(8,128)(2,1)}), bf16[1024,1024]{1,0:T(8,128)(2,1)}) %all-gather.21.cloned.1.call-update) | async-done | bytes 2097168 | tf_op jit(solution)/shard_map/all_gather | solution.py:139
  143.5 29.6 %all-gather.19.cloned.1.call-done = bf16[1024,1024]{1,0:T(8,128)(2,1)} async-done(((bf16[512,1024]{1,0:T(8,128)(2,1)}), bf16[1024,1024]{1,0:T(8,128)(2,1)}) %all-gather.19.cloned.1.call-update) | async-done | bytes 2097168 | tf_op jit(solution)/shard_map/all_gather | solution.py:182
  173.1 3.9 copy.56
  177.0 31.2 %all-gather.25.cloned.1.call-done = bf16[1024,1024]{1,0:T(8,128)(2,1)} async-done(((bf16[512,1024]{1,0:T(8,128)(2,1)}), bf16[1024,1024]{1,0:T(8,128)(2,1)}) %all-gather.25.cloned.1.call-update) | async-done | bytes 2097168 | tf_op jit(solution)/shard_map/all_gather | solution.py:181
  211.1 16.1 fusion.1
  227.2 15.9 fusion
  243.2 4.7 copy-done
  247.8 10.4 divide_convert_fusion
  258.3 18.1 %convolution_convert_fusion.2 = bf16[16,64,512]{2,1,0:T(8,128)(2,1)S(1)} fusion(bf16[1024,16,64]{0,2,1:T(8,128)(2,1)} %bitcast.242, bf16[16,512,1024]{2,1,0:T(8,128)(2,1)} %divide_convert_fusion), kind=kOutput, calls=%fused_computation.140 | convolution fusion | flops 1074266112 | bytes 19922944 | tf_op jit(solution)/shard_map/hqk,khd->qhd/dot_general | solution.py:194
  276.4 5.0 fusion.104
  287.2 5.6 all-to-all-start
  292.8 33.6 %all-gather.2 = bf16[16,1,512]{2,1,0:T(2,128)(2,1)S(1)} all-gather(bf16[1,1,512]{2,1,0:T(2,128)(2,1)S(1)} %bitcast.294), channel_id=1, replica_groups=mesh['seq'=2,'fsdp'=16] {'fsdp'}, dimensions={0}, use_global_device_ids=true | all-gather | bytes 17408 | tf_op jit(solution)/shard_map/all_gather | solution.py:144
  326.4 21.4 %all-gather = bf16[16,1,512]{2,1,0:T(2,128)(2,1)S(1)} all-gather(bf16[1,1,512]{2,1,0:T(2,128)(2,1)S(1)} %bitcast.295), channel_id=1, replica_groups=mesh['seq'=2,'fsdp'=16] {'fsdp'}, dimensions={0}, use_global_device_ids=true | all-gather | bytes 17408 | tf_op jit(solution)/shard_map/all_gather | solution.py:151
  347.8 17.5 %all-gather.1 = bf16[16,1,512]{2,1,0:T(2,128)(2,1)S(1)} all-gather(bf16[1,1,512]{2,1,0:T(2,128)(2,1)S(1)} %bitcast.296), channel_id=1, replica_groups=mesh['seq'=2,'fsdp'=16] {'fsdp'}, dimensions={0}, use_global_device_ids=true | all-gather | bytes 17408 | tf_op jit(solution)/shard_map/all_gather | solution.py:143
  365.3 18.8 %all-gather.4 = bf16[16,1,512]{2,1,0:T(2,128)(2,1)S(1)} all-gather(bf16[1,1,512]{2,1,0:T(2,128)(2,1)S(1)} %bitcast.297), channel_id=1, replica_groups=mesh['seq'=2,'fsdp'=16] {'fsdp'}, dimensions={0}, use_global_device_ids=true | all-gather | bytes 17408 | tf_op jit(solution)/shard_map/all_gather | solution.py:146
  384.2 17.5 %all-gather.5 = bf16[16,1,512]{2,1,0:T(2,128)(2,1)S(1)} all-gather(bf16[1,1,512]{2,1,0:T(2,128)(2,1)S(1)} %bitcast.298), channel_id=1, replica_groups=mesh['seq'=2,'fsdp'=16] {'fsdp'}, dimensions={0}, use_global_device_ids=true | all-gather | bytes 17408 | tf_op jit(solution)/shard_map/all_gather | solution.py:147
  401.7 18.8 %all-gather.6 = bf16[16,1,512]{2,1,0:T(2,128)(2,1)S(1)} all-gather(bf16[1,1,512]{2,1,0:T(2,128)(2,1)S(1)} %bitcast.299), channel_id=1, replica_groups=mesh['seq'=2,'fsdp'=16] {'fsdp'}, dimensions={0}, use_global_device_ids=true | all-gather | bytes 17408 | tf_op jit(solution)/shard_map/all_gather | solution.py:148
  420.5 17.8 %all-gather.7 = bf16[16,1,2048]{2,1,0:T(2,128)(2,1)S(1)} all-gather(bf16[1,1,2048]{2,1,0:T(2,128)(2,1)S(1)} %bitcast.283), channel_id=1, replica_groups=mesh['seq'=2,'fsdp'=16] {'fsdp'}, dimensions={0}, use_global_device_ids=true | all-gather | bytes 69632 | tf_op jit(solution)/shard_map/all_gather | solution.py:149
  438.3 19.1 %all-gather.3 = bf16[16,1,2048]{2,1,0:T(2,128)(2,1)S(1)} all-gather(bf16[1,1,2048]{2,1,0:T(2,128)(2,1)S(1)} %bitcast.284), channel_id=1, replica_groups=mesh['seq'=2,'fsdp'=16] {'fsdp'}, dimensions={0}, use_global_device_ids=true | all-gather | bytes 69632 | tf_op jit(solution)/shard_map/all_gather | solution.py:145
  461.3 33.4 %all-gather.8 = bf16[16,1,512]{2,1,0:T(2,128)(2,1)S(1)} all-gather(bf16[1,1,512]{2,1,0:T(2,128)(2,1)S(1)} %bitcast.300), channel_id=1, replica_groups=mesh['seq'=2,'fsdp'=16] {'fsdp'}, dimensions={0}, use_global_device_ids=true | all-gather | bytes 17408 | tf_op jit(solution)/shard_map/all_gather | solution.py:150
  502.4 138.1 %all-gather.29.cloned.1.call-done = bf16[4,4096,1024]{2,1,0:T(8,128)(2,1)} async-done(((bf16[4,2048,1024]{2,1,0:T(8,128)(2,1)}), bf16[4,4096,1024]{2,1,0:T(8,128)(2,1)}) %all-gather.29.cloned.1.call-update) | async-done | bytes 33554448 | tf_op jit(solution)/shard_map/all_gather | solution.py:45
  640.6 26.4 %multiply_convert_fusion.2 = (bf16[512,4096]{1,0:T(8,128)(2,1)S(1)}, f32[512,4096]{1,0:T(8,128)}, f32[512,4096]{1,0:T(8,128)}) fusion(f32[4096]{0:T(1024)S(1)} %bitcast.275, bf16[512,1024]{1,0:T(8,128)(2,1)S(1)} %bitcast.258, bf16[4,4096,1024]{2,1,0:T(8,128)(2,1)} %all-gather.29.cloned.1.call-done), kind=kOutput, calls=%fused_computation.44 | convolution fusion | flops 4433379328 | bytes 30425088 | tf_op jit(solution)/shard_map/dot_general | solution.py:58
  667.0 8.5 fusion.98
  676.0 27.0 %multiply_convert_fusion.1 = (bf16[512,4096]{1,0:T(8,128)(2,1)}, f32[512,4096]{1,0:T(8,128)}, f32[512,4096]{1,0:T(8,128)}) fusion(f32[4096]{0:T(1024)S(1)} %bitcast.277, bf16[4,4096,1024]{2,1,0:T(8,128)(2,1)} %all-gather.29.cloned.1.call-done, f32[512,1024]{1,0:T(8,128)S(1)} %get-tuple-element.72, f32[1024]{0:T(1024)S(1)} %bitcast.289, ...), kind=kOutput, calls=%fused_computation.31 | convolution fusion | flops 4436000768 | bytes 31485952 | tf_op jit(solution)/shard_map/dot_general | solution.py:58
  702.9 15.3 convert_reduce_fusion
  718.2 9.6 multiply_reduce_fusion.1
  728.6 10.5 fusion.43
  739.1 6.8 convert_bitcast_fusion.2
  745.9 15.3 convert_reduce_fusion.1
  761.3 9.4 fusion.92
  774.4 5.6 all-to-all-start.3
  780.1 10.5 convert_bitcast_fusion
  790.6 7.0 convert_bitcast_fusion.3
  797.6 7.2 convert_bitcast_fusion.1
  807.6 4.2 convolution_convert_fusion.1
  813.4 26.0 %multiply_reduce_fusion = (f32[16,512]{1,0:T(8,128)S(1)}, f32[16,512,1024]{2,1,0:T(8,128)}) fusion(f32[16,512,1024]{2,1,0:T(8,128)} %get-tuple-element.105, f32[16,512]{1,0:T(8,128)S(1)} %copy-done.30, pred[512,1024]{1,0:T(8,128)(4,1)S(1)} %copy-done.6, bf16[512,16,64]{0,2,1:T(8,128)(2,1)S(1)} %bitcast.246, bf16[1024,16,64]{0,2,1:T(8,128)(2,1)} %bitcast.243), kind=kOutput, calls=%fused_computation.6 | convolution fusion | flops 1115676672 | bytes 70844416 | tf_op jit(solution)/shard_map/qhd,khd->hqk/dot_general | solution.py:306
  839.4 28.1 %multiply_convert_fusion = bf16[16,512,1024]{2,1,0:T(8,128)(2,1)} fusion(f32[16,512,1024]{2,1,0:T(8,128)} %get-tuple-element.114, f32[16,512,1024]{2,1,0:T(8,128)} %get-tuple-element.105, f32[16,512]{1,0:T(8,128)S(1)} %get-tuple-element.113, f32[16,512]{1,0:T(8,128)S(1)} %copy-done.30, pred[512,1024]{1,0:T(8,128)(4,1)S(1)} %copy-done.6), kind=kLoop, calls=%fused_computation.5 | loop fusion | flops 50331648 | bytes 84475904 | tf_op jit(solution)/shard_map/convert_element_type | solution.py:310
  867.5 10.1 multiply_convert_fusion.3
  877.7 22.7 %pad_maximum_fusion = bf16[4,4096,1024]{2,1,0:T(8,128)(2,1)} fusion(bf16[1,4096,1024]{2,1,0:T(8,128)(2,1)} %convert_bitcast_fusion, bf16[1,4096,1024]{2,1,0:T(8,128)(2,1)} %convert_bitcast_fusion.1, bf16[1,4096,1024]{2,1,0:T(8,128)(2,1)} %convert_bitcast_fusion.2, bf16[1,4096,1024]{2,1,0:T(8,128)(2,1)} %convert_bitcast_fusion.3), kind=kLoop, calls=%fused_computation.4 | loop fusion | flops 50331648 | bytes 67108864 | tf_op jit(solution)/shard_map/stack | solution.py:287
  900.5 10.7 convolution_convert_fusion
  911.2 12.0 multiply_convert_fusion.4
  923.2 5.2 fusion.64
  928.5 4.7 fusion.80
  933.7 4.8 fusion.87
  938.6 342.7 %reduce-scatter.20.cloned.1.call-done = bf16[4,2048,1024]{2,1,0:T(8,128)(2,1)} async-done(((bf16[4,4096,1024]{2,1,0:T(8,128)(2,1)}), bf16[4,2048,1024]{2,1,0:T(8,128)(2,1)}) %reduce-scatter.20.cloned.1.call-update) | async-done | bytes 16777232 | tf_op jit(solution)/shard_map/reduce_scatter | solution.py:49
  1281.3 7.6 slice.74
  1289.1 26.8 %reduce-scatter.10.cloned.1.call-done = bf16[512,1024]{0,1:T(8,128)(2,1)} async-done(((bf16[1024,1024]{0,1:T(8,128)(2,1)}), bf16[512,1024]{0,1:T(8,128)(2,1)}) %reduce-scatter.10.cloned.1.call-update) | async-done | bytes 1048592 | tf_op jit(solution)/shard_map/reduce_scatter | solution.py:330
  1316.0 4.8 fusion.85
  1320.7 5.6 all-to-all-start.1
  1333.5 15.8 all-to-all-done.1
  1361.9 72.2 %all-reduce.21 = (bf16[1024]{0:T(1024)(128)(2,1)}, bf16[1024]{0:T(1024)(128)(2,1)}, bf16[16,512]{1,0:T(8,128)(2,1)}, bf16[16,512]{1,0:T(8,128)(2,1)}, bf16[16,20...) all-reduce(f32[1024]{0:T(1024)} %get-tuple-element.26, ...), channel_id=4, replica_groups=mesh['seq'=2,'fsdp'=16] {'fsdp'}, use_global_device_ids=true, to_apply=%region_20.22.clone | all-reduce | flops 124928 | bytes 749568
  1447.9 7.0 all-reduce.15
  1463.4 6.9 reduce-scatter.18.cloned.1.call-done
  1471.9 74.3 %reduce-scatter.14.cloned.1.call-done = f32[64,1024]{1,0:T(8,128)} async-done(((f32[1024,1024]{1,0:T(8,128)}), f32[64,1024]{1,0:T(8,128)}) %reduce-scatter.14.cloned.1.call-update) | async-done | bytes 262160 | tf_op jit(solution)/shard_map/reduce_scatter | solution.py:353
  1547.8 74.6 %reduce-scatter.16.cloned.1.call-done = f32[64,1024]{1,0:T(8,128)} async-done(((f32[1024,1024]{1,0:T(8,128)}), f32[64,1024]{1,0:T(8,128)}) %reduce-scatter.16.cloned.1.call-update) | async-done | bytes 262160 | tf_op jit(solution)/shard_map/reduce_scatter | solution.py:354
  1624.0 4.3 add_bitcast_fusion
  1628.3 25.3 %all-reduce.20.cloned.1.call-done = (bf16[64,1024]{1,0:T(8,128)(2,1)}, bf16[64,1024]{1,0:T(8,128)(2,1)}, bf16[64,1024]{1,0:T(8,128)(2,1)}, bf16[64,1024]{1,0:T(8,128)(2,1)}) async-done(((bf16[64,1024]{1,0:T(8,128)(2,1)}, bf16[64,1024]{1,0:T(8,128)(2,1)}, bf16[64,1024]{1,0:T(8,128)(2,1)}, bf16[64,1024]{1,0:T(8,128)(2,1)}), (bf16[64,1024]{1,0:T(8,128)(2,1)}, bf16[64,1024]{1,0:T(8,128)(2,1)}, ...) | async-done | bytes 524304 | tf_op jit(solution)/shard_map/psum | solution.py:414
  1660.1 7.8 convert_add_fusion
  1667.9 6.0 fusion.100
  (357 shorter events, 105.8 us)
Async XLA Ops:
  7.2 53.8 %all-gather.17.cloned.1.call-start = ((), (), s32[]{:S(2)}) async-start(), calls=%async_computation.11 | async-start | bytes 2228224 | tf_op jit(solution)/shard_map/all_gather | solution.py:141
  7.9 88.9 %all-gather.23.cloned.1.call-start = ((), (), s32[]{:S(2)}) async-start(), calls=%async_computation.14 | async-start | bytes 2228224 | tf_op jit(solution)/shard_map/all_gather | solution.py:140
  8.7 130.5 %all-gather.21.cloned.1.call-start = ((), (), s32[]{:S(2)}) async-start(), calls=%async_computation.13 | async-start | bytes 2228224 | tf_op jit(solution)/shard_map/all_gather | solution.py:139
  9.4 50.9 %copy-start.9 = (bf16[1,512,1024]{2,1,0:T(8,128)(2,1)S(1)}, bf16[1,512,1024]{2,1,0:T(8,128)(2,1)}, u32[]{:S(2)}) copy-start(bf16[1,512,1024]{2,1,0:T(8,128)(2,1)} %param.25) | copy-start | bytes 3145732
  9.5 163.6 %all-gather.19.cloned.1.call-start = ((), (), s32[]{:S(2)}) async-start(), calls=%async_computation.12 | async-start | bytes 3145728 | tf_op jit(solution)/shard_map/all_gather | solution.py:182
  18.9 82.8 %collective-permute-start = (bf16[4,1024,1024]{2,1,0:T(8,128)(2,1)}, bf16[4,1024,1024]{2,1,0:T(8,128)(2,1)}, u32[]{:S(2)}, u32[]{:S(2)}) collective-permute-start(bf16[4,1024,1024]{2,1,0:T(8,128)(2,1)} %constant_dynamic-update-slice_fusion), channel_id=1, source_target_pairs={{0,1},{1,0},{2,3},{3,2},{4,5},{5,4},{6,7},{7,6},{8,9},{9,8},{10,11... | collective-permute-start | bytes 25165832 | tf_op jit(solution)/shard_map/ppermute | solution.py:16
  60.3 78.9 %copy-start.36 = (f32[1024]{0:T(1024)}, f32[1024]{0:T(1024)S(1)}, u32[]{:S(2)}) copy-start(f32[1024]{0:T(1024)S(1)} %convert_element_type.364) | copy-start | bytes 12292
  60.3 78.9 %copy-start.66 = (f32[1024]{0:T(1024)}, f32[1024]{0:T(1024)S(1)}, u32[]{:S(2)}) copy-start(f32[1024]{0:T(1024)S(1)} %convert_element_type.365) | copy-start | bytes 12292
  60.5 78.7 %copy-start.40 = (f32[512]{0:T(512)}, f32[512]{0:T(512)S(1)}, u32[]{:S(2)}) copy-start(f32[512]{0:T(512)S(1)} %broadcast_multiply_fusion.2) | copy-start | bytes 6148
  61.0 39.7 %copy-start.50 = (f32[512]{0:T(512)}, f32[512]{0:T(512)S(1)}, u32[]{:S(2)}) copy-start(f32[512]{0:T(512)S(1)} %fusion.33) | copy-start | bytes 6148
  61.0 78.2 %copy-start.47 = (f32[512]{0:T(512)}, f32[512]{0:T(512)S(1)}, u32[]{:S(2)}) copy-start(f32[512]{0:T(512)S(1)} %fusion.77) | copy-start | bytes 6148
  64.9 143.3 %all-gather.25.cloned.1.call-start = ((), (), s32[]{:S(2)}) async-start(), calls=%async_computation.15 | async-start | bytes 3145728 | tf_op jit(solution)/shard_map/all_gather | solution.py:181
  100.7 175.7 %all-gather.27.cloned.1.call-start = ((), (), s32[]{:S(2)}) async-start(), calls=%async_computation.16 | async-start | bytes 2228224 | tf_op jit(solution)/shard_map/all_gather | solution.py:142
  101.3 539.3 %all-gather.29.cloned.1.call-start = ((), (), s32[]{:S(2)}) async-start(), calls=%async_computation.17 | async-start | bytes 50331648 | tf_op jit(solution)/shard_map/all_gather | solution.py:45
  119.7 123.4 %copy-start.5 = (pred[512,1024]{1,0:T(8,128)(4,1)}, pred[512,1024]{1,0:T(8,128)(4,1)S(1)}, u32[]{:S(2)}) copy-start(pred[512,1024]{1,0:T(8,128)(4,1)S(1)} %iota_compare_fusion) | copy-start | bytes 1572868
  211.1 16.1 copy-start.7
  227.2 20.6 %copy-start = (f32[16,512,1024]{2,1,0:T(8,128)S(1)}, f32[16,512,1024]{2,1,0:T(8,128)}, u32[]{:S(2)}) copy-start(f32[16,512,1024]{2,1,0:T(8,128)} %get-tuple-element.105) | copy-start | bytes 100663296
  258.3 18.2 %copy-start.10 = (bf16[1,512,1024]{2,1,0:T(8,128)(2,1)S(1)}, bf16[1,512,1024]{2,1,0:T(8,128)(2,1)}, u32[]{:S(2)}) copy-start(bf16[1,512,1024]{2,1,0:T(8,128)(2,1)} %param.25) | copy-start | bytes 3145732
  281.4 45.0 %copy-start.74 = (bf16[1,512]{1,0:T(2,128)(2,1)S(1)}, bf16[1,512]{1,0:T(2,128)(2,1)}, u32[]{:S(2)}) copy-start(bf16[1,512]{1,0:T(2,128)(2,1)} %param.44) | copy-start | bytes 3076
  281.4 66.4 %copy-start.75 = (bf16[1,512]{1,0:T(2,128)(2,1)S(1)}, bf16[1,512]{1,0:T(2,128)(2,1)}, u32[]{:S(2)}) copy-start(bf16[1,512]{1,0:T(2,128)(2,1)} %param.32) | copy-start | bytes 3076
  281.4 83.9 %copy-start.76 = (bf16[1,512]{1,0:T(2,128)(2,1)S(1)}, bf16[1,512]{1,0:T(2,128)(2,1)}, u32[]{:S(2)}) copy-start(bf16[1,512]{1,0:T(2,128)(2,1)} %param.37) | copy-start | bytes 3076
  281.4 102.7 %copy-start.77 = (bf16[1,512]{1,0:T(2,128)(2,1)S(1)}, bf16[1,512]{1,0:T(2,128)(2,1)}, u32[]{:S(2)}) copy-start(bf16[1,512]{1,0:T(2,128)(2,1)} %param.38) | copy-start | bytes 3076
  281.4 120.2 %copy-start.78 = (bf16[1,512]{1,0:T(2,128)(2,1)S(1)}, bf16[1,512]{1,0:T(2,128)(2,1)}, u32[]{:S(2)}) copy-start(bf16[1,512]{1,0:T(2,128)(2,1)} %param.39) | copy-start | bytes 3076
  281.4 139.0 %copy-start.57 = (bf16[1,2048]{1,0:T(2,128)(2,1)S(1)}, bf16[1,2048]{1,0:T(2,128)(2,1)}, u32[]{:S(2)}) copy-start(bf16[1,2048]{1,0:T(2,128)(2,1)} %param.41) | copy-start | bytes 12292
  281.5 156.8 %copy-start.58 = (bf16[1,2048]{1,0:T(2,128)(2,1)S(1)}, bf16[1,2048]{1,0:T(2,128)(2,1)}, u32[]{:S(2)}) copy-start(bf16[1,2048]{1,0:T(2,128)(2,1)} %param.35) | copy-start | bytes 12292
  281.5 179.8 %copy-start.79 = (bf16[1,512]{1,0:T(2,128)(2,1)S(1)}, bf16[1,512]{1,0:T(2,128)(2,1)}, u32[]{:S(2)}) copy-start(bf16[1,512]{1,0:T(2,128)(2,1)} %param.43) | copy-start | bytes 3076
  281.5 213.9 %copy-start.63 = (s32[1,512]{1,0:T(1,128)S(1)}, s32[1,512]{1,0:T(1,128)}, u32[]{:S(2)}) copy-start(s32[1,512]{1,0:T(1,128)} %param.46) | copy-start | bytes 6148
  287.2 170.4 %all-to-all-start = ((bf16[16,32,1024]{2,1,0:T(8,128)(2,1)}), bf16[16,32,1024]{2,1,0:T(8,128)(2,1)S(1)}, u32[]{:S(2)}, u32[]{:S(2)}) async-start(bf16[16,32,1024]{2,1,0:T(8,128)(2,1)} %bitcast.253), calls=%async_computation | async-start | bytes 2097152 | tf_op jit(solution)/shard_map/all_to_all | solution.py:234
  457.4 209.6 %copy-start.42 = (f32[2,1,512]{2,1,0:T(1,128)}, f32[2,1,512]{2,1,0:T(1,128)S(1)}, u32[]{:S(2)}) copy-start(f32[2,1,512]{2,1,0:T(1,128)S(1)} %dynamic-slice_convert_fusion.6) | copy-start | bytes 12292
  457.4 44.6 %copy-start.44 = (f32[2,1,512]{2,1,0:T(1,128)}, f32[2,1,512]{2,1,0:T(1,128)S(1)}, u32[]{:S(2)}) copy-start(f32[2,1,512]{2,1,0:T(1,128)S(1)} %dynamic-slice_convert_fusion.8) | copy-start | bytes 12292
  457.4 209.6 %copy-start.38 = (f32[2,1,512]{2,1,0:T(1,128)}, f32[2,1,512]{2,1,0:T(1,128)S(1)}, u32[]{:S(2)}) copy-start(f32[2,1,512]{2,1,0:T(1,128)S(1)} %dynamic-slice_convert_fusion.7) | copy-start | bytes 12292
  457.6 314.6 %copy-start.3 = (bf16[16,32,1024]{2,1,0:T(8,128)(2,1)}, bf16[16,32,1024]{2,1,0:T(8,128)(2,1)S(1)}, u32[]{:S(2)}) copy-start(bf16[16,32,1024]{2,1,0:T(8,128)(2,1)S(1)} %all-to-all-done) | copy-start | bytes 3145732
  457.6 42.5 %all-to-all-start.2 = ((bf16[16,32,1024]{2,1,0:T(8,128)(2,1)}), bf16[16,32,1024]{2,1,0:T(8,128)(2,1)S(1)}, u32[]{:S(2)}, u32[]{:S(2)}) async-start(bf16[16,32,1024]{2,1,0:T(8,128)(2,1)} %bitcast.252), calls=%async_computation.2 | async-start | bytes 2097152 | tf_op jit(solution)/shard_map/all_to_all | solution.py:235
  500.1 166.9 %copy-start.22 = (bf16[16,32,1024]{2,1,0:T(8,128)(2,1)}, bf16[16,32,1024]{2,1,0:T(8,128)(2,1)S(1)}, u32[]{:S(2)}) copy-start(bf16[16,32,1024]{2,1,0:T(8,128)(2,1)S(1)} %all-to-all-done.2) | copy-start | bytes 3145732
  675.6 52.3 %copy-start.18 = (f32[512,1024]{1,0:T(8,128)}, f32[512,1024]{1,0:T(8,128)S(1)}, u32[]{:S(2)}) copy-start(f32[512,1024]{1,0:T(8,128)S(1)} %get-tuple-element.72) | copy-start | bytes 6291460
  675.9 27.0 %copy-start.28 = (bf16[16,32,1024]{2,1,0:T(8,128)(2,1)S(1)}, bf16[16,32,1024]{2,1,0:T(8,128)(2,1)}, u32[]{:S(2)}) copy-start(bf16[16,32,1024]{2,1,0:T(8,128)(2,1)} %get-tuple-element.64) | copy-start | bytes 3145732
  745.9 15.3 copy-start.39
  745.9 15.3 copy-start.46
  774.4 30.4 %all-to-all-start.3 = ((bf16[16,32,1024]{2,1,0:T(8,128)(2,1)}), bf16[16,32,1024]{2,1,0:T(8,128)(2,1)S(1)}, u32[]{:S(2)}, u32[]{:S(2)}) async-start(bf16[16,32,1024]{2,1,0:T(8,128)(2,1)} %bitcast.43), calls=%async_computation.3 | async-start | bytes 2097152 | tf_op jit(solution)/shard_map/all_to_all | solution.py:276
  780.0 153.7 %reduce-scatter.8.cloned.1.call-start = ((), (), s32[]{:S(2)}) async-start(), calls=%async_computation.18 | async-start | bytes 3145728 | tf_op jit(solution)/shard_map/reduce_scatter | solution.py:324
  813.3 26.1 %copy-start.15 = (bf16[512,1024]{0,1:T(8,128)(2,1)}, bf16[512,1024]{0,1:T(8,128)(2,1)S(1)}, u32[]{:S(2)}) copy-start(bf16[512,1024]{0,1:T(8,128)(2,1)S(1)} %copy.59) | copy-start | bytes 3145732
  839.4 28.1 %copy-start.14 = (bf16[512,1024]{0,1:T(8,128)(2,1)S(1)}, bf16[512,1024]{0,1:T(8,128)(2,1)}, u32[]{:S(2)}) copy-start(bf16[512,1024]{0,1:T(8,128)(2,1)} %copy.57) | copy-start | bytes 3145732
  877.6 403.7 %reduce-scatter.20.cloned.1.call-start = ((), (), s32[]{:S(2)}) async-start(), calls=%async_computation.24 | async-start | bytes 50331648 | tf_op jit(solution)/shard_map/reduce_scatter | solution.py:49
  900.4 415.5 %reduce-scatter.10.cloned.1.call-start = ((), (), s32[]{:S(2)}) async-start(), calls=%async_computation.19 | async-start | bytes 3145728 | tf_op jit(solution)/shard_map/reduce_scatter | solution.py:330
  911.2 550.6 %reduce-scatter.12.cloned.1.call-start = ((), (), s32[]{:S(2)}) async-start(), calls=%async_computation.20 | async-start | bytes 4456448 | tf_op jit(solution)/shard_map/reduce_scatter | solution.py:352
  928.4 541.8 %reduce-scatter.18.cloned.1.call-start = ((), (), s32[]{:S(2)}) async-start(), calls=%async_computation.23 | async-start | bytes 4456448 | tf_op jit(solution)/shard_map/reduce_scatter | solution.py:355
  933.2 612.9 %reduce-scatter.14.cloned.1.call-start = ((), (), s32[]{:S(2)}) async-start(), calls=%async_computation.21 | async-start | bytes 4456448 | tf_op jit(solution)/shard_map/reduce_scatter | solution.py:353
  938.5 683.8 %reduce-scatter.16.cloned.1.call-start = ((), (), s32[]{:S(2)}) async-start(), calls=%async_computation.22 | async-start | bytes 4456448 | tf_op jit(solution)/shard_map/reduce_scatter | solution.py:354
  1289.0 38.1 %copy-start.53 = (f32[1024]{0:T(1024)S(1)}, f32[1024]{0:T(1024)}, u32[]{:S(2)}) copy-start(f32[1024]{0:T(1024)} %get-tuple-element.63) | copy-start | bytes 12292
  1289.0 38.4 %copy-start.60 = (f32[512]{0:T(512)S(1)}, f32[512]{0:T(512)}, u32[]{:S(2)}) copy-start(f32[512]{0:T(512)} %copy-done.59) | copy-start | bytes 6148
  1289.0 39.0 %copy-start.54 = (f32[1024]{0:T(1024)S(1)}, f32[1024]{0:T(1024)}, u32[]{:S(2)}) copy-start(f32[1024]{0:T(1024)} %get-tuple-element.24) | copy-start | bytes 12292
  1289.0 39.3 %copy-start.71 = (f32[1024]{0:T(1024)S(1)}, f32[1024]{0:T(1024)}, u32[]{:S(2)}) copy-start(f32[1024]{0:T(1024)} %get-tuple-element.29) | copy-start | bytes 12292
  1289.0 39.5 %copy-start.56 = (f32[4096]{0:T(1024)S(1)}, f32[4096]{0:T(1024)}, u32[]{:S(2)}) copy-start(f32[4096]{0:T(1024)} %get-tuple-element.116) | copy-start | bytes 49156
  1289.0 40.0 %copy-start.70 = (f32[1024]{0:T(1024)S(1)}, f32[1024]{0:T(1024)}, u32[]{:S(2)}) copy-start(f32[1024]{0:T(1024)} %get-tuple-element.84) | copy-start | bytes 12292
  1289.0 40.2 %copy-start.69 = (f32[1024]{0:T(1024)S(1)}, f32[1024]{0:T(1024)}, u32[]{:S(2)}) copy-start(f32[1024]{0:T(1024)} %get-tuple-element.22) | copy-start | bytes 12292
  1289.0 40.5 %copy-start.68 = (f32[1024]{0:T(1024)S(1)}, f32[1024]{0:T(1024)}, u32[]{:S(2)}) copy-start(f32[1024]{0:T(1024)} %get-tuple-element.28) | copy-start | bytes 12292
  1289.0 40.7 %copy-start.55 = (f32[4096]{0:T(1024)S(1)}, f32[4096]{0:T(1024)}, u32[]{:S(2)}) copy-start(f32[4096]{0:T(1024)} %get-tuple-element.118) | copy-start | bytes 49156
  1289.0 43.2 %copy-start.35 = (f32[16,32]{1,0:T(8,128)S(1)}, f32[16,32]{1,0:T(8,128)}, u32[]{:S(2)}) copy-start(f32[16,32]{1,0:T(8,128)} %copy-done.34) | copy-start | bytes 6148
  1289.0 43.9 %copy-start.4 = (bf16[16,32,1024]{2,1,0:T(8,128)(2,1)S(1)}, bf16[16,32,1024]{2,1,0:T(8,128)(2,1)}, u32[]{:S(2)}) copy-start(bf16[16,32,1024]{2,1,0:T(8,128)(2,1)} %copy-done.3) | copy-start | bytes 3145732
  1289.1 371.0 %collective-permute-start.1 = (bf16[4,1024,1024]{2,1,0:T(8,128)(2,1)}, bf16[4,1024,1024]{2,1,0:T(8,128)(2,1)}, u32[]{:S(2)}, u32[]{:S(2)}) collective-permute-start(bf16[4,1024,1024]{2,1,0:T(8,128)(2,1)} %slice.74), channel_id=1, source_target_pairs={{0,1},{1,0},{2,3},{3,2},{4,5},{5,4},{6,7},{7,6},{8,9},{9,8},{10,11... | collective-permute-start | bytes 25165832 | tf_op jit(solution)/shard_map/ppermute | solution.py:16
  1320.7 28.6 %all-to-all-start.1 = ((bf16[16,32,1024]{2,1,0:T(8,128)(2,1)}), bf16[16,32,1024]{2,1,0:T(8,128)(2,1)S(1)}, u32[]{:S(2)}, u32[]{:S(2)}) async-start(bf16[16,32,1024]{2,1,0:T(8,128)(2,1)} %bitcast.256), calls=%async_computation.1 | async-start | bytes 2097152 | tf_op jit(solution)/shard_map/all_to_all | solution.py:256
  1326.4 327.2 %all-reduce.20.cloned.1.call-start = ((), (), s32[]{:S(2)}) async-start(), calls=%async_computation.25 | async-start | bytes 1048576 | tf_op jit(solution)/shard_map/psum | solution.py:414
  1333.3 19.0 %copy-start.27 = (bf16[16,64,512]{2,1,0:T(8,128)(2,1)S(1)}, bf16[16,64,512]{2,1,0:T(8,128)(2,1)}, u32[]{:S(2)}) copy-start(bf16[16,64,512]{2,1,0:T(8,128)(2,1)} %multiply_convert_fusion.4) | copy-start | bytes 3145732
  1356.7 267.3 %copy-start.17 = (bf16[512,1024]{1,0:T(8,128)(2,1)S(1)}, bf16[512,1024]{1,0:T(8,128)(2,1)}, u32[]{:S(2)}) copy-start(bf16[512,1024]{1,0:T(8,128)(2,1)} %gather_fusion.3) | copy-start | bytes 3145732
  (47 other events, 332.8 us)
Sparse Core Ops, SparseCore 0:
  10.2 44.0 all-gather.16
  56.4 40.3 all-gather.22
  99.0 40.1 all-gather.20
  141.2 31.8 all-gather.18
  175.1 33.1 all-gather.24
  210.2 41.3 all-gather.26
  253.2 387.3 all-gather.28
  877.8 32.2 reduce-scatter.7
  912.4 368.8 reduce-scatter.19
  1284.1 31.8 reduce-scatter.9
  1320.4 73.8 reduce-scatter.11
  1399.1 71.1 reduce-scatter.17
  1474.7 71.4 reduce-scatter.13
  1550.9 71.3 reduce-scatter.15
  1625.3 28.2 all-reduce.19
where the time goes:
time: 1690 us; the launch traced here: 1680 us
  waiting for transfers between devices  820 us (49%)
  blocking collectives  316 us (19%)
  matrix products  292 us (17%)
  other arithmetic  140 us (8%)
  local copies, waits for them, and re-layouts  73.4 us (4%)
  starting transfers between devices  22.3 us (1%)
    reduce_scatter x1, waiting for transfers between devices, holders_sum(): lax.psum_scatter(stack.astype(jnp.bfloat16), 'seq', scatter_dimension=1,...  343 us
    all_gather x1, waiting for transfers between devices, holders_gather(): return lax.all_gather(paired, 'seq', axis=1, tiled=True)  138 us
    unnamed x2, blocking collectives  111 us
    dot_general x4, matrix products, contract_last(): lax.dot_general(left, right, (((1,), (1,)), ((), ())), preferred_element_...  84 us
    reduce_scatter x1, waiting for transfers between devices, body(): lax.psum_scatter(grad_wv, 'fsdp', scatter_dimension=0, tiled=True)  74.6 us
    reduce_scatter x1, waiting for transfers between devices, body(): lax.psum_scatter(grad_wk, 'fsdp', scatter_dimension=0, tiled=True)  74.3 us
  transfers between devices with their start and end apart: 21, of which 12 were waited for; matrix products, arithmetic and copies ran while one was open for 17% of the time, Pallas kernels for 0%

commit v1 on v0

v1 whole, which is shorter than its diff:
```python
import functools

import jax
import jax.numpy as jnp
from jax import lax
from jax.experimental import pallas as pl
from jax.experimental.pallas import tpu as pltpu
from jax.sharding import PartitionSpec as P

HEADS = 16
EPS = 1e-05
MASKED = -1e30
BLOCK = 256
CHUNK = 512
BF16 = jnp.bfloat16
F32 = jnp.float32
VMEM_LIMIT = 56 * 1024 * 1024


def swapped(value, axis):
    pairs = [(source, source ^ 1) for source in range(lax.axis_size(axis))]
    return lax.ppermute(value, axis, pairs)


def dot_last(left, right):
    return lax.dot_general(left, right, (((1,), (1,)), ((), ())), preferred_element_type=F32)


def dot_first(left, right):
    return lax.dot_general(left, right, (((0,), (0,)), ((), ())), preferred_element_type=F32)


def dot(left, right):
    return jnp.dot(left, right, preferred_element_type=F32)


def normalised(values):
    centred = values - jnp.mean(values, axis=-1, keepdims=True)
    spread = jnp.mean(centred * centred, axis=-1, keepdims=True)
    rate = lax.rsqrt(spread + EPS)
    return centred * rate, rate


def norm_back(grad, xhat, rate, gain):
    scaled = grad * gain
    inner = jnp.mean(scaled * xhat, axis=-1, keepdims=True)
    return rate * (scaled - jnp.mean(scaled, axis=-1, keepdims=True) - xhat * inner)


def causal_mask(scores):
    keys = lax.broadcasted_iota(jnp.int32, scores.shape, 0)
    queries = lax.broadcasted_iota(jnp.int32, scores.shape, 1)
    return jnp.where(keys <= queries, scores, MASKED)


def attention_forward_kernel(size, q_ref, k_ref, v_ref, o_ref, log_ref):
    length = q_ref.shape[0]
    for head in range(q_ref.shape[1] // size):
        lanes = slice(head * size, (head + 1) * size)
        for start in range(0, length, BLOCK):
            query = q_ref[start : start + BLOCK, lanes] * BF16(size**-0.5)
            last = causal_mask(dot_last(k_ref[start : start + BLOCK, lanes], query))
            peak = jnp.max(last, axis=0, keepdims=True)
            if start:
                early = dot_last(k_ref[:start, lanes], query)
                peak = jnp.maximum(peak, jnp.max(early, axis=0, keepdims=True))
            last = jnp.exp(last - peak)
            total = jnp.sum(last, axis=0, keepdims=True)
            out = dot_first(v_ref[start : start + BLOCK, lanes], last.astype(BF16))
            if start:
                early = jnp.exp(early - peak)
                total = total + jnp.sum(early, axis=0, keepdims=True)
                out = out + dot_first(v_ref[:start, lanes], early.astype(BF16))
            o_ref[start : start + BLOCK, lanes] = (out / total).T.astype(BF16)
            log_ref[0, head : head + 1, start : start + BLOCK] = peak + jnp.log(total)


def attention_backward_kernel(size, q_ref, k_ref, v_ref, g_ref, log_ref, d_ref, dk_sum, dv_sum):
    length = q_ref.shape[0]
    scale = size**-0.5
    for head in range(q_ref.shape[1] // size):
        lanes = slice(head * size, (head + 1) * size)
        dk_sum[...] = jnp.zeros_like(dk_sum)
        dv_sum[...] = jnp.zeros_like(dv_sum)
        for start in range(0, length, BLOCK):
            rows = slice(start, start + BLOCK)
            query = q_ref[rows, lanes] * BF16(scale)
            grad = g_ref[rows, lanes]
            log_total = log_ref[0, head : head + 1, rows]
            spans = ([slice(0, start)] if start else []) + [rows]
            probs, weighted = [], []
            inner = jnp.zeros((1, BLOCK), F32)
            for span in spans:
                scores = dot_last(k_ref[span, lanes], query)
                if span is rows:
                    scores = causal_mask(scores)
                prob = jnp.exp(scores - log_total)
                grad_prob = dot_last(v_ref[span, lanes], grad)
                inner = inner + jnp.sum(prob * grad_prob, axis=0, keepdims=True)
                probs.append(prob)
                weighted.append(grad_prob)
            grad_query = jnp.zeros((BLOCK, size), F32)
            for span, prob, grad_prob in zip(spans, probs, weighted):
                low = (prob * (grad_prob - inner)).astype(BF16)
                dv_sum[span, :] += dot(prob.astype(BF16), grad)
                dk_sum[span, :] += dot(low, query)
                grad_query = grad_query + dot_first(low, k_ref[span, lanes])
            d_ref[0, rows, lanes] = (grad_query * scale).astype(BF16)
        d_ref[1, :, lanes] = dk_sum[...].astype(BF16)
        d_ref[2, :, lanes] = dv_sum[...].astype(BF16)


def attention_specs(length, half):
    parts = half // 128
    column = lambda which: pl.BlockSpec((length, 128), lambda i: (0, which * parts + i))
    return parts, column


def attention_forward(qkv, size):
    length, half = qkv.shape[0], qkv.shape[1] // 3
    parts, column = attention_specs(length, half)
    per = 128 // size
    return pl.pallas_call(
        functools.partial(attention_forward_kernel, size),
        grid=(parts,),
        out_shape=(
            jax.ShapeDtypeStruct((length, half), BF16),
            jax.ShapeDtypeStruct((parts, per, length), F32),
        ),
        in_specs=[column(0), column(1), column(2)],
        out_specs=(column(0), pl.BlockSpec((1, per, length), lambda i: (i, 0, 0))),
        compiler_params=pltpu.CompilerParams(vmem_limit_bytes=VMEM_LIMIT),
        cost_estimate=pl.CostEstimate(
            flops=8 * length * length * half, bytes_accessed=10 * length * half, transcendentals=0
        ),
        name="attention_forward",
    )(qkv, qkv, qkv)


def attention_backward(qkv, grad, logs, size):
    length, half = grad.shape
    parts, column = attention_specs(length, half)
    per = 128 // size
    return pl.pallas_call(
        functools.partial(attention_backward_kernel, size),
        grid=(parts,),
        out_shape=jax.ShapeDtypeStruct((3, length, half), BF16),
        in_specs=[
            column(0),
            column(1),
            column(2),
            column(0),
            pl.BlockSpec((1, per, length), lambda i: (i, 0, 0)),
        ],
        out_specs=pl.BlockSpec((3, length, 128), lambda i: (0, 0, i)),
        scratch_shapes=[pltpu.VMEM((length, size), F32), pltpu.VMEM((length, size), F32)],
        compiler_params=pltpu.CompilerParams(vmem_limit_bytes=VMEM_LIMIT),
        cost_estimate=pl.CostEstimate(
            flops=20 * length * length * half, bytes_accessed=16 * length * half, transcendentals=0
        ),
        name="attention_backward",
    )(qkv, qkv, qkv, grad, logs)


def stream(step, steps, parts, pairs, buffers, sems):
    per = steps // parts

    def fetch(which):
        slot = lax.rem(which, 2)
        row = pl.multiple_of(lax.rem(which, per) * CHUNK, CHUNK)
        for quarter in range(parts):

            @pl.when(which // per == quarter)
            def _():
                for m, refs in enumerate(pairs):
                    pltpu.make_async_copy(
                        refs[quarter].at[pl.ds(row, CHUNK)], buffers[m].at[slot], sems.at[m, slot]
                    ).start()

    @pl.when(step == 0)
    def _():
        fetch(step)

    @pl.when(step + 1 < steps)
    def _():
        fetch(step + 1)

    slot = lax.rem(step, 2)
    for m, refs in enumerate(pairs):
        pltpu.make_async_copy(
            refs[0].at[pl.ds(0, CHUNK)], buffers[m].at[slot], sems.at[m, slot]
        ).wait()
    return slot


def gelu_parts(inner):
    cdf = 0.5 * (1.0 + lax.erf(inner * 0.7071067811865476))
    slope = cdf + inner * (jnp.exp(-0.5 * inner * inner) * 0.3989422804014327)
    return inner * cdf, slope


def forward_first_kernel(parts, steps, *refs):
    z_ref, gain_ref, shift_ref, bias_ref, out_bias_ref = refs[:5]
    win, wout = refs[5 : 5 + parts], refs[5 + parts : 5 + 2 * parts]
    first_ref, normed_ref, active_ref, slope_ref, in_buf, out_buf, sems = refs[5 + 2 * parts :]
    step = pl.program_id(0)

    @pl.when(step == 0)
    def _():
        xhat, _ = normalised(z_ref[...].astype(F32))
        normed_ref[...] = (xhat * gain_ref[...] + shift_ref[...]).astype(BF16)
        first_ref[...] = jnp.broadcast_to(out_bias_ref[...], first_ref.shape)

    slot = stream(step, steps, parts, (win, wout), (in_buf, out_buf), sems)
    active, slope = gelu_parts(dot_last(normed_ref[...], in_buf[slot]) + bias_ref[0])
    low = active.astype(BF16)
    active_ref[...] = low
    slope_ref[...] = slope.astype(BF16)
    first_ref[...] += dot(low, out_buf[slot])


def forward_second_kernel(parts, steps, *refs):
    z_ref, first_ref, cot_ref, centre_ref, gain_ref, shift_ref, bias_ref, out_bias_ref = refs[:8]
    win, wout = refs[8 : 8 + parts], refs[8 + parts : 8 + 2 * parts]
    normed_ref, active_ref, slope_ref, gated_ref, grad_ref, score_ref = refs[
        8 + 2 * parts : 14 + 2 * parts
    ]
    total, in_buf, out_buf, sems = refs[14 + 2 * parts :]
    step = pl.program_id(0)

    @pl.when(step == 0)
    def _():
        xhat, _ = normalised(z_ref[...].astype(F32) + first_ref[...])
        normed_ref[...] = (xhat * gain_ref[...] + shift_ref[...]).astype(BF16)
        total[...] = first_ref[...] + out_bias_ref[...]

    slot = stream(step, steps, parts, (win, wout), (in_buf, out_buf), sems)
    active, slope = gelu_parts(dot_last(normed_ref[...], in_buf[slot]) + bias_ref[0])
    low = active.astype(BF16)
    active_ref[...] = low
    slope_ref[...] = slope.astype(BF16)
    total[...] += dot(low, out_buf[slot])

    @pl.when(step == steps - 1)
    def _():
        branch = total[...]
        grad_gated = cot_ref[...].astype(F32)
        logit = jnp.sum(z_ref[...].astype(F32) * centre_ref[...], axis=-1, keepdims=True)
        gate = jax.nn.sigmoid(logit)
        gated_ref[...] = (gate * branch).astype(BF16)
        grad_ref[...] = (gate * grad_gated).astype(BF16)
        grad_gate = jnp.sum(grad_gated * branch, axis=-1, keepdims=True)
        score_ref[...] = jnp.broadcast_to(grad_gate * gate * (1.0 - gate), score_ref.shape)


def backward_kernel(second, parts, steps, *refs):
    grad_ref, normed_ref, active_ref, slope_ref, z_ref, centre_ref, gain_ref = refs[:7]
    extra_one, extra_two = refs[7:9]
    win, wout = refs[9 : 9 + parts], refs[9 + parts : 9 + 2 * parts]
    base = 9 + 2 * parts
    result = refs[base : base + (2 if second else 1)]
    base += len(result)
    vector_ref, bias_ref = refs[base : base + 2]
    gwin, gwout = refs[base + 2 : base + 2 + parts], refs[base + 2 + parts : base + 2 + 2 * parts]
    total, in_buf, out_buf, sems = refs[base + 2 + 2 * parts :]
    step = pl.program_id(0)
    per = steps // parts

    @pl.when(step == 0)
    def _():
        total[...] = jnp.zeros_like(total)

    slot = stream(step, steps, parts, (win, wout), (in_buf, out_buf), sems)
    grad = grad_ref[...]
    inner = (slope_ref[...].astype(F32) * dot_last(grad, out_buf[slot])).astype(BF16)
    bias_ref[0] = jnp.sum(inner.astype(F32), axis=0, keepdims=True)
    total[...] += dot(inner, in_buf[slot])
    grad_out = dot_first(active_ref[...], grad).astype(BF16)
    grad_in = dot_first(inner, normed_ref[...]).astype(BF16)
    for quarter in range(parts):

        @pl.when(step // per == quarter)
        def _():
            gwin[quarter][...] = grad_in
            gwout[quarter][...] = grad_out

    @pl.when(step == steps - 1)
    def _():
        z = z_ref[...].astype(F32)
        source = z + extra_one[...] if second else z
        xhat, rate = normalised(source)
        grad_normed = total[...]
        grad_rows = norm_back(grad_normed, xhat, rate, gain_ref[...])
        vector_ref[...] = jnp.zeros_like(vector_ref)
        vector_ref[0:1] = jnp.sum(grad_normed * xhat, axis=0, keepdims=True)
        vector_ref[1:2] = jnp.sum(grad_normed, axis=0, keepdims=True)
        vector_ref[2:3] = jnp.sum(grad.astype(F32), axis=0, keepdims=True)
        if second:
            gate = jax.nn.sigmoid(jnp.sum(z * centre_ref[...], axis=-1, keepdims=True))
            result[0][...] = grad_rows
            result[1][...] = (gate * extra_two[...].astype(F32) + grad_rows).astype(BF16)
        else:
            score = extra_two[:, 0:1]
            vector_ref[3:4] = jnp.sum(score * z, axis=0, keepdims=True)
            result[0][...] = (extra_one[...] + grad_rows + score * centre_ref[...]).astype(BF16)


def expert_call(kernel, name, steps, rows, inputs, weights, outs, scratch, flops):
    whole = lambda shape: pl.BlockSpec(shape, lambda c: (0,) * len(shape))
    spec = lambda shape, block, at: whole(shape) if block is None else pl.BlockSpec(block, at)
    features = weights[0].shape[1]
    return pl.pallas_call(
        kernel,
        grid=(steps,),
        out_shape=tuple(s for s, _, _ in outs),
        in_specs=[spec(a.shape, b, m) for a, b, m in inputs]
        + [pl.BlockSpec(memory_space=pl.ANY)] * len(weights),
        out_specs=tuple(spec(s.shape, b, m) for s, b, m in outs),
        scratch_shapes=scratch
        + [
            pltpu.VMEM((2, CHUNK, features), BF16),
            pltpu.VMEM((2, CHUNK, features), BF16),
            pltpu.SemaphoreType.DMA((2, 2)),
        ],
        compiler_params=pltpu.CompilerParams(vmem_limit_bytes=VMEM_LIMIT),
        cost_estimate=pl.CostEstimate(
            flops=flops, bytes_accessed=2 * sum(w.size for w in weights), transcendentals=0
        ),
        name=name,
    )(*[a for a, _, _ in inputs], *weights)


def expert(z, cot, vectors, biases, one, two):
    rows, features = z.shape
    parts = len(one[0])
    hidden = sum(w.shape[0] for w in one[0])
    steps = hidden // CHUNK
    per = steps // parts
    line = lambda i: (vectors[i : i + 1], None, None)
    shape = jax.ShapeDtypeStruct
    wide = ((rows, CHUNK), lambda c: (0, c))
    thin = ((1, 1, CHUNK), lambda c: (c, 0, 0))
    chunked = biases.reshape(2, steps, 1, CHUNK)
    hidden_out = [
        (shape((rows, features), BF16), None, None),
        (shape((rows, hidden), BF16), *wide),
        (shape((rows, hidden), BF16), *wide),
    ]
    matmul = 2 * rows * hidden * features
    first, normed_one, active_one, slope_one = expert_call(
        functools.partial(forward_first_kernel, parts, steps),
        "forward_first",
        steps,
        rows,
        [(z, None, None), line(0), line(1), (chunked[0], *thin), line(2)],
        one[0] + one[1],
        [(shape((rows, features), F32), None, None)] + hidden_out,
        [],
        2 * matmul,
    )
    normed_two, active_two, slope_two, gated, grad_second, score = expert_call(
        functools.partial(forward_second_kernel, parts, steps),
        "forward_second",
        steps,
        rows,
        [
            (z, None, None),
            (first, None, None),
            (cot, None, None),
            line(6),
            line(3),
            line(4),
            (chunked[1], *thin),
            line(5),
        ],
        two[0] + two[1],
        hidden_out
        + [
            (shape((rows, features), BF16), None, None),
            (shape((rows, features), BF16), None, None),
            (shape((rows, 128), F32), None, None),
        ],
        [pltpu.VMEM((rows, features), F32)],
        2 * matmul,
    )

    def quarter_outs():
        return [
            (
                shape((hidden // parts, features), BF16),
                (CHUNK, features),
                lambda c, q=q: (jnp.clip(c - q * per, 0, per - 1), 0),
            )
            for q in range(parts)
        ]

    sums = [
        (shape((8, features), F32), None, None),
        (shape((steps, 1, CHUNK), F32), *thin),
    ]

    def back(second, grad, normed, active, slope, gain, extra_one, extra_two, weights, results):
        outs = expert_call(
            functools.partial(backward_kernel, second, parts, steps),
            "backward_second" if second else "backward_first",
            steps,
            rows,
            [
                (grad, None, None),
                (normed, None, None),
                (active, *wide),
                (slope, *wide),
                (z, None, None),
                line(6),
                line(gain),
                (extra_one, None, None),
                (extra_two, None, None),
            ],
            weights[0] + weights[1],
            results + sums + quarter_outs() + quarter_outs(),
            [pltpu.VMEM((rows, features), F32)],
            4 * matmul,
        )
        n = len(results)
        tail = outs[n + 2 :]
        return outs[:n], outs[n], outs[n + 1].reshape(hidden), tail[:parts], tail[parts:]

    (grad_in_two, grad_first), sums_two, bias_two, gwin_two, gwout_two = back(
        True,
        grad_second,
        normed_two,
        active_two,
        slope_two,
        3,
        first,
        cot,
        two,
        [
            (shape((rows, features), F32), None, None),
            (shape((rows, features), BF16), None, None),
        ],
    )
    (grad_sent,), sums_one, bias_one, gwin_one, gwout_one = back(
        False,
        grad_first,
        normed_one,
        active_one,
        slope_one,
        0,
        grad_in_two,
        score,
        one,
        [(shape((rows, features), BF16), None, None)],
    )
    vector_grads = jnp.concatenate([sums_one[:3], sums_two[:3], sums_one[3:4]], axis=0)
    bias_grads = jnp.stack([bias_one, bias_two])
    return gated, grad_sent, vector_grads, bias_grads, (gwin_one, gwout_one), (gwin_two, gwout_two)


def body(
    inputs,
    ln_gain,
    ln_shift,
    w_query,
    w_key,
    w_value,
    w_output,
    exp_gain1,
    exp_shift1,
    w_in1,
    b_in1,
    w_out1,
    b_out1,
    exp_gain2,
    exp_shift2,
    w_in2,
    b_in2,
    w_out2,
    b_out2,
    centroid,
    order,
    inverse,
    cotangent,
):
    seq, peer = lax.axis_index("seq"), lax.axis_index("fsdp")
    peers = lax.axis_size("fsdp")
    rows = inputs[0]
    tokens, features = rows.shape
    half = features // 2
    size = features // HEADS
    left, even = seq == 0, lax.rem(peer, 2) == 0
    over = lambda value: swapped(value, "seq")
    beside = lambda value: swapped(value, "fsdp")
    ordered = lambda flag, mine, other, axis: jnp.where(
        flag, jnp.concatenate([mine, other], axis), jnp.concatenate([other, mine], axis)
    )

    other_rows = over(rows)
    columns = lambda w: lax.dynamic_slice_in_dim(w, seq * half, half, 1)
    norm_vectors = jnp.pad(jnp.stack([ln_gain, ln_shift], axis=1), ((0, 0), (0, 126)))
    gathered = lax.all_gather(
        jnp.concatenate([columns(w_query), columns(w_key), columns(w_value), norm_vectors], axis=1),
        "fsdp",
        axis=0,
        tiled=True,
    )
    output_full = lax.all_gather(w_output, "fsdp", axis=0, tiled=True)
    own_vectors = jnp.concatenate(
        [exp_gain1, exp_shift1, b_out1, exp_gain2, exp_shift2, b_out2, centroid], axis=0
    )
    own_biases = jnp.concatenate([b_in1, b_in2], axis=0)
    pair = beside(jnp.concatenate([own_vectors.reshape(-1), own_biases.reshape(-1)]))
    other_vectors = pair[: own_vectors.size].reshape(own_vectors.shape)
    other_biases = pair[own_vectors.size :].reshape(own_biases.shape)
    vectors = ordered(even, own_vectors, other_vectors, 1).astype(F32)

    quarter = w_in1.shape[1]
    pick = lambda table, which: lax.dynamic_slice_in_dim(table, which * quarter, quarter, 1)
    biases = jnp.concatenate(
        [
            pick(own_biases, seq),
            pick(other_biases, seq),
            pick(own_biases, 1 - seq),
            pick(other_biases, 1 - seq),
        ],
        axis=1,
    ).astype(F32)

    def holders(weight):
        mine = weight[0]
        far = over(mine)
        return [mine, beside(mine), far, beside(far)]

    one = (holders(w_in1), holders(w_out1))
    two = (holders(w_in2), holders(w_out2))
    cot = cotangent[0]
    exchange = lambda value: lax.all_to_all(
        value.reshape(peers, tokens // peers, features),
        "fsdp",
        split_axis=0,
        concat_axis=0,
        tiled=True,
    ).reshape(tokens, features)
    cot_slots = exchange(jnp.take(cot, order[0], axis=0))

    sequence = ordered(left, rows, other_rows, 0).astype(F32)
    gain, shift = gathered[:, 3 * half].astype(F32), gathered[:, 3 * half + 1].astype(F32)
    xhat, rate = normalised(sequence)
    normed = (xhat * gain + shift).astype(BF16)
    qkv_weight = gathered[:, : 3 * half]
    qkv = dot(normed, qkv_weight).astype(BF16)
    mixed_heads, logs = attention_forward(qkv, size)
    block_of = lambda value, which: lax.dynamic_slice_in_dim(value, which * tokens, tokens, 0)
    mixed = ordered(
        left, block_of(mixed_heads, seq), over(block_of(mixed_heads, 1 - seq)), 1
    )
    middle = rows.astype(F32) + dot(mixed, output_full)

    z = exchange(jnp.take(middle.astype(BF16), order[0], axis=0))
    gated, grad_sent, vector_grads, bias_grads, grads_one, grads_two = expert(
        z, cot_slots, vectors, biases, one, two
    )
    home = jnp.take(exchange(gated), inverse[0], axis=0)
    layer_out = (middle + home.astype(F32)).astype(BF16)
    coming = jnp.take(exchange(grad_sent), inverse[0], axis=0)
    grad_middle = cot.astype(F32) + coming.astype(F32)

    def holders_sum(quarters):
        mine, near, far, cross = quarters
        mine = mine.astype(F32) + beside(near).astype(F32)
        far = (far.astype(F32) + beside(cross).astype(F32)).astype(BF16)
        return mine + over(far).astype(F32)

    grad_win_two, grad_wout_two = [holders_sum(g) for g in grads_two]
    grad_win_one, grad_wout_one = [holders_sum(g) for g in grads_one]

    own_half = lambda table, which: lax.dynamic_slice_in_dim(table, which * half, half, 1)
    core = lax.rem(peer, 2)
    bias_quarters = bias_grads.reshape(2, 4, quarter)
    bias_rows = lambda first: ordered(left, bias_quarters[:, first], bias_quarters[:, first + 2], 1)
    flat = lambda table, bias: jnp.concatenate([table.reshape(-1), bias.reshape(-1)])
    small = flat(own_half(vector_grads, core), bias_rows(0)) + beside(
        flat(own_half(vector_grads, 1 - core), bias_rows(1))
    )
    small = small + over(small)
    count = vector_grads.shape[0]
    vector_out = small[: count * half].reshape(count, 1, half)
    bias_out = small[count * half :].reshape(2, 1, 2 * quarter)

    grad_attn = grad_middle.astype(BF16)
    grad_wo = lax.psum_scatter(
        dot_first(mixed, grad_attn).astype(BF16), "fsdp", scatter_dimension=0, tiled=True
    ).astype(F32)
    grad_wo = grad_wo + over(grad_wo)
    grad_mixed = dot_last(grad_attn, output_full).astype(BF16)
    part_of = lambda value, which: lax.dynamic_slice_in_dim(value, which * half, half, 1)
    grad_heads = ordered(left, part_of(grad_mixed, seq), over(part_of(grad_mixed, 1 - seq)), 0)
    parts = attention_backward(qkv, grad_heads, logs, size)
    grad_normed = dot_last(parts[0], qkv_weight[:, :half])
    grad_normed = grad_normed + dot_last(parts[1], qkv_weight[:, half : 2 * half])
    grad_normed = grad_normed + dot_last(parts[2], qkv_weight[:, 2 * half :])
    norm_sums = jnp.stack([jnp.sum(grad_normed * xhat, axis=0), jnp.sum(grad_normed, axis=0)], axis=1)
    packed = jnp.concatenate(
        [dot_first(normed, parts[i]).astype(BF16) for i in range(3)]
        + [jnp.pad(norm_sums, ((0, 0), (0, 126))).astype(BF16)],
        axis=1,
    )
    shard = lax.psum_scatter(packed, "fsdp", scatter_dimension=0, tiled=True)
    other_shard = over(shard)
    join = lambda which: ordered(
        left,
        shard[:, which * half : (which + 1) * half],
        other_shard[:, which * half : (which + 1) * half],
        1,
    ).astype(F32)
    norm_grads = shard[:, 3 * half : 3 * half + 2].astype(F32)
    norm_grads = norm_grads + other_shard[:, 3 * half : 3 * half + 2].astype(F32)
    arrived = over(block_of(grad_normed, 1 - seq).astype(BF16)).astype(F32)
    grad_own = block_of(grad_normed, seq) + arrived
    own_xhat, own_rate = normalised(rows.astype(F32))
    grad_inputs = grad_middle + norm_back(grad_own, own_xhat, own_rate, gain)
    return (
        layer_out[None],
        grad_inputs[None],
        norm_grads[:, 0],
        norm_grads[:, 1],
        join(0),
        join(1),
        join(2),
        grad_wo,
        vector_out[0],
        vector_out[1],
        grad_win_one[None],
        bias_out[0],
        grad_wout_one[None],
        vector_out[2],
        vector_out[3],
        vector_out[4],
        grad_win_two[None],
        bias_out[1],
        grad_wout_two[None],
        vector_out[5],
        vector_out[6],
    )


def solution(mesh):
    both, rows, vector = P("fsdp", "seq", None), P("fsdp", None), P("fsdp")
    return jax.shard_map(
        body,
        mesh=mesh,
        in_specs=(both, vector, vector, rows, rows, rows, rows)
        + (rows, rows, both, rows, both, rows) * 2
        + (rows, P("fsdp", "seq"), P("fsdp", "seq"), both),
        out_specs=(both, both, vector, vector, rows, rows, rows, rows)
        + (rows, rows, both, rows, both, rows) * 2
        + (rows,),
        check_vma=False,
    )
```

time: 1690 us -> 696 us (0.41)
  waiting for transfers between devices: 820 us -> 353 us
  blocking collectives: 316 us -> 0 us
  matrix products: 292 us -> 28.8 us
  Pallas kernels: 0 us -> 144 us
  other arithmetic: 140 us -> 59.7 us
  local copies, waits for them, and re-layouts: 73.4 us -> 34.4 us
  starting transfers between devices: 22.3 us -> 52 us
    reduce_scatter x7 -> x1, waiting for transfers between devices: 525 us -> 0.01 us  [body(): lax.psum_scatter(dot_first(mixed, grad_attn).astype(BF16), 'fsdp', scatte...]
    ppermute x2 -> x33, waiting for transfers between devices: 0.01 us -> 316 us  [swapped(): return lax.ppermute(value, axis, pairs)]
    dot_general x30 -> x10, matrix products: 292 us -> 28.8 us  [the longest x4 12.3 us: dot_last(): lax.dot_general(left, right, (((1,), (1,)), ((), ())), preferred_element_...]
    all_gather x7 -> x2, waiting for transfers between devices: 250 us -> 18 us  [the longest x1 18 us: body(): lax.all_gather(jnp.concatenate([columns(w_query), columns(w_key), columns...]
    all_gather x9 -> x0, blocking collectives: 198 us -> none  [the longest x1 33.6 us: body(): lax.all_gather(exp_shift1, 'fsdp', axis=0, tiled=True)]
    pallas_call x0 -> x6, Pallas kernels: none -> 144 us  [the longest x4 104 us: expert_call(): pl.pallas_call(kernel, grid=(steps,), out_shape=tuple((s for s, _, _ in o...]
    unnamed x2 -> x0, blocking collectives: 111 us -> none
    convert_element_type x32 -> x12, other arithmetic: 61.1 us -> 19.2 us  [the longest x4 14.1 us: holders_sum(): far = (far.astype(F32) + beside(cross).astype(F32)).astype(BF16)]
  transfers between devices with their start and end apart: 21 -> 41, of which waited for: 12 -> 16; matrix products, arithmetic and copies ran while one was open for 17% -> 16% of each run, Pallas kernels for 0% -> 8%
where the time goes in v1:
time: 696 us; the launch traced here: 686 us
  waiting for transfers between devices  353 us (51%)
  Pallas kernels  144 us (21%)
  other arithmetic  59.7 us (9%)
  starting transfers between devices  52 us (7%)
  local copies, waits for them, and re-layouts  34.4 us (5%)
  matrix products  28.8 us (4%)
  between operations  15.2 us (2%)
    ppermute x33, waiting for transfers between devices, swapped(): return lax.ppermute(value, axis, pairs)  316 us
    pallas_call x4, Pallas kernels, expert_call(): pl.pallas_call(kernel, grid=(steps,), out_shape=tuple((s for s, _, _ in o...  104 us
    all_to_all x4, starting transfers between devices, body(): lax.all_to_all(value.reshape(peers, tokens // peers, features), 'fsdp', s...  26.9 us
    ppermute x33, starting transfers between devices, swapped(): return lax.ppermute(value, axis, pairs)  24.7 us
    pallas_call x1, Pallas kernels, attention_backward(): pl.pallas_call(functools.partial(attention_backward_kernel, size), grid=(...  23.9 us
    all_to_all x4, waiting for transfers between devices, body(): lax.all_to_all(value.reshape(peers, tokens // peers, features), 'fsdp', s...  18.6 us
    all_gather x1, waiting for transfers between devices, body(): lax.all_gather(jnp.concatenate([columns(w_query), columns(w_key), columns...  18 us
    pallas_call x1, Pallas kernels, attention_forward(): pl.pallas_call(functools.partial(attention_forward_kernel, size), grid=(p...  15.9 us
  transfers between devices with their start and end apart: 41, of which 16 were waited for; matrix products, arithmetic and copies ran while one was open for 16% of the time, Pallas kernels for 8%

profile of v1, /device:TPU:0, one launch (start us, length us, event | category | flops | bytes accessed | tf_op | source)
XLA Modules:
  0.0 686.3 jit_solution(1076204384746547372)
XLA Ops:
  9.8 3.0 collective-permute-start
  17.1 19.9 %collective-permute-done = bf16[512,1024]{1,0:T(8,128)(2,1)S(1)} collective-permute-done((bf16[512,1024]{1,0:T(8,128)(2,1)}, bf16[512,1024]{1,0:T(8,128)(2,1)S(1)}, u32[]{:S(2)}, u32[]{:S(2)}) %collective-permute-start) | collective-permute-done | bytes 1048608 | tf_op jit(solution)/shard_map/ppermute | solution.py:22
  37.1 2.5 convert_reduce_fusion
  39.6 2.5 fusion.7
  42.2 18.0 %all-gather.3.cloned.1.call-done = bf16[1024,1664]{1,0:T(8,128)(2,1)} async-done(((bf16[64,1664]{1,0:T(8,128)(2,1)}), bf16[1024,1664]{1,0:T(8,128)(2,1)}) %all-gather.3.cloned.1.call-update) | async-done | bytes 3407888 | tf_op jit(solution)/shard_map/all_gather | solution.py:501
  61.5 2.5 fusion.5
  65.4 4.8 convolution_convert_fusion.q_ref.k_ref.v_ref
  70.2 15.9 %attention_forward.1 = (bf16[1024,512]{1,0:T(8,128)(2,1)}, f32[4,2,1024]{2,1,0:T(2,128)}) custom-call(bf16[1024,1536]{1,0:T(8,128)(2,1)} %convolution_convert_fusion.q_ref.k_ref.v_ref, bf16[1024,1536]{1,0:T(8,128)(2,1)} %convolution_convert_fusion.q_ref.k_ref.v_ref, bf16[1024,1536]{1,0:T(8,128)(2,1)} %convolution_convert_fusion.q_ref.k_ref.v_ref), custom_call_target="tpu_custom_call" | custom-call | flops 4294967296 | bytes 5242880 | tf_op jit(solution)/shard_map/attention_forward/pallas_call | solution.py:123
  86.1 2.2 constant_dynamic-slice_fusion.11
  88.3 1.5 collective-permute-start.1
  89.8 2.8 gather_fusion.1
  93.2 33.8 %collective-permute-done.7.refs_11_.refs_15_ = bf16[1024,1024]{1,0:T(8,128)(2,1)} collective-permute-done((bf16[1024,1024]{1,0:T(8,128)(2,1)}, bf16[1024,1024]{1,0:T(8,128)(2,1)}, u32[]{:S(2)}, u32[]{:S(2)}) %collective-permute-start.7) | collective-permute-done | bytes 2097184 | tf_op jit(solution)/shard_map/ppermute | solution.py:22
  127.0 2.1 collective-permute-start.13
  129.1 9.1 %collective-permute-done.1 = bf16[512,512]{1,0:T(8,128)(2,1)S(1)} collective-permute-done((bf16[512,512]{1,0:T(8,128)(2,1)S(1)}, bf16[512,512]{1,0:T(8,128)(2,1)S(1)}, u32[]{:S(2)}, u32[]{:S(2)}) %collective-permute-start.1) | collective-permute-done | bytes 524320 | tf_op jit(solution)/shard_map/ppermute | solution.py:22
  139.0 4.8 fusion.51
  143.8 2.8 gather_fusion
  146.6 3.1 broadcast_select_fusion.1
  149.7 6.9 all-to-all-start
  157.6 25.6 %collective-permute-done.10.refs_10_.refs_11_ = bf16[1024,1024]{1,0:T(8,128)(2,1)} collective-permute-done((bf16[1024,1024]{1,0:T(8,128)(2,1)}, bf16[1024,1024]{1,0:T(8,128)(2,1)}, u32[]{:S(2)}, u32[]{:S(2)}) %collective-permute-start.10) | collective-permute-done | bytes 2097184 | tf_op jit(solution)/shard_map/ppermute | solution.py:22
  183.2 44.1 %collective-permute-done.13.refs_14_.refs_15_ = bf16[1024,1024]{1,0:T(8,128)(2,1)} collective-permute-done((bf16[1024,1024]{1,0:T(8,128)(2,1)}, bf16[1024,1024]{1,0:T(8,128)(2,1)}, u32[]{:S(2)}, u32[]{:S(2)}) %collective-permute-start.13) | collective-permute-done | bytes 2097184 | tf_op jit(solution)/shard_map/ppermute | solution.py:22
  227.9 6.2 all-to-all-start.1
  235.4 17.2 %forward_first.1 = (f32[512,1024]{1,0:T(8,128)}, bf16[512,1024]{1,0:T(8,128)(2,1)}, bf16[512,4096]{1,0:T(8,128)(2,1)}, bf16[512,4096]{1,0:T(8,128)(2,1)}) custom-call(bf16[512,1024]{1,0:T(8,128)(2,1)} %bitcast.105, f32[1,1024]{1,0:T(1,128)} %get-tuple-element.192.refs_1_.refs_6_, f32[1,1024]{1,0:T(1,128)} %get-tuple-element.191.refs_2_, ...), custom_call_target="tpu_custom_call" | custom-call | flops 8589934592 | bytes 16777216 | tf_op jit(solution)/shard_map/forward_first/pallas_call | solution.py:312
  252.6 4.4 all-to-all-done.1
  258.0 20.6 %forward_second.1 = (bf16[512,1024]{1,0:T(8,128)(2,1)}, bf16[512,4096]{1,0:T(8,128)(2,1)}, bf16[512,4096]{1,0:T(8,128)(2,1)}, bf16[512,1024]{1,0:T(8,128)(2,1)},...) custom-call(bf16[512,1024]{1,0:T(8,128)(2,1)} %bitcast.106, f32[512,1024]{1,0:T(8,128)} %get-tuple-element.58.refs_1_.refs_7_, ...), custom_call_target="tpu_custom_call" | custom-call | flops 8589934592 | bytes 16777216 | tf_op jit(solution)/shard_map/forward_second/pallas_call | solution.py:312
  278.7 33.3 %backward_second.1 = (f32[512,1024]{1,0:T(8,128)}, bf16[512,1024]{1,0:T(8,128)(2,1)}, f32[8,1024]{1,0:T(8,128)}, f32[8,1,512]{2,1,0:T(1,128)}, bf16[1024,1024]{1...) custom-call(bf16[512,1024]{1,0:T(8,128)(2,1)} %get-tuple-element.60., ...), custom_call_target="tpu_custom_call" | custom-call | flops 17179869184 | bytes 16777216 | tf_op jit(solution)/shard_map/backward_second/pallas_call | solution.py:312
  312.0 32.7 %backward_first.1 = (bf16[512,1024]{1,0:T(8,128)(2,1)}, f32[8,1024]{1,0:T(8,128)}, f32[8,1,512]{2,1,0:T(1,128)}, bf16[1024,1024]{1,0:T(8,128)(2,1)}, bf16[1024,1...) custom-call(bf16[512,1024]{1,0:T(8,128)(2,1)} %get-tuple-element.64., ...), custom_call_target="tpu_custom_call" | custom-call | flops 17179869184 | bytes 16777216 | tf_op jit(solution)/shard_map/backward_first/pallas_call | solution.py:312
  344.8 7.0 %all-to-all-start.3 = ((bf16[16,32,1024]{2,1,0:T(8,128)(2,1)}), bf16[16,32,1024]{2,1,0:T(8,128)(2,1)S(1)}, u32[]{:S(2)}, u32[]{:S(2)}) async-start(bf16[16,32,1024]{2,1,0:T(8,128)(2,1)} %bitcast.109), calls=%async_computation.3 | async-start | bytes 2097152 | tf_op jit(solution)/shard_map/all_to_all | solution.py:537
  353.3 3.2 collective-permute-done.19
  356.6 1.6 collective-permute-start.20
  358.8 1.8 collective-permute-done.20
  360.6 14.1 %all-to-all-done.3 = bf16[16,32,1024]{2,1,0:T(8,128)(2,1)S(1)} async-done(((bf16[16,32,1024]{2,1,0:T(8,128)(2,1)}), bf16[16,32,1024]{2,1,0:T(8,128)(2,1)S(1)}, u32[]{:S(2)}, u32[]{:S(2)}) %all-to-all-start.3) | async-done | bytes 1048608 | tf_op jit(solution)/shard_map/all_to_all | solution.py:537
  374.7 6.9 %all-to-all-start.2 = ((bf16[16,32,1024]{2,1,0:T(8,128)(2,1)}), bf16[16,32,1024]{2,1,0:T(8,128)(2,1)S(1)}, u32[]{:S(2)}, u32[]{:S(2)}) async-start(bf16[16,32,1024]{2,1,0:T(8,128)(2,1)} %bitcast.104), calls=%async_computation.2 | async-start | bytes 2097152 | tf_op jit(solution)/shard_map/all_to_all | solution.py:537
  381.7 2.8 gather_fusion.3
  384.5 3.2 convolution_convert_fusion.5
  388.8 1.5 collective-permute-start.15
  390.3 2.9 convolution_convert_fusion.1
  393.7 4.6 add_convert_fusion
  398.3 5.1 collective-permute-done.15
  403.4 2.6 maximum_select_fusion.2.g_ref
  406.0 23.9 %attention_backward.1 = bf16[3,1024,512]{2,1,0:T(8,128)(2,1)} custom-call(bf16[1024,1536]{1,0:T(8,128)(2,1)} %convolution_convert_fusion.q_ref.k_ref.v_ref, bf16[1024,1536]{1,0:T(8,128)(2,1)} %convolution_convert_fusion.q_ref.k_ref.v_ref, bf16[1024,1536]{1,0:T(8,128)(2,1)} %convolution_convert_fusion.q_ref.k_ref.v_ref, ...), custom_call_target="tpu_custom_call" | custom-call | flops 10737418240 | bytes 8388608 | tf_op jit(solution)/shard_map/attention_backward/pallas_call | solution.py:144
  429.9 2.7 fusion.22
  434.2 5.2 fusion.6
  443.3 2.0 pad_maximum_fusion
  445.3 5.6 copy.65
  450.9 1.6 collective-permute-start.32
  453.7 2.8 gather_fusion.2
  456.5 1.9 dynamic-slice_convert_fusion
  459.0 2.7 add_convert_fusion.1
  461.7 2.7 add_convert_fusion.2
  464.4 1.6 collective-permute-start.29
  466.0 4.2 add_convert_fusion.3
  470.3 51.8 %collective-permute-done.16 = bf16[512,1024]{1,0:T(8,128)(2,1)S(1)} collective-permute-done((bf16[512,1024]{1,0:T(8,128)(2,1)S(1)}, bf16[512,1024]{1,0:T(8,128)(2,1)S(1)}, u32[]{:S(2)}, u32[]{:S(2)}) %collective-permute-start.16) | collective-permute-done | bytes 1048608 | tf_op jit(solution)/shard_map/ppermute | solution.py:22
  522.1 1.6 collective-permute-start.26
  525.1 3.1 fusion.17
  528.2 5.8 add_bitcast_fusion
  533.9 33.1 %collective-permute-done.29 = bf16[1024,1024]{1,0:T(8,128)(2,1)S(1)} collective-permute-done((bf16[1024,1024]{1,0:T(8,128)(2,1)S(1)}, bf16[1024,1024]{1,0:T(8,128)(2,1)S(1)}, u32[]{:S(2)}, u32[]{:S(2)}) %collective-permute-start.29) | collective-permute-done | bytes 2097184 | tf_op jit(solution)/shard_map/ppermute | solution.py:22
  567.0 5.1 add_bitcast_fusion.1
  572.2 39.8 %collective-permute-done.26 = bf16[1024,1024]{1,0:T(8,128)(2,1)S(1)} collective-permute-done((bf16[1024,1024]{1,0:T(8,128)(2,1)S(1)}, bf16[1024,1024]{1,0:T(8,128)(2,1)S(1)}, u32[]{:S(2)}, u32[]{:S(2)}) %collective-permute-start.26) | collective-permute-done | bytes 2097184 | tf_op jit(solution)/shard_map/ppermute | solution.py:22
  611.9 3.4 add_bitcast_fusion.2
  616.3 1.6 collective-permute-start.18
  617.9 39.1 %collective-permute-done.23 = bf16[1024,1024]{1,0:T(8,128)(2,1)} collective-permute-done((bf16[1024,1024]{1,0:T(8,128)(2,1)}, bf16[1024,1024]{1,0:T(8,128)(2,1)}, u32[]{:S(2)}, u32[]{:S(2)}) %collective-permute-start.23) | collective-permute-done | bytes 2097184 | tf_op jit(solution)/shard_map/ppermute | solution.py:22
  657.0 5.7 add_bitcast_fusion.3
  664.6 1.6 collective-permute-start.17
  666.2 9.6 %collective-permute-done.17 = bf16[64,1664]{0,1:T(8,128)(2,1)S(1)} collective-permute-done((bf16[64,1664]{0,1:T(8,128)(2,1)S(1)}, bf16[64,1664]{0,1:T(8,128)(2,1)S(1)}, u32[]{:S(2)}, u32[]{:S(2)}) %collective-permute-start.17) | collective-permute-done | bytes 213024 | tf_op jit(solution)/shard_map/ppermute | solution.py:22
  (221 shorter events, 33.6 us)
Async XLA Ops:
  7.2 32.4 %copy-start.3 = (bf16[1,512,1024]{2,1,0:T(8,128)(2,1)S(1)}, bf16[1,512,1024]{2,1,0:T(8,128)(2,1)}, u32[]{:S(2)}) copy-start(bf16[1,512,1024]{2,1,0:T(8,128)(2,1)} %param.25) | copy-start | bytes 3145732
  7.2 52.9 %all-gather.3.cloned.1.call-start = ((), (), s32[]{:S(2)}) async-start(), calls=%async_computation.6 | async-start | bytes 3620864 | tf_op jit(solution)/shard_map/all_gather | solution.py:501
  9.8 128.4 %all-gather.5.cloned.1.call-start = ((), (), s32[]{:S(2)}) async-start(), calls=%async_computation.7 | async-start | bytes 2228224 | tf_op jit(solution)/shard_map/all_gather | solution.py:507
  9.8 27.2 %collective-permute-start = (bf16[512,1024]{1,0:T(8,128)(2,1)}, bf16[512,1024]{1,0:T(8,128)(2,1)S(1)}, u32[]{:S(2)}, u32[]{:S(2)}) collective-permute-start(bf16[512,1024]{1,0:T(8,128)(2,1)} %bitcast.99), channel_id=1, source_target_pairs={{0,16},{16,0},{1,17},{17,1},{2,18},{18,2},{3,19},{19,3},{4,20},{20... | collective-permute-start | bytes 3145736 | tf_op jit(solution)/shard_map/ppermute | solution.py:22
  12.9 79.7 %collective-permute-start.4 = (bf16[1024,1024]{1,0:T(8,128)(2,1)}, bf16[1024,1024]{1,0:T(8,128)(2,1)}, u32[]{:S(2)}, u32[]{:S(2)}) collective-permute-start(bf16[1024,1024]{1,0:T(8,128)(2,1)} %bitcast.142), channel_id=1, source_target_pairs={{0,16},{16,0},{1,17},{17,1},{2,18},{18,2},{3,19},{19,3},{4,20},{20... | collective-permute-start | bytes 6291464 | tf_op jit(solution)/shard_map/ppermute | solution.py:22
  13.6 143.0 %collective-permute-start.3 = (bf16[1024,1024]{1,0:T(8,128)(2,1)}, bf16[1024,1024]{1,0:T(8,128)(2,1)}, u32[]{:S(2)}, u32[]{:S(2)}) collective-permute-start(bf16[1024,1024]{1,0:T(8,128)(2,1)} %bitcast.143), channel_id=1, source_target_pairs={{0,1},{1,0},{2,3},{3,2},{4,5},{5,4},{6,7},{7,6},{8,9},{9,8},{10,11... | collective-permute-start | bytes 6291464 | tf_op jit(solution)/shard_map/ppermute | solution.py:22
  15.2 77.4 %collective-permute-start.2 = (bf16[7680]{0:T(1024)(128)(2,1)S(1)}, bf16[7680]{0:T(1024)(128)(2,1)S(1)}, u32[]{:S(2)}, u32[]{:S(2)}) collective-permute-start(bf16[7680]{0:T(1024)(128)(2,1)S(1)} %pad_maximum_fusion.3), channel_id=1, source_target_pairs={{0,1},{1,0},{2,3},{3,2},{4,5},{5,4},{6,7},{7,6},{8,9},{9,8},{10,11... | collective-permute-start | bytes 46088 | tf_op jit(solution)/shard_map/ppermute | solution.py:22
  15.7 111.3 %collective-permute-start.7 = (bf16[1024,1024]{1,0:T(8,128)(2,1)}, bf16[1024,1024]{1,0:T(8,128)(2,1)}, u32[]{:S(2)}, u32[]{:S(2)}) collective-permute-start(bf16[1024,1024]{1,0:T(8,128)(2,1)} %bitcast.146), channel_id=1, source_target_pairs={{0,16},{16,0},{1,17},{17,1},{2,18},{18,2},{3,19},{19,3},{4,20},{20... | collective-permute-start | bytes 6291464 | tf_op jit(solution)/shard_map/ppermute | solution.py:22
  37.1 24.4 %copy-start.6 = (bf16[512,1024]{1,0:T(8,128)(2,1)}, bf16[512,1024]{1,0:T(8,128)(2,1)S(1)}, u32[]{:S(2)}) copy-start(bf16[512,1024]{1,0:T(8,128)(2,1)S(1)} %collective-permute-done) | copy-start | bytes 3145732
  88.3 49.9 %collective-permute-start.1 = (bf16[512,512]{1,0:T(8,128)(2,1)S(1)}, bf16[512,512]{1,0:T(8,128)(2,1)S(1)}, u32[]{:S(2)}, u32[]{:S(2)}) collective-permute-start(bf16[512,512]{1,0:T(8,128)(2,1)S(1)} %get-tuple-element.164), channel_id=1, source_target_pairs={{0,16},{16,0},{1,17},{17,1},{2,18},{18,2},{3,19},{19,3},{4,20},{20... | collective-permute-start | bytes 1572872 | tf_op jit(solution)/shard_map/ppermute | solution.py:22
  92.6 65.0 %collective-permute-start.6 = (bf16[1024,1024]{1,0:T(8,128)(2,1)}, bf16[1024,1024]{1,0:T(8,128)(2,1)}, u32[]{:S(2)}, u32[]{:S(2)}) collective-permute-start(bf16[1024,1024]{1,0:T(8,128)(2,1)} %bitcast.147), channel_id=1, source_target_pairs={{0,1},{1,0},{2,3},{3,2},{4,5},{5,4},{6,7},{7,6},{8,9},{9,8},{10,11... | collective-permute-start | bytes 6291464 | tf_op jit(solution)/shard_map/ppermute | solution.py:22
  92.6 90.6 %collective-permute-start.10 = (bf16[1024,1024]{1,0:T(8,128)(2,1)}, bf16[1024,1024]{1,0:T(8,128)(2,1)}, u32[]{:S(2)}, u32[]{:S(2)}) collective-permute-start(bf16[1024,1024]{1,0:T(8,128)(2,1)} %bitcast.134), channel_id=1, source_target_pairs={{0,16},{16,0},{1,17},{17,1},{2,18},{18,2},{3,19},{19,3},{4,20},{20... | collective-permute-start | bytes 6291464 | tf_op jit(solution)/shard_map/ppermute | solution.py:22
  127.0 100.3 %collective-permute-start.13 = (bf16[1024,1024]{1,0:T(8,128)(2,1)}, bf16[1024,1024]{1,0:T(8,128)(2,1)}, u32[]{:S(2)}, u32[]{:S(2)}) collective-permute-start(bf16[1024,1024]{1,0:T(8,128)(2,1)} %bitcast.138), channel_id=1, source_target_pairs={{0,16},{16,0},{1,17},{17,1},{2,18},{18,2},{3,19},{19,3},{4,20},{20... | collective-permute-start | bytes 6291464 | tf_op jit(solution)/shard_map/ppermute | solution.py:22
  138.2 89.2 %collective-permute-start.5 = (bf16[1024,1024]{1,0:T(8,128)(2,1)}, bf16[1024,1024]{1,0:T(8,128)(2,1)}, u32[]{:S(2)}, u32[]{:S(2)}) collective-permute-start(bf16[1024,1024]{1,0:T(8,128)(2,1)} %collective-permute-done.4.refs_7_.refs_11_), channel_id=1, source_target_pairs={{0,1},{1,0},{2,3},{3,2},{4,5},{5,4},{6,7},{7,6},{8,9},{9,8},{10,11... | collective-permute-start | bytes 6291464 | tf_op jit(solution)/shard_map/ppermute | solution.py:22
  149.7 6.9 %copy-start.35 = (s32[1,512]{1,0:T(1,128)S(1)}, s32[1,512]{1,0:T(1,128)}, u32[]{:S(2)}) copy-start(s32[1,512]{1,0:T(1,128)} %param.46) | copy-start | bytes 6148
  149.7 7.7 %copy-start.29 = (bf16[1,2048]{1,0:T(2,128)(2,1)S(1)}, bf16[1,2048]{1,0:T(2,128)(2,1)}, u32[]{:S(2)}) copy-start(bf16[1,2048]{1,0:T(2,128)(2,1)} %param.41) | copy-start | bytes 12292
  149.7 7.7 %copy-start.30 = (bf16[1,2048]{1,0:T(2,128)(2,1)S(1)}, bf16[1,2048]{1,0:T(2,128)(2,1)}, u32[]{:S(2)}) copy-start(bf16[1,2048]{1,0:T(2,128)(2,1)} %param.35) | copy-start | bytes 12292
  149.7 78.2 %all-to-all-start = ((bf16[16,32,1024]{2,1,0:T(8,128)(2,1)}), bf16[16,32,1024]{2,1,0:T(8,128)(2,1)S(1)}, u32[]{:S(2)}, u32[]{:S(2)}) async-start(bf16[16,32,1024]{2,1,0:T(8,128)(2,1)} %bitcast.5), calls=%async_computation | async-start | bytes 2097152 | tf_op jit(solution)/shard_map/all_to_all | solution.py:537
  156.6 78.8 %collective-permute-start.8 = (bf16[1024,1024]{1,0:T(8,128)(2,1)}, bf16[1024,1024]{1,0:T(8,128)(2,1)}, u32[]{:S(2)}, u32[]{:S(2)}) collective-permute-start(bf16[1024,1024]{1,0:T(8,128)(2,1)} %collective-permute-done.7.refs_11_.refs_15_), channel_id=1, source_target_pairs={{0,1},{1,0},{2,3},{3,2},{4,5},{5,4},{6,7},{7,6},{8,9},{9,8},{10,11... | collective-permute-start | bytes 6291464 | tf_op jit(solution)/shard_map/ppermute | solution.py:22
  157.5 95.1 %collective-permute-start.12 = (bf16[1024,1024]{1,0:T(8,128)(2,1)}, bf16[1024,1024]{1,0:T(8,128)(2,1)}, u32[]{:S(2)}, u32[]{:S(2)}) collective-permute-start(bf16[1024,1024]{1,0:T(8,128)(2,1)} %bitcast.139), channel_id=1, source_target_pairs={{0,1},{1,0},{2,3},{3,2},{4,5},{5,4},{6,7},{7,6},{8,9},{9,8},{10,11... | collective-permute-start | bytes 6291464 | tf_op jit(solution)/shard_map/ppermute | solution.py:22
  183.2 69.4 %collective-permute-start.9 = (bf16[1024,1024]{1,0:T(8,128)(2,1)}, bf16[1024,1024]{1,0:T(8,128)(2,1)}, u32[]{:S(2)}, u32[]{:S(2)}) collective-permute-start(bf16[1024,1024]{1,0:T(8,128)(2,1)} %bitcast.135), channel_id=1, source_target_pairs={{0,1},{1,0},{2,3},{3,2},{4,5},{5,4},{6,7},{7,6},{8,9},{9,8},{10,11... | collective-permute-start | bytes 6291464 | tf_op jit(solution)/shard_map/ppermute | solution.py:22
  227.3 25.3 %collective-permute-start.11 = (bf16[1024,1024]{1,0:T(8,128)(2,1)}, bf16[1024,1024]{1,0:T(8,128)(2,1)}, u32[]{:S(2)}, u32[]{:S(2)}) collective-permute-start(bf16[1024,1024]{1,0:T(8,128)(2,1)} %collective-permute-done.10.refs_10_.refs_11_), channel_id=1, source_target_pairs={{0,1},{1,0},{2,3},{3,2},{4,5},{5,4},{6,7},{7,6},{8,9},{9,8},{10,11... | collective-permute-start | bytes 6291464 | tf_op jit(solution)/shard_map/ppermute | solution.py:22
  227.3 25.3 %collective-permute-start.14 = (bf16[1024,1024]{1,0:T(8,128)(2,1)}, bf16[1024,1024]{1,0:T(8,128)(2,1)}, u32[]{:S(2)}, u32[]{:S(2)}) collective-permute-start(bf16[1024,1024]{1,0:T(8,128)(2,1)} %collective-permute-done.13.refs_14_.refs_15_), channel_id=1, source_target_pairs={{0,1},{1,0},{2,3},{3,2},{4,5},{5,4},{6,7},{7,6},{8,9},{9,8},{10,11... | collective-permute-start | bytes 6291464 | tf_op jit(solution)/shard_map/ppermute | solution.py:22
  227.9 7.5 %copy-start.23 = (bf16[16,32,1024]{2,1,0:T(8,128)(2,1)}, bf16[16,32,1024]{2,1,0:T(8,128)(2,1)S(1)}, u32[]{:S(2)}) copy-start(bf16[16,32,1024]{2,1,0:T(8,128)(2,1)S(1)} %all-to-all-done) | copy-start | bytes 3145732
  227.9 29.1 %all-to-all-start.1 = ((bf16[16,32,1024]{2,1,0:T(8,128)(2,1)}), bf16[16,32,1024]{2,1,0:T(8,128)(2,1)S(1)}, u32[]{:S(2)}, u32[]{:S(2)}) async-start(bf16[16,32,1024]{2,1,0:T(8,128)(2,1)} %bitcast.11), calls=%async_computation.1 | async-start | bytes 2097152 | tf_op jit(solution)/shard_map/all_to_all | solution.py:537
  344.7 7.1 %copy-start.4 = (bf16[1,512,1024]{2,1,0:T(8,128)(2,1)S(1)}, bf16[1,512,1024]{2,1,0:T(8,128)(2,1)}, u32[]{:S(2)}) copy-start(bf16[1,512,1024]{2,1,0:T(8,128)(2,1)} %param.25) | copy-start | bytes 3145732
  344.7 7.5 %copy-start.33 = (f32[8,1024]{1,0:T(8,128)S(1)}, f32[8,1024]{1,0:T(8,128)}, u32[]{:S(2)}) copy-start(f32[8,1024]{1,0:T(8,128)} %get-tuple-element.72) | copy-start | bytes 98308
  344.8 8.0 %copy-start.32 = (f32[8,1,512]{2,1,0:T(1,128)S(1)}, f32[8,1,512]{2,1,0:T(1,128)}, u32[]{:S(2)}) copy-start(f32[8,1,512]{2,1,0:T(1,128)} %get-tuple-element.74) | copy-start | bytes 49156
  344.8 8.1 %copy-start.31 = (f32[8,1,512]{2,1,0:T(1,128)S(1)}, f32[8,1,512]{2,1,0:T(1,128)}, u32[]{:S(2)}) copy-start(f32[8,1,512]{2,1,0:T(1,128)} %get-tuple-element.75) | copy-start | bytes 49156
  344.8 8.2 %copy-start.36 = (f32[8,1024]{1,0:T(8,128)S(1)}, f32[8,1024]{1,0:T(8,128)}, u32[]{:S(2)}) copy-start(f32[8,1024]{1,0:T(8,128)} %get-tuple-element.73) | copy-start | bytes 98308
  344.8 30.0 %all-to-all-start.3 = ((bf16[16,32,1024]{2,1,0:T(8,128)(2,1)}), bf16[16,32,1024]{2,1,0:T(8,128)(2,1)S(1)}, u32[]{:S(2)}, u32[]{:S(2)}) async-start(bf16[16,32,1024]{2,1,0:T(8,128)(2,1)} %bitcast.109), calls=%async_computation.3 | async-start | bytes 2097152 | tf_op jit(solution)/shard_map/all_to_all | solution.py:537
  352.3 41.2 %collective-permute-start.31 = (bf16[1024,1024]{1,0:T(8,128)(2,1)}, bf16[1024,1024]{1,0:T(8,128)(2,1)}, u32[]{:S(2)}, u32[]{:S(2)}) collective-permute-start(bf16[1024,1024]{1,0:T(8,128)(2,1)} %get-tuple-element.91), channel_id=1, source_target_pairs={{0,1},{1,0},{2,3},{3,2},{4,5},{5,4},{6,7},{7,6},{8,9},{9,8},{10,11... | collective-permute-start | bytes 6291464 | tf_op jit(solution)/shard_map/ppermute | solution.py:22
  353.1 3.5 collective-permute-start.19
  356.6 4.0 collective-permute-start.20
  358.2 112.0 %collective-permute-start.30 = (bf16[1024,1024]{1,0:T(8,128)(2,1)}, bf16[1024,1024]{1,0:T(8,128)(2,1)}, u32[]{:S(2)}, u32[]{:S(2)}) collective-permute-start(bf16[1024,1024]{1,0:T(8,128)(2,1)} %get-tuple-element.89), channel_id=1, source_target_pairs={{0,1},{1,0},{2,3},{3,2},{4,5},{5,4},{6,7},{7,6},{8,9},{9,8},{10,11... | collective-permute-start | bytes 6291464 | tf_op jit(solution)/shard_map/ppermute | solution.py:22
  358.3 92.6 %collective-permute-start.28 = (bf16[1024,1024]{1,0:T(8,128)(2,1)}, bf16[1024,1024]{1,0:T(8,128)(2,1)}, u32[]{:S(2)}, u32[]{:S(2)}) collective-permute-start(bf16[1024,1024]{1,0:T(8,128)(2,1)} %get-tuple-element.87), channel_id=1, source_target_pairs={{0,1},{1,0},{2,3},{3,2},{4,5},{5,4},{6,7},{7,6},{8,9},{9,8},{10,11... | collective-permute-start | bytes 6291464 | tf_op jit(solution)/shard_map/ppermute | solution.py:22
  358.7 165.7 %collective-permute-start.27 = (bf16[1024,1024]{1,0:T(8,128)(2,1)}, bf16[1024,1024]{1,0:T(8,128)(2,1)}, u32[]{:S(2)}, u32[]{:S(2)}) collective-permute-start(bf16[1024,1024]{1,0:T(8,128)(2,1)} %get-tuple-element.85), channel_id=1, source_target_pairs={{0,1},{1,0},{2,3},{3,2},{4,5},{5,4},{6,7},{7,6},{8,9},{9,8},{10,11... | collective-permute-start | bytes 6291464 | tf_op jit(solution)/shard_map/ppermute | solution.py:22
  374.7 79.0 %all-to-all-start.2 = ((bf16[16,32,1024]{2,1,0:T(8,128)(2,1)}), bf16[16,32,1024]{2,1,0:T(8,128)(2,1)S(1)}, u32[]{:S(2)}, u32[]{:S(2)}) async-start(bf16[16,32,1024]{2,1,0:T(8,128)(2,1)} %bitcast.104), calls=%async_computation.2 | async-start | bytes 2097152 | tf_op jit(solution)/shard_map/all_to_all | solution.py:537
  381.6 233.8 %reduce-scatter.5.cloned.1.call-start = ((), (), s32[]{:S(2)}) async-start(), calls=%async_computation.8 | async-start | bytes 2228224 | tf_op jit(solution)/shard_map/reduce_scatter | solution.py:591
  388.8 14.6 %collective-permute-start.15 = (bf16[512,512]{1,0:T(8,128)(2,1)}, bf16[512,512]{1,0:T(8,128)(2,1)}, u32[]{:S(2)}, u32[]{:S(2)}) collective-permute-start(bf16[512,512]{1,0:T(8,128)(2,1)} %get-tuple-element.162), channel_id=1, source_target_pairs={{0,16},{16,0},{1,17},{17,1},{2,18},{18,2},{3,19},{19,3},{4,20},{20... | collective-permute-start | bytes 1572872 | tf_op jit(solution)/shard_map/ppermute | solution.py:22
  393.3 270.1 %reduce-scatter.7.cloned.1.call-start = ((), (), s32[]{:S(2)}) async-start(), calls=%async_computation.9 | async-start | bytes 3620864
  393.5 64.9 %collective-permute-start.25 = (bf16[1024,1024]{1,0:T(8,128)(2,1)}, bf16[1024,1024]{1,0:T(8,128)(2,1)}, u32[]{:S(2)}, u32[]{:S(2)}) collective-permute-start(bf16[1024,1024]{1,0:T(8,128)(2,1)} %get-tuple-element.83), channel_id=1, source_target_pairs={{0,1},{1,0},{2,3},{3,2},{4,5},{5,4},{6,7},{7,6},{8,9},{9,8},{10,11... | collective-permute-start | bytes 6291464 | tf_op jit(solution)/shard_map/ppermute | solution.py:22
  393.7 9.7 %copy-start.21 = (bf16[512,512]{1,0:T(8,128)(2,1)S(1)}, bf16[512,512]{1,0:T(8,128)(2,1)}, u32[]{:S(2)}) copy-start(bf16[512,512]{1,0:T(8,128)(2,1)} %get-tuple-element.161) | copy-start | bytes 1572868
  403.4 61.0 %collective-permute-start.22 = (bf16[1024,1024]{1,0:T(8,128)(2,1)}, bf16[1024,1024]{1,0:T(8,128)(2,1)}, u32[]{:S(2)}, u32[]{:S(2)}) collective-permute-start(bf16[1024,1024]{1,0:T(8,128)(2,1)} %get-tuple-element.79), channel_id=1, source_target_pairs={{0,1},{1,0},{2,3},{3,2},{4,5},{5,4},{6,7},{7,6},{8,9},{9,8},{10,11... | collective-permute-start | bytes 6291464 | tf_op jit(solution)/shard_map/ppermute | solution.py:22
  406.0 23.9 %copy-start.28 = (bf16[1024,1664]{1,0:T(8,128)(2,1)S(1)}, bf16[1024,1664]{1,0:T(8,128)(2,1)}, u32[]{:S(2)}) copy-start(bf16[1024,1664]{1,0:T(8,128)(2,1)} %all-gather.3.cloned.1.call-done) | copy-start | bytes 10223620
  434.2 5.2 copy-start.20
  450.9 73.6 %collective-permute-start.32 = (bf16[1024,1024]{1,0:T(8,128)(2,1)}, bf16[1024,1024]{1,0:T(8,128)(2,1)}, u32[]{:S(2)}, u32[]{:S(2)}) collective-permute-start(bf16[1024,1024]{1,0:T(8,128)(2,1)} %add_convert_fusion), channel_id=1, source_target_pairs={{0,16},{16,0},{1,17},{17,1},{2,18},{18,2},{3,19},{19,3},{4,20},{20... | collective-permute-start | bytes 6291464 | tf_op jit(solution)/shard_map/ppermute | solution.py:22
  458.4 63.6 %collective-permute-start.16 = (bf16[512,1024]{1,0:T(8,128)(2,1)S(1)}, bf16[512,1024]{1,0:T(8,128)(2,1)S(1)}, u32[]{:S(2)}, u32[]{:S(2)}) collective-permute-start(bf16[512,1024]{1,0:T(8,128)(2,1)S(1)} %dynamic-slice_convert_fusion), channel_id=1, source_target_pairs={{0,16},{16,0},{1,17},{17,1},{2,18},{18,2},{3,19},{19,3},{4,20},{20... | collective-permute-start | bytes 3145736 | tf_op jit(solution)/shard_map/ppermute | solution.py:22
  461.7 4.3 copy-start.17
  464.4 102.6 %collective-permute-start.29 = (bf16[1024,1024]{1,0:T(8,128)(2,1)S(1)}, bf16[1024,1024]{1,0:T(8,128)(2,1)S(1)}, u32[]{:S(2)}, u32[]{:S(2)}) collective-permute-start(bf16[1024,1024]{1,0:T(8,128)(2,1)S(1)} %add_convert_fusion.1), channel_id=1, source_target_pairs={{0,16},{16,0},{1,17},{17,1},{2,18},{18,2},{3,19},{19,3},{4,20},{20... | collective-permute-start | bytes 6291464 | tf_op jit(solution)/shard_map/ppermute | solution.py:22
  466.0 57.6 %copy-start.8 = (f32[1024,1024]{1,0:T(8,128)S(1)}, f32[1024,1024]{1,0:T(8,128)}, u32[]{:S(2)}) copy-start(f32[1024,1024]{1,0:T(8,128)} %get-tuple-element.207) | copy-start | bytes 12582916
  470.2 54.8 %copy-start.10 = (bf16[512,1024]{1,0:T(8,128)(2,1)S(1)}, bf16[512,1024]{1,0:T(8,128)(2,1)}, u32[]{:S(2)}) copy-start(bf16[512,1024]{1,0:T(8,128)(2,1)} %gather_fusion.3) | copy-start | bytes 3145732
  470.2 54.8 %copy-start.11 = (bf16[512,1024]{1,0:T(8,128)(2,1)S(1)}, bf16[512,1024]{1,0:T(8,128)(2,1)}, u32[]{:S(2)}) copy-start(bf16[512,1024]{1,0:T(8,128)(2,1)} %gather_fusion.2) | copy-start | bytes 3145732
  470.2 54.8 %copy-start.22 = (f32[512,1024]{1,0:T(8,128)S(1)}, f32[512,1024]{1,0:T(8,128)}, u32[]{:S(2)}) copy-start(f32[512,1024]{1,0:T(8,128)} %get-tuple-element.206) | copy-start | bytes 6291460
  470.2 101.9 %collective-permute-start.24 = (bf16[1024,1024]{1,0:T(8,128)(2,1)S(1)}, bf16[1024,1024]{1,0:T(8,128)(2,1)S(1)}, u32[]{:S(2)}, u32[]{:S(2)}) collective-permute-start(bf16[1024,1024]{1,0:T(8,128)(2,1)S(1)} %copy-done.37), channel_id=1, source_target_pairs={{0,1},{1,0},{2,3},{3,2},{4,5},{5,4},{6,7},{7,6},{8,9},{9,8},{10,11... | collective-permute-start | bytes 6291464 | tf_op jit(solution)/shard_map/ppermute | solution.py:22
  522.1 89.9 %collective-permute-start.26 = (bf16[1024,1024]{1,0:T(8,128)(2,1)S(1)}, bf16[1024,1024]{1,0:T(8,128)(2,1)S(1)}, u32[]{:S(2)}, u32[]{:S(2)}) collective-permute-start(bf16[1024,1024]{1,0:T(8,128)(2,1)S(1)} %add_convert_fusion.2), channel_id=1, source_target_pairs={{0,16},{16,0},{1,17},{17,1},{2,18},{18,2},{3,19},{19,3},{4,20},{20... | collective-permute-start | bytes 6291464 | tf_op jit(solution)/shard_map/ppermute | solution.py:22
  524.4 93.5 %collective-permute-start.21 = (bf16[1024,1024]{1,0:T(8,128)(2,1)}, bf16[1024,1024]{1,0:T(8,128)(2,1)}, u32[]{:S(2)}, u32[]{:S(2)}) collective-permute-start(bf16[1024,1024]{1,0:T(8,128)(2,1)} %get-tuple-element.77), channel_id=1, source_target_pairs={{0,1},{1,0},{2,3},{3,2},{4,5},{5,4},{6,7},{7,6},{8,9},{9,8},{10,11... | collective-permute-start | bytes 6291464 | tf_op jit(solution)/shard_map/ppermute | solution.py:22
  524.5 132.5 %collective-permute-start.23 = (bf16[1024,1024]{1,0:T(8,128)(2,1)}, bf16[1024,1024]{1,0:T(8,128)(2,1)}, u32[]{:S(2)}, u32[]{:S(2)}) collective-permute-start(bf16[1024,1024]{1,0:T(8,128)(2,1)} %add_convert_fusion.3), channel_id=1, source_target_pairs={{0,16},{16,0},{1,17},{17,1},{2,18},{18,2},{3,19},{19,3},{4,20},{20... | collective-permute-start | bytes 6291464 | tf_op jit(solution)/shard_map/ppermute | solution.py:22
  528.1 38.8 %copy-start.13 = (bf16[1024,1024]{1,0:T(8,128)(2,1)S(1)}, bf16[1024,1024]{1,0:T(8,128)(2,1)}, u32[]{:S(2)}) copy-start(bf16[1024,1024]{1,0:T(8,128)(2,1)} %get-tuple-element.84) | copy-start | bytes 6291460
  567.0 44.9 %copy-start.15 = (bf16[1024,1024]{1,0:T(8,128)(2,1)S(1)}, bf16[1024,1024]{1,0:T(8,128)(2,1)}, u32[]{:S(2)}) copy-start(bf16[1024,1024]{1,0:T(8,128)(2,1)} %get-tuple-element.80) | copy-start | bytes 6291460
  611.9 45.0 %copy-start.12 = (bf16[1024,1024]{1,0:T(8,128)(2,1)S(1)}, bf16[1024,1024]{1,0:T(8,128)(2,1)}, u32[]{:S(2)}) copy-start(bf16[1024,1024]{1,0:T(8,128)(2,1)} %get-tuple-element.76) | copy-start | bytes 6291460
  616.3 46.3 %collective-permute-start.18 = (f32[64,1024]{1,0:T(8,128)S(1)}, f32[64,1024]{1,0:T(8,128)S(1)}, u32[]{:S(2)}, u32[]{:S(2)}) collective-permute-start(f32[64,1024]{1,0:T(8,128)S(1)} %convert_element_type.201), channel_id=1, source_target_pairs={{0,16},{16,0},{1,17},{17,1},{2,18},{18,2},{3,19},{19,3},{4,20},{20... | collective-permute-start | bytes 786440 | tf_op jit(solution)/shard_map/ppermute | solution.py:22
  657.0 5.7 copy-start.25
  664.6 11.3 %collective-permute-start.17 = (bf16[64,1664]{0,1:T(8,128)(2,1)S(1)}, bf16[64,1664]{0,1:T(8,128)(2,1)S(1)}, u32[]{:S(2)}, u32[]{:S(2)}) collective-permute-start(bf16[64,1664]{0,1:T(8,128)(2,1)S(1)} %copy.66), channel_id=1, source_target_pairs={{0,16},{16,0},{1,17},{17,1},{2,18},{18,2},{3,19},{19,3},{4,20},{20... | collective-permute-start | bytes 638984 | tf_op jit(solution)/shard_map/ppermute | solution.py:22
  (18 other events, 44.6 us)
Sparse Core Ops, SparseCore 0:
  10.9 49.1 all-gather.2
  62.3 40.2 all-gather.4
  393.4 64.8 reduce-scatter.4
  462.5 68.8 reduce-scatter.6

commit v2 on v1

--- a/solution.py
+++ b/solution.py
@@ -20,6 +20,10 @@
 def swapped(value, axis):
     pairs = [(source, source ^ 1) for source in range(lax.axis_size(axis))]
     return lax.ppermute(value, axis, pairs)
+
+
+def after(value, *others):
+    return lax.optimization_barrier((value, *others))[0]
 
 
 def dot_last(left, right):
@@ -162,20 +166,22 @@
     )(qkv, qkv, qkv, grad, logs)
 
 
-def stream(step, steps, parts, pairs, buffers, sems):
-    per = steps // parts
-
+def stream(step, steps, pairs, buffers, sems):
     def fetch(which):
         slot = lax.rem(which, 2)
-        row = pl.multiple_of(lax.rem(which, per) * CHUNK, CHUNK)
-        for quarter in range(parts):
-
-            @pl.when(which // per == quarter)
-            def _():
-                for m, refs in enumerate(pairs):
+        for m, refs in enumerate(pairs):
+            first = 0
+            for ref in refs:
+                count = ref.shape[0] // CHUNK
+
+                @pl.when(jnp.logical_and(which >= first, which < first + count))
+                def _(m=m, ref=ref, first=first):
+                    row = pl.multiple_of((which - first) * CHUNK, CHUNK)
                     pltpu.make_async_copy(
-                        refs[quarter].at[pl.ds(row, CHUNK)], buffers[m].at[slot], sems.at[m, slot]
+                        ref.at[pl.ds(row, CHUNK)], buffers[m].at[slot], sems.at[m, slot]
                     ).start()
+
+                first += count
 
     @pl.when(step == 0)
     def _():
@@ -199,42 +205,43 @@
     return inner * cdf, slope
 
 
-def forward_first_kernel(parts, steps, *refs):
-    z_ref, gain_ref, shift_ref, bias_ref, out_bias_ref = refs[:5]
-    win, wout = refs[5 : 5 + parts], refs[5 + parts : 5 + 2 * parts]
-    first_ref, normed_ref, active_ref, slope_ref, in_buf, out_buf, sems = refs[5 + 2 * parts :]
+def forward_first_kernel(ins, count, steps, *refs):
+    z_ref, gain_ref, shift_ref, out_bias_ref, gain_two, shift_two, bias_ref = refs[:7]
+    win, wout = refs[7 : 7 + ins], refs[7 + ins : 7 + count]
+    first_ref, normed_ref, active_ref, slope_ref, normed_two = refs[7 + count : 12 + count]
+    in_buf, out_buf, sems = refs[12 + count :]
     step = pl.program_id(0)
 
     @pl.when(step == 0)
     def _():
-        xhat, _ = normalised(z_ref[...].astype(F32))
+        z = z_ref[...].astype(F32)
+        xhat, _ = normalised(z)
         normed_ref[...] = (xhat * gain_ref[...] + shift_ref[...]).astype(BF16)
         first_ref[...] = jnp.broadcast_to(out_bias_ref[...], first_ref.shape)
 
-    slot = stream(step, steps, parts, (win, wout), (in_buf, out_buf), sems)
+    slot = stream(step, steps, (win, wout), (in_buf, out_buf), sems)
     active, slope = gelu_parts(dot_last(normed_ref[...], in_buf[slot]) + bias_ref[0])
     low = active.astype(BF16)
     active_ref[...] = low
     slope_ref[...] = slope.astype(BF16)
     first_ref[...] += dot(low, out_buf[slot])
 
-
-def forward_second_kernel(parts, steps, *refs):
-    z_ref, first_ref, cot_ref, centre_ref, gain_ref, shift_ref, bias_ref, out_bias_ref = refs[:8]
-    win, wout = refs[8 : 8 + parts], refs[8 + parts : 8 + 2 * parts]
-    normed_ref, active_ref, slope_ref, gated_ref, grad_ref, score_ref = refs[
-        8 + 2 * parts : 14 + 2 * parts
-    ]
-    total, in_buf, out_buf, sems = refs[14 + 2 * parts :]
+    @pl.when(step == steps - 1)
+    def _():
+        xhat, _ = normalised(z_ref[...].astype(F32) + first_ref[...])
+        normed_two[...] = (xhat * gain_two[...] + shift_two[...]).astype(BF16)
+
+
+def forward_second_kernel(parts, steps, normed_ref, bias_ref, *refs):
+    win, wout = refs[:parts], refs[parts : 2 * parts]
+    part_ref, active_ref, slope_ref, total, in_buf, out_buf, sems = refs[2 * parts :]
     step = pl.program_id(0)
 
     @pl.when(step == 0)
     def _():
-        xhat, _ = normalised(z_ref[...].astype(F32) + first_ref[...])
-        normed_ref[...] = (xhat * gain_ref[...] + shift_ref[...]).astype(BF16)
-        total[...] = first_ref[...] + out_bias_ref[...]
-
-    slot = stream(step, steps, parts, (win, wout), (in_buf, out_buf), sems)
+        total[...] = jnp.zeros_like(total)
+
+    slot = stream(step, steps, (win, wout), (in_buf, out_buf), sems)
     active, slope = gelu_parts(dot_last(normed_ref[...], in_buf[slot]) + bias_ref[0])
     low = active.astype(BF16)
     active_ref[...] = low
@@ -243,40 +250,42 @@
 
     @pl.when(step == steps - 1)
     def _():
-        branch = total[...]
-        grad_gated = cot_ref[...].astype(F32)
-        logit = jnp.sum(z_ref[...].astype(F32) * centre_ref[...], axis=-1, keepdims=True)
-        gate = jax.nn.sigmoid(logit)
-        gated_ref[...] = (gate * branch).astype(BF16)
-        grad_ref[...] = (gate * grad_gated).astype(BF16)
-        grad_gate = jnp.sum(grad_gated * branch, axis=-1, keepdims=True)
-        score_ref[...] = jnp.broadcast_to(grad_gate * gate * (1.0 - gate), score_ref.shape)
-
-
-def backward_kernel(second, parts, steps, *refs):
-    grad_ref, normed_ref, active_ref, slope_ref, z_ref, centre_ref, gain_ref = refs[:7]
-    extra_one, extra_two = refs[7:9]
-    win, wout = refs[9 : 9 + parts], refs[9 + parts : 9 + 2 * parts]
-    base = 9 + 2 * parts
-    result = refs[base : base + (2 if second else 1)]
-    base += len(result)
-    vector_ref, bias_ref = refs[base : base + 2]
-    gwin, gwout = refs[base + 2 : base + 2 + parts], refs[base + 2 + parts : base + 2 + 2 * parts]
-    total, in_buf, out_buf, sems = refs[base + 2 + 2 * parts :]
+        part_ref[...] = total[...].astype(part_ref.dtype)
+
+
+def backward_second_kernel(parts, steps, grad_ref, slope_ref, *refs):
+    win, wout = refs[:parts], refs[parts : 2 * parts]
+    part_ref, inner_ref, total, in_buf, out_buf, sems = refs[2 * parts :]
+    step = pl.program_id(0)
+
+    @pl.when(step == 0)
+    def _():
+        total[...] = jnp.zeros_like(total)
+
+    slot = stream(step, steps, (win, wout), (in_buf, out_buf), sems)
+    inner = (slope_ref[...].astype(F32) * dot_last(grad_ref[...], out_buf[slot])).astype(BF16)
+    inner_ref[...] = inner
+    total[...] += dot(inner, in_buf[slot])
+
+    @pl.when(step == steps - 1)
+    def _():
+        part_ref[...] = total[...].astype(part_ref.dtype)
+
+
+def weights_second_kernel(parts, steps, *refs):
+    inner, active, normed, grad = refs[:2], refs[2:4], refs[4:6], refs[6:8]
+    bias_ref = refs[8]
+    gwin, gwout = refs[9 : 9 + parts], refs[9 + parts : 9 + 2 * parts]
     step = pl.program_id(0)
     per = steps // parts
-
-    @pl.when(step == 0)
-    def _():
-        total[...] = jnp.zeros_like(total)
-
-    slot = stream(step, steps, parts, (win, wout), (in_buf, out_buf), sems)
-    grad = grad_ref[...]
-    inner = (slope_ref[...].astype(F32) * dot_last(grad, out_buf[slot])).astype(BF16)
-    bias_ref[0] = jnp.sum(inner.astype(F32), axis=0, keepdims=True)
-    total[...] += dot(inner, in_buf[slot])
-    grad_out = dot_first(active_ref[...], grad).astype(BF16)
-    grad_in = dot_first(inner, normed_ref[...]).astype(BF16)
+    one, two = inner[0][...], inner[1][...]
+    bias_ref[0] = jnp.sum(one.astype(F32), axis=0, keepdims=True) + jnp.sum(
+        two.astype(F32), axis=0, keepdims=True
+    )
+    grad_in = (dot_first(one, normed[0][...]) + dot_first(two, normed[1][...])).astype(BF16)
+    grad_out = (
+        dot_first(active[0][...], grad[0][...]) + dot_first(active[1][...], grad[1][...])
+    ).astype(BF16)
     for quarter in range(parts):
 
         @pl.when(step // per == quarter)
@@ -284,31 +293,73 @@
             gwin[quarter][...] = grad_in
             gwout[quarter][...] = grad_out
 
+
+def backward_first_kernel(ins, count, parts, steps, *refs):
+    own_ref, arrived_ref, grad_two_ref, z_ref, first_ref, cot_ref, score_ref = refs[:7]
+    normed_ref, active_ref, slope_ref, gain_ref, gain_two, centre_ref = refs[7:13]
+    win, wout = refs[13 : 13 + ins], refs[13 + ins : 13 + count]
+    sent_ref, vector_ref, bias_ref = refs[13 + count : 16 + count]
+    rest = refs[16 + count :]
+    gwin, gwout = rest[:parts], rest[parts : 2 * parts]
+    total, grad_in, grad_low, in_buf, out_buf, sems = rest[2 * parts :]
+    step = pl.program_id(0)
+    per = steps // parts
+    down = lambda value: jnp.sum(value, axis=0, keepdims=True)
+
+    @pl.when(step == 0)
+    def _():
+        total[...] = jnp.zeros_like(total)
+        z = z_ref[...].astype(F32)
+        xhat, rate = normalised(z + first_ref[...])
+        grad_normed = own_ref[...] + arrived_ref[...].astype(F32)
+        grad_rows = norm_back(grad_normed, xhat, rate, gain_two[...])
+        grad_in[...] = grad_rows
+        gate = jax.nn.sigmoid(jnp.sum(z * centre_ref[...], axis=-1, keepdims=True))
+        low = (gate * cot_ref[...].astype(F32) + grad_rows).astype(BF16)
+        grad_low[...] = low
+        vector_ref[2:3] = down(low.astype(F32))
+        vector_ref[3:4] = down(grad_normed * xhat)
+        vector_ref[4:5] = down(grad_normed)
+        vector_ref[5:6] = down(grad_two_ref[...].astype(F32))
+        vector_ref[6:7] = down(score_ref[:, 0:1] * z)
+        vector_ref[7:8] = jnp.zeros_like(vector_ref[7:8])
+
+    slot = stream(step, steps, (win, wout), (in_buf, out_buf), sems)
+    grad = grad_low[...]
+    inner = (slope_ref[...].astype(F32) * dot_last(grad, out_buf[slot])).astype(BF16)
+    bias_ref[0] = down(inner.astype(F32))
+    total[...] += dot(inner, in_buf[slot])
+    low_out = dot_first(active_ref[...], grad).astype(BF16)
+    low_in = dot_first(inner, normed_ref[...]).astype(BF16)
+    for quarter in range(parts):
+
+        @pl.when(step // per == quarter)
+        def _():
+            gwin[quarter][...] = low_in
+            gwout[quarter][...] = low_out
+
     @pl.when(step == steps - 1)
     def _():
-        z = z_ref[...].astype(F32)
-        source = z + extra_one[...] if second else z
-        xhat, rate = normalised(source)
+        xhat, rate = normalised(z_ref[...].astype(F32))
         grad_normed = total[...]
+        vector_ref[0:1] = down(grad_normed * xhat)
+        vector_ref[1:2] = down(grad_normed)
         grad_rows = norm_back(grad_normed, xhat, rate, gain_ref[...])
-        vector_ref[...] = jnp.zeros_like(vector_ref)
-        vector_ref[0:1] = jnp.sum(grad_normed * xhat, axis=0, keepdims=True)
-        vector_ref[1:2] = jnp.sum(grad_normed, axis=0, keepdims=True)
-        vector_ref[2:3] = jnp.sum(grad.astype(F32), axis=0, keepdims=True)
-        if second:
-            gate = jax.nn.sigmoid(jnp.sum(z * centre_ref[...], axis=-1, keepdims=True))
-            result[0][...] = grad_rows
-            result[1][...] = (gate * extra_two[...].astype(F32) + grad_rows).astype(BF16)
-        else:
-            score = extra_two[:, 0:1]
-            vector_ref[3:4] = jnp.sum(score * z, axis=0, keepdims=True)
-            result[0][...] = (extra_one[...] + grad_rows + score * centre_ref[...]).astype(BF16)
-
-
-def expert_call(kernel, name, steps, rows, inputs, weights, outs, scratch, flops):
+        score = score_ref[:, 0:1]
+        sent_ref[...] = (grad_in[...] + grad_rows + score * centre_ref[...]).astype(BF16)
+
+
+def expert_call(kernel, name, steps, inputs, weights, outs, scratch, flops):
     whole = lambda shape: pl.BlockSpec(shape, lambda c: (0,) * len(shape))
     spec = lambda shape, block, at: whole(shape) if block is None else pl.BlockSpec(block, at)
-    features = weights[0].shape[1]
+    if weights:
+        features = weights[0].shape[1]
+        scratch = scratch + [
+            pltpu.VMEM((2, CHUNK, features), BF16),
+            pltpu.VMEM((2, CHUNK, features), BF16),
+            pltpu.SemaphoreType.DMA((2, 2)),
+        ]
+    moved = sum(a.size * a.dtype.itemsize for a, _, _ in inputs + outs)
     return pl.pallas_call(
         kernel,
         grid=(steps,),
@@ -316,145 +367,128 @@
         in_specs=[spec(a.shape, b, m) for a, b, m in inputs]
         + [pl.BlockSpec(memory_space=pl.ANY)] * len(weights),
         out_specs=tuple(spec(s.shape, b, m) for s, b, m in outs),
-        scratch_shapes=scratch
-        + [
-            pltpu.VMEM((2, CHUNK, features), BF16),
-            pltpu.VMEM((2, CHUNK, features), BF16),
-            pltpu.SemaphoreType.DMA((2, 2)),
-        ],
+        scratch_shapes=scratch,
         compiler_params=pltpu.CompilerParams(vmem_limit_bytes=VMEM_LIMIT),
         cost_estimate=pl.CostEstimate(
-            flops=flops, bytes_accessed=2 * sum(w.size for w in weights), transcendentals=0
+            flops=2 * flops,
+            bytes_accessed=moved + 2 * sum(w.size for w in weights),
+            transcendentals=0,
         ),
         name=name,
     )(*[a for a, _, _ in inputs], *weights)
 
 
-def expert(z, cot, vectors, biases, one, two):
+def expert(z, cot, vectors, biases, one, two, over):
     rows, features = z.shape
-    parts = len(one[0])
-    hidden = sum(w.shape[0] for w in one[0])
+    hidden = biases.shape[1]
     steps = hidden // CHUNK
-    per = steps // parts
+    near = steps // 2
     line = lambda i: (vectors[i : i + 1], None, None)
+    flat = lambda array: (array, None, None)
     shape = jax.ShapeDtypeStruct
+    low_rows, wide_rows = flat(shape((rows, features), BF16)), flat(shape((rows, features), F32))
     wide = ((rows, CHUNK), lambda c: (0, c))
     thin = ((1, 1, CHUNK), lambda c: (c, 0, 0))
     chunked = biases.reshape(2, steps, 1, CHUNK)
-    hidden_out = [
-        (shape((rows, features), BF16), None, None),
-        (shape((rows, hidden), BF16), *wide),
-        (shape((rows, hidden), BF16), *wide),
-    ]
     matmul = 2 * rows * hidden * features
-    first, normed_one, active_one, slope_one = expert_call(
-        functools.partial(forward_first_kernel, parts, steps),
-        "forward_first",
-        steps,
-        rows,
-        [(z, None, None), line(0), line(1), (chunked[0], *thin), line(2)],
-        one[0] + one[1],
-        [(shape((rows, features), F32), None, None)] + hidden_out,
-        [],
-        2 * matmul,
-    )
-    normed_two, active_two, slope_two, gated, grad_second, score = expert_call(
-        functools.partial(forward_second_kernel, parts, steps),
-        "forward_second",
-        steps,
-        rows,
-        [
-            (z, None, None),
-            (first, None, None),
-            (cot, None, None),
-            line(6),
-            line(3),
-            line(4),
-            (chunked[1], *thin),
-            line(5),
-        ],
-        two[0] + two[1],
-        hidden_out
-        + [
-            (shape((rows, features), BF16), None, None),
-            (shape((rows, features), BF16), None, None),
-            (shape((rows, 128), F32), None, None),
-        ],
-        [pltpu.VMEM((rows, features), F32)],
-        2 * matmul,
-    )
-
-    def quarter_outs():
+
+    def quarter_outs(parts, count):
+        per = count // parts
         return [
             (
-                shape((hidden // parts, features), BF16),
+                shape((per * CHUNK, features), BF16),
                 (CHUNK, features),
                 lambda c, q=q: (jnp.clip(c - q * per, 0, per - 1), 0),
             )
             for q in range(parts)
         ]
 
-    sums = [
-        (shape((8, features), F32), None, None),
-        (shape((steps, 1, CHUNK), F32), *thin),
-    ]
-
-    def back(second, grad, normed, active, slope, gain, extra_one, extra_two, weights, results):
-        outs = expert_call(
-            functools.partial(backward_kernel, second, parts, steps),
-            "backward_second" if second else "backward_first",
-            steps,
-            rows,
-            [
-                (grad, None, None),
-                (normed, None, None),
-                (active, *wide),
-                (slope, *wide),
-                (z, None, None),
-                line(6),
-                line(gain),
-                (extra_one, None, None),
-                (extra_two, None, None),
-            ],
-            weights[0] + weights[1],
-            results + sums + quarter_outs() + quarter_outs(),
+    lines = [line(i) for i in range(7)]
+    counts = len(one[0]), len(one[0]) + len(one[1])
+    wide_z, wide_cot = z.astype(F32), cot.astype(F32)
+    gate = jax.nn.sigmoid(jnp.sum(wide_z * vectors[6], axis=-1, keepdims=True))
+    grad_two = (gate * wide_cot).astype(BF16)
+    grad_far = over(grad_two)
+    first, normed_one, active_one, slope_one, normed_two = expert_call(
+        functools.partial(forward_first_kernel, *counts, steps),
+        "forward_first",
+        steps,
+        [flat(z)] + lines[:5] + [(chunked[0], *thin)],
+        one[0] + one[1],
+        [wide_rows, low_rows] + [(shape((rows, hidden), BF16), *wide)] * 2 + [low_rows],
+        [],
+        2 * matmul,
+    )
+    normed_far = over(after(normed_two, grad_far))
+
+    def forward_second(normed, kind):
+        return expert_call(
+            functools.partial(forward_second_kernel, 2, near),
+            "forward_second",
+            near,
+            [flat(normed), (chunked[1, :near], *thin)],
+            two[0] + two[1],
+            [flat(shape((rows, features), kind))]
+            + [(shape((rows, hidden // 2), BF16), *wide)] * 2,
             [pltpu.VMEM((rows, features), F32)],
-            4 * matmul,
+            matmul,
         )
-        n = len(results)
-        tail = outs[n + 2 :]
-        return outs[:n], outs[n], outs[n + 1].reshape(hidden), tail[:parts], tail[parts:]
-
-    (grad_in_two, grad_first), sums_two, bias_two, gwin_two, gwout_two = back(
-        True,
-        grad_second,
-        normed_two,
-        active_two,
-        slope_two,
-        3,
-        first,
-        cot,
-        two,
+
+    def backward_second(grad, slope, kind):
+        return expert_call(
+            functools.partial(backward_second_kernel, 2, near),
+            "backward_second",
+            near,
+            [flat(grad), (slope, *wide)],
+            two[0] + two[1],
+            [flat(shape((rows, features), kind)), (shape((rows, hidden // 2), BF16), *wide)],
+            [pltpu.VMEM((rows, features), F32)],
+            matmul,
+        )
+
+    own_part, active_own, slope_own = forward_second(normed_two, F32)
+    far_part, active_far, slope_far = forward_second(normed_far, BF16)
+    grad_far_part, inner_far = backward_second(grad_far, slope_far, BF16)
+    grad_own_part, inner_own = backward_second(grad_two, slope_own, F32)
+    outs = expert_call(
+        functools.partial(weights_second_kernel, 2, near),
+        "weights_second",
+        near,
+        [(a, *wide) for a in (inner_own, inner_far, active_own, active_far)]
+        + [flat(a) for a in (normed_two, normed_far, grad_two, grad_far)],
+        [],
+        [(shape((near, 1, CHUNK), F32), *thin)] + quarter_outs(2, near) + quarter_outs(2, near),
+        [],
+        2 * matmul,
+    )
+    bias_two, gwin_two, gwout_two = outs[0].reshape(hidden // 2), outs[1:3], outs[3:5]
+
+    branch = first + (own_part + over(far_part).astype(F32) + vectors[5])
+    gated = (gate * branch).astype(BF16)
+    grad_gate = jnp.sum(wide_cot * branch, axis=-1, keepdims=True)
+    score = jnp.broadcast_to(grad_gate * gate * (1.0 - gate), (rows, 128))
+
+    grad_arrived = after(over(grad_far_part), outs[0])
+    outs = expert_call(
+        functools.partial(backward_first_kernel, *counts, 4, steps),
+        "backward_first",
+        steps,
+        [flat(a) for a in (grad_own_part, grad_arrived, grad_two, z, first, cot, score)]
+        + [flat(normed_one), (active_one, *wide), (slope_one, *wide)]
+        + [line(0), line(3), line(6)],
+        one[0] + one[1],
+        [low_rows, flat(shape((8, features), F32)), (shape((steps, 1, CHUNK), F32), *thin)]
+        + quarter_outs(4, steps)
+        + quarter_outs(4, steps),
         [
-            (shape((rows, features), F32), None, None),
-            (shape((rows, features), BF16), None, None),
+            pltpu.VMEM((rows, features), F32),
+            pltpu.VMEM((rows, features), F32),
+            pltpu.VMEM((rows, features), BF16),
         ],
-    )
-    (grad_sent,), sums_one, bias_one, gwin_one, gwout_one = back(
-        False,
-        grad_first,
-        normed_one,
-        active_one,
-        slope_one,
-        0,
-        grad_in_two,
-        score,
-        one,
-        [(shape((rows, features), BF16), None, None)],
-    )
-    vector_grads = jnp.concatenate([sums_one[:3], sums_two[:3], sums_one[3:4]], axis=0)
-    bias_grads = jnp.stack([bias_one, bias_two])
-    return gated, grad_sent, vector_grads, bias_grads, (gwin_one, gwout_one), (gwin_two, gwout_two)
+        4 * matmul,
+    )
+    grad_sent, sums, bias_one = outs[0], outs[1], outs[2].reshape(hidden)
+    return gated, grad_sent, sums[:7], bias_one, bias_two, (outs[3:7], outs[7:11]), (gwin_two, gwout_two)
 
 
 def body(
@@ -526,13 +560,13 @@
         axis=1,
     ).astype(F32)
 
-    def holders(weight):
-        mine = weight[0]
-        far = over(mine)
+    def holders(mine, far):
         return [mine, beside(mine), far, beside(far)]
 
-    one = (holders(w_in1), holders(w_out1))
-    two = (holders(w_in2), holders(w_out2))
+    far_in = over(after(w_in1[0], other_rows))
+    far_out = over(after(w_out1[0], far_in))
+    one = (holders(w_in1[0], far_in), holders(w_out1[0], far_out))
+    two = ([w_in2[0], beside(w_in2[0])], [w_out2[0], beside(w_out2[0])])
     cot = cotangent[0]
     exchange = lambda value: lax.all_to_all(
         value.reshape(peers, tokens // peers, features),
@@ -543,40 +577,46 @@
     ).reshape(tokens, features)
     cot_slots = exchange(jnp.take(cot, order[0], axis=0))
 
+    gathered = after(gathered, cot_slots)
+
     sequence = ordered(left, rows, other_rows, 0).astype(F32)
     gain, shift = gathered[:, 3 * half].astype(F32), gathered[:, 3 * half + 1].astype(F32)
     xhat, rate = normalised(sequence)
     normed = (xhat * gain + shift).astype(BF16)
     qkv_weight = gathered[:, : 3 * half]
     qkv = dot(normed, qkv_weight).astype(BF16)
+    qkv = after(qkv, far_in)
     mixed_heads, logs = attention_forward(qkv, size)
     block_of = lambda value, which: lax.dynamic_slice_in_dim(value, which * tokens, tokens, 0)
-    mixed = ordered(
-        left, block_of(mixed_heads, seq), over(block_of(mixed_heads, 1 - seq)), 1
-    )
+    other_mixed = over(block_of(mixed_heads, 1 - seq))
+    mixed = ordered(left, block_of(mixed_heads, seq), other_mixed, 1)
     middle = rows.astype(F32) + dot(mixed, output_full)
 
-    z = exchange(jnp.take(middle.astype(BF16), order[0], axis=0))
-    gated, grad_sent, vector_grads, bias_grads, grads_one, grads_two = expert(
-        z, cot_slots, vectors, biases, one, two
+    z = exchange(after(jnp.take(middle.astype(BF16), order[0], axis=0), far_out))
+    gated, grad_sent, vector_grads, bias_one, bias_two, grads_one, grads_two = expert(
+        z, cot_slots, vectors, biases, one, two, over
     )
     home = jnp.take(exchange(gated), inverse[0], axis=0)
     layer_out = (middle + home.astype(F32)).astype(BF16)
-    coming = jnp.take(exchange(grad_sent), inverse[0], axis=0)
+    add = lambda *values: sum(value.astype(F32) for value in values)
+    cut = quarter // 2
+    far_sums = []
+    for _, _, far, cross in grads_one:
+        near = beside(cross)
+        far_sums += [add(far[at : at + cut], near[at : at + cut]).astype(BF16) for at in (0, cut)]
+    coming = jnp.take(after(exchange(grad_sent), *far_sums), inverse[0], axis=0)
+    grads_far = [over(far_sums[0])]
     grad_middle = cot.astype(F32) + coming.astype(F32)
 
-    def holders_sum(quarters):
-        mine, near, far, cross = quarters
-        mine = mine.astype(F32) + beside(near).astype(F32)
-        far = (far.astype(F32) + beside(cross).astype(F32)).astype(BF16)
-        return mine + over(far).astype(F32)
-
-    grad_win_two, grad_wout_two = [holders_sum(g) for g in grads_two]
-    grad_win_one, grad_wout_one = [holders_sum(g) for g in grads_one]
+    grad_win_two, grad_wout_two = [
+        mine.astype(F32) + beside(near).astype(F32) for mine, near in grads_two
+    ]
 
     own_half = lambda table, which: lax.dynamic_slice_in_dim(table, which * half, half, 1)
     core = lax.rem(peer, 2)
-    bias_quarters = bias_grads.reshape(2, 4, quarter)
+    bias_quarters = jnp.stack(
+        [bias_one, jnp.concatenate([bias_two, jnp.zeros_like(bias_two)])]
+    ).reshape(2, 4, quarter)
     bias_rows = lambda first: ordered(left, bias_quarters[:, first], bias_quarters[:, first + 2], 1)
     flat = lambda table, bias: jnp.concatenate([table.reshape(-1), bias.reshape(-1)])
     small = flat(own_half(vector_grads, core), bias_rows(0)) + beside(
@@ -594,8 +634,15 @@
     grad_wo = grad_wo + over(grad_wo)
     grad_mixed = dot_last(grad_attn, output_full).astype(BF16)
     part_of = lambda value, which: lax.dynamic_slice_in_dim(value, which * half, half, 1)
-    grad_heads = ordered(left, part_of(grad_mixed, seq), over(part_of(grad_mixed, 1 - seq)), 0)
-    parts = attention_backward(qkv, grad_heads, logs, size)
+    other_grad = over(after(part_of(grad_mixed, 1 - seq), grads_far[0]))
+    grad_heads = ordered(left, part_of(grad_mixed, seq), other_grad, 0)
+    for value in far_sums[1:]:
+        grads_far.append(over(after(value, other_grad, grads_far[-1])))
+    grad_win_one, grad_wout_one = [
+        add(g[0], beside(g[1]), jnp.concatenate(grads_far[i : i + 2], axis=0))
+        for g, i in zip(grads_one, (0, 2))
+    ]
+    parts = after(attention_backward(qkv, grad_heads, logs, size), grads_far[1])
     grad_normed = dot_last(parts[0], qkv_weight[:, :half])
     grad_normed = grad_normed + dot_last(parts[1], qkv_weight[:, half : 2 * half])
     grad_normed = grad_normed + dot_last(parts[2], qkv_weight[:, 2 * half :])
@@ -605,6 +652,7 @@
         + [jnp.pad(norm_sums, ((0, 0), (0, 126))).astype(BF16)],
         axis=1,
     )
+    packed = after(packed, grads_far[2])
     shard = lax.psum_scatter(packed, "fsdp", scatter_dimension=0, tiled=True)
     other_shard = over(shard)
     join = lambda which: ordered(
@@ -616,6 +664,7 @@
     norm_grads = shard[:, 3 * half : 3 * half + 2].astype(F32)
     norm_grads = norm_grads + other_shard[:, 3 * half : 3 * half + 2].astype(F32)
     arrived = over(block_of(grad_normed, 1 - seq).astype(BF16)).astype(F32)
+    arrived = after(arrived, grads_far[3])
     grad_own = block_of(grad_normed, seq) + arrived
     own_xhat, own_rate = normalised(rows.astype(F32))
     grad_inputs = grad_middle + norm_back(grad_own, own_xhat, own_rate, gain)

time: 696 us -> 553 us (0.79)
  waiting for transfers between devices: 353 us -> 195 us
  Pallas kernels: 144 us -> 154 us
    ppermute x33 -> x31, waiting for transfers between devices: 316 us -> 164 us  [swapped(): return lax.ppermute(value, axis, pairs)]
    all_gather x1, waiting for transfers between devices: 18 us -> 0.01 us  [body(): lax.all_gather(jnp.concatenate([columns(w_query), columns(w_key), columns...]
    all_to_all x4, waiting for transfers between devices: 18.6 us -> 29.7 us  [body(): lax.all_to_all(value.reshape(peers, tokens // peers, features), 'fsdp', s...]
    pallas_call x4 -> x7, Pallas kernels: 104 us -> 114 us  [expert_call(): pl.pallas_call(kernel, grid=(steps,), out_shape=tuple((s for s, _, _ in o...]
    convert_element_type x5 -> x4, other arithmetic: 14.2 us -> 12 us  [the longest x2 9.03 us: body(): add(far[at:at + cut], near[at:at + cut]).astype(BF16)]
    unnamed x96 -> x116, local copies, waits for them, and re-layouts: 13.2 us -> 14.3 us
    ppermute x33 -> x31, starting transfers between devices: 24.7 us -> 24.8 us  [swapped(): return lax.ppermute(value, axis, pairs)]
  transfers between devices with their start and end apart: 41 -> 39, of which waited for: 16 -> 17; matrix products, arithmetic and copies ran while one was open for 16% -> 21% of each run, Pallas kernels for 8% -> 20%
where the time goes in v2:
time: 553 us; the launch traced here: 543 us
  waiting for transfers between devices  195 us (35%)
  Pallas kernels  154 us (28%)
  other arithmetic  61.9 us (11%)
  starting transfers between devices  52 us (9%)
  local copies, waits for them, and re-layouts  35.8 us (6%)
  matrix products  29.3 us (5%)
  between operations  15.3 us (3%)
    ppermute x31, waiting for transfers between devices, swapped(): return lax.ppermute(value, axis, pairs)  164 us
    pallas_call x7, Pallas kernels, expert_call(): pl.pallas_call(kernel, grid=(steps,), out_shape=tuple((s for s, _, _ in o...  114 us
    all_to_all x4, waiting for transfers between devices, body(): lax.all_to_all(value.reshape(peers, tokens // peers, features), 'fsdp', s...  29.7 us
    all_to_all x4, starting transfers between devices, body(): lax.all_to_all(value.reshape(peers, tokens // peers, features), 'fsdp', s...  26.6 us
    ppermute x31, starting transfers between devices, swapped(): return lax.ppermute(value, axis, pairs)  24.8 us
    pallas_call x1, Pallas kernels, attention_backward(): pl.pallas_call(functools.partial(attention_backward_kernel, size), grid=(...  24 us
    pallas_call x1, Pallas kernels, attention_forward(): pl.pallas_call(functools.partial(attention_forward_kernel, size), grid=(p...  15.9 us
    unnamed x116, local copies, waits for them, and re-layouts  14.3 us
  transfers between devices with their start and end apart: 39, of which 17 were waited for; matrix products, arithmetic and copies ran while one was open for 21% of the time, Pallas kernels for 20%

profile of v2, /device:TPU:0, one launch (start us, length us, event | category | flops | bytes accessed | tf_op | source)
XLA Modules:
  0.0 543.3 jit_solution(1675209966901529617)
XLA Ops:
  9.8 3.0 collective-permute-start
  13.5 2.8 gather_fusion
  16.3 19.9 %collective-permute-done = bf16[512,1024]{1,0:T(8,128)(2,1)S(1)} collective-permute-done((bf16[512,1024]{1,0:T(8,128)(2,1)}, bf16[512,1024]{1,0:T(8,128)(2,1)S(1)}, u32[]{:S(2)}, u32[]{:S(2)}) %collective-permute-start) | collective-permute-done | bytes 1048608 | tf_op jit(solution)/shard_map/ppermute | solution.py:22
  36.2 1.7 collective-permute-start.1
  37.9 2.4 broadcast_select_fusion.2
  40.3 6.0 %all-to-all-start = ((bf16[16,32,1024]{2,1,0:T(8,128)(2,1)}), bf16[16,32,1024]{2,1,0:T(8,128)(2,1)}, u32[]{:S(2)}, u32[]{:S(2)}) async-start(bf16[16,32,1024]{2,1,0:T(8,128)(2,1)} %bitcast.118), calls=%async_computation | async-start | bytes 2097152 | tf_op jit(solution)/shard_map/all_to_all | solution.py:571
  47.7 2.5 fusion.7
  50.2 33.1 %collective-permute-done.1.refs_9_.refs_15_ = bf16[1024,1024]{1,0:T(8,128)(2,1)} collective-permute-done((bf16[1024,1024]{1,0:T(8,128)(2,1)}, bf16[1024,1024]{1,0:T(8,128)(2,1)}, u32[]{:S(2)}, u32[]{:S(2)}) %collective-permute-start.1) | collective-permute-done | bytes 2097184 | tf_op jit(solution)/shard_map/ppermute | solution.py:22
  86.1 2.5 fusion.5
  90.0 4.8 convolution_convert_fusion.q_ref.k_ref.v_ref
  94.8 15.9 %attention_forward.1 = (bf16[1024,512]{1,0:T(8,128)(2,1)}, f32[4,2,1024]{2,1,0:T(2,128)}) custom-call(bf16[1024,1536]{1,0:T(8,128)(2,1)} %convolution_convert_fusion.q_ref.k_ref.v_ref, bf16[1024,1536]{1,0:T(8,128)(2,1)} %convolution_convert_fusion.q_ref.k_ref.v_ref, bf16[1024,1536]{1,0:T(8,128)(2,1)} %convolution_convert_fusion.q_ref.k_ref.v_ref), custom_call_target="tpu_custom_call" | custom-call | flops 4294967296 | bytes 5242880 | tf_op jit(solution)/shard_map/attention_forward/pallas_call | solution.py:127
  110.7 2.1 constant_dynamic-slice_fusion.11
  114.3 26.3 %collective-permute-done.2 = bf16[512,512]{1,0:T(8,128)(2,1)S(1)} collective-permute-done((bf16[512,512]{1,0:T(8,128)(2,1)S(1)}, bf16[512,512]{1,0:T(8,128)(2,1)S(1)}, u32[]{:S(2)}, u32[]{:S(2)}) %collective-permute-start.2) | collective-permute-done | bytes 524320 | tf_op jit(solution)/shard_map/ppermute | solution.py:22
  141.5 4.8 fusion.66
  146.3 2.8 gather_fusion.1
  149.1 2.4 broadcast_select_fusion.1
  151.6 5.8 %all-to-all-start.1 = ((bf16[16,32,1024]{2,1,0:T(8,128)(2,1)}), bf16[16,32,1024]{2,1,0:T(8,128)(2,1)S(1)}, u32[]{:S(2)}, u32[]{:S(2)}) async-start(bf16[16,32,1024]{2,1,0:T(8,128)(2,1)} %bitcast.10), calls=%async_computation.1 | async-start | bytes 2097152 | tf_op jit(solution)/shard_map/all_to_all | solution.py:571
  159.0 2.6 collective-permute-done.4
  164.0 16.3 %all-to-all-done.1 = bf16[16,32,1024]{2,1,0:T(8,128)(2,1)S(1)} async-done(((bf16[16,32,1024]{2,1,0:T(8,128)(2,1)}), bf16[16,32,1024]{2,1,0:T(8,128)(2,1)S(1)}, u32[]{:S(2)}, u32[]{:S(2)}) %all-to-all-start.1) | async-done | bytes 1048608 | tf_op jit(solution)/shard_map/all_to_all | solution.py:571
  181.3 1.5 fusion.19.grad_ref.refs_6_.refs_2_
  182.8 1.6 collective-permute-start.11
  184.4 20.0 %forward_first.1 = (f32[512,1024]{1,0:T(8,128)}, bf16[512,1024]{1,0:T(8,128)(2,1)}, bf16[512,4096]{1,0:T(8,128)(2,1)}, bf16[512,4096]{1,0:T(8,128)(2,1)}, bf16[512,1024]{1,0:T(8,128)(2,1)}) custom-call(bf16[512,1024]{1,0:T(8,128)(2,1)} %bitcast.119, f32[1,1024]{1,0:T(1,128)} %get-tuple-element.224.refs_1_.refs_10_, f32[1,1024]{1,0:T(1,128)} %get-tuple-element.223.refs_2_, ...), custom_call_target="tpu_custom_call" | custom-call | flops 17179869184 | bytes 30445568 | tf_op jit(solution)/shard_map/forward_first/pallas_call | solution.py:363
  204.4 3.6 collective-permute-done.11.grad_ref.refs_7_
  208.0 1.5 collective-permute-start.12
  209.5 11.5 %forward_second.2 = (f32[512,1024]{1,0:T(8,128)}, bf16[512,2048]{1,0:T(8,128)(2,1)}, bf16[512,2048]{1,0:T(8,128)(2,1)}) custom-call(bf16[512,1024]{1,0:T(8,128)(2,1)} %get-tuple-element.79.normed_ref.refs_4_, f32[4,1,512]{2,1,0:T(1,128)} %fusion.52.bias_ref, bf16[1024,1024]{1,0:T(8,128)(2,1)} %bitcast.149, ...), custom_call_target="tpu_custom_call" | custom-call | flops 8589934592 | bytes 15736832 | tf_op jit(solution)/shard_map/forward_second/pallas_call | solution.py:363
  221.0 10.6 %backward_second.2 = (f32[512,1024]{1,0:T(8,128)}, bf16[512,2048]{1,0:T(8,128)(2,1)}) custom-call(bf16[512,1024]{1,0:T(8,128)(2,1)} %copy-done.19, bf16[512,2048]{1,0:T(8,128)(2,1)} %get-tuple-element.81.slope_ref, bf16[1024,1024]{1,0:T(8,128)(2,1)} %bitcast.150, bf16[1024,1024]{1,0:T(8,128)(2,1)} %collective-permute-done.9.refs_1_, ...), custom_call_target="tpu_custom_call" | custom-call | flops 8589934592 | bytes 15728640 | tf_op jit(solution)/shard_map/backward_second/pallas_call | solution.py:363
  233.4 11.1 %forward_second.3 = (bf16[512,1024]{1,0:T(8,128)(2,1)}, bf16[512,2048]{1,0:T(8,128)(2,1)}, bf16[512,2048]{1,0:T(8,128)(2,1)}) custom-call(bf16[512,1024]{1,0:T(8,128)(2,1)} %copy-done.47, f32[4,1,512]{2,1,0:T(1,128)} %fusion.52.bias_ref, bf16[1024,1024]{1,0:T(8,128)(2,1)} %bitcast.151, bf16[1024,1024]{1,0:T(8,128)(2,1)} %collective-permute-done.9.refs_1_, ...), custom_call_target="tpu_custom_call" | custom-call | flops 8589934592 | bytes 14688256 | tf_op jit(solution)/shard_map/forward_second/pallas_call | solution.py:363
  244.5 1.6 collective-permute-start.13
  246.1 10.3 %backward_second.3 = (bf16[512,1024]{1,0:T(8,128)(2,1)}, bf16[512,2048]{1,0:T(8,128)(2,1)}) custom-call(bf16[512,1024]{1,0:T(8,128)(2,1)} %copy-done.46, bf16[512,2048]{1,0:T(8,128)(2,1)} %get-tuple-element.83.slope_ref, bf16[1024,1024]{1,0:T(8,128)(2,1)} %bitcast.152, bf16[1024,1024]{1,0:T(8,128)(2,1)} %collective-permute-done.9.refs_1_, ...), custom_call_target="tpu_custom_call" | custom-call | flops 8589934592 | bytes 14680064 | tf_op jit(solution)/shard_map/backward_second/pallas_call | solution.py:363
  257.0 16.1 %weights_second.1 = (f32[4,1,512]{2,1,0:T(1,128)}, bf16[1024,1024]{1,0:T(8,128)(2,1)}, bf16[1024,1024]{1,0:T(8,128)(2,1)}, bf16[1024,1024]{1,0:T(8,128)(2,1)}, bf16[1024,1024]{1,0:T(8,128)(2,1)}) custom-call(bf16[512,2048]{1,0:T(8,128)(2,1)} %get-tuple-element.85.refs_0_, bf16[512,2048]{1,0:T(8,128)(2,1)} %get-tuple-element.86.refs_1_, ...), custom_call_target="tpu_custom_call" | custom-call | flops 17179869184 | bytes 20979712 | tf_op jit(solution)/shard_map/weights_second/pallas_call | solution.py:363
  273.2 2.8 fusion.20
  276.0 14.7 %collective-permute-done.14.refs_1_ = bf16[512,1024]{1,0:T(8,128)(2,1)} collective-permute-done((bf16[512,1024]{1,0:T(8,128)(2,1)}, bf16[512,1024]{1,0:T(8,128)(2,1)}, u32[]{:S(2)}, u32[]{:S(2)}) %collective-permute-start.14) | collective-permute-done | bytes 1048608 | tf_op jit(solution)/shard_map/ppermute | solution.py:22
  291.5 34.6 %backward_first.1 = (bf16[512,1024]{1,0:T(8,128)(2,1)}, f32[8,1024]{1,0:T(8,128)}, f32[8,1,512]{2,1,0:T(1,128)}, bf16[1024,1024]{1,0:T(8,128)(2,1)}, bf16[1024,1...) custom-call(f32[512,1024]{1,0:T(8,128)} %get-tuple-element.82.refs_0, ...), custom_call_target="tpu_custom_call" | custom-call | flops 34359738368 | bytes 52752384 | tf_op jit(solution)/shard_map/backward_first/pallas_call | solution.py:363
  326.7 7.4 %all-to-all-start.3 = ((bf16[16,32,1024]{2,1,0:T(8,128)(2,1)}), bf16[16,32,1024]{2,1,0:T(8,128)(2,1)S(1)}, u32[]{:S(2)}, u32[]{:S(2)}) async-start(bf16[16,32,1024]{2,1,0:T(8,128)(2,1)} %bitcast.122), calls=%async_computation.3 | async-start | bytes 2097152 | tf_op jit(solution)/shard_map/all_to_all | solution.py:571
  334.7 4.5 add_convert_fusion.2
  339.2 1.5 collective-permute-start.17
  341.9 4.5 add_convert_fusion
  346.5 10.6 %all-to-all-done.3 = bf16[16,32,1024]{2,1,0:T(8,128)(2,1)S(1)} async-done(((bf16[16,32,1024]{2,1,0:T(8,128)(2,1)}), bf16[16,32,1024]{2,1,0:T(8,128)(2,1)S(1)}, u32[]{:S(2)}, u32[]{:S(2)}) %all-to-all-start.3) | async-done | bytes 1048608 | tf_op jit(solution)/shard_map/all_to_all | solution.py:571
  357.1 2.8 gather_fusion.3
  359.8 3.2 convolution_convert_fusion.5
  365.0 1.5 collective-permute-start.18
  366.5 2.9 convolution_convert_fusion.1
  369.6 9.0 %collective-permute-done.18 = bf16[512,512]{1,0:T(8,128)(2,1)S(1)} collective-permute-done((bf16[512,512]{1,0:T(8,128)(2,1)}, bf16[512,512]{1,0:T(8,128)(2,1)S(1)}, u32[]{:S(2)}, u32[]{:S(2)}) %collective-permute-start.18) | collective-permute-done | bytes 524320 | tf_op jit(solution)/shard_map/ppermute | solution.py:22
  378.7 1.5 collective-permute-start.19
  381.6 24.0 %attention_backward.1 = bf16[3,1024,512]{2,1,0:T(8,128)(2,1)} custom-call(bf16[1024,1536]{1,0:T(8,128)(2,1)} %convolution_convert_fusion.q_ref.k_ref.v_ref, bf16[1024,1536]{1,0:T(8,128)(2,1)} %convolution_convert_fusion.q_ref.k_ref.v_ref, bf16[1024,1536]{1,0:T(8,128)(2,1)} %convolution_convert_fusion.q_ref.k_ref.v_ref, ...), custom_call_target="tpu_custom_call" | custom-call | flops 10737418240 | bytes 8388608 | tf_op jit(solution)/shard_map/attention_backward/pallas_call | solution.py:148
  406.2 3.2 fusion.26
  410.8 5.2 fusion.6
  420.1 2.0 pad_maximum_fusion
  422.0 7.2 %collective-permute-done.21 = bf16[512,1024]{1,0:T(8,128)(2,1)} collective-permute-done((bf16[512,1024]{1,0:T(8,128)(2,1)S(1)}, bf16[512,1024]{1,0:T(8,128)(2,1)}, u32[]{:S(2)}, u32[]{:S(2)}) %collective-permute-start.21) | collective-permute-done | bytes 1048608 | tf_op jit(solution)/shard_map/ppermute | solution.py:22
  429.3 5.6 %copy.65 = bf16[1024,1664]{1,0:T(8,128)(2,1)} copy(bf16[1024,1664]{0,1:T(8,128)(2,1)} %pad_maximum_fusion) | data formatting | bytes 6815744
  435.7 7.4 %all-to-all-start.2 = ((bf16[16,32,1024]{2,1,0:T(8,128)(2,1)}), bf16[16,32,1024]{2,1,0:T(8,128)(2,1)S(1)}, u32[]{:S(2)}, u32[]{:S(2)}) async-start(bf16[16,32,1024]{2,1,0:T(8,128)(2,1)} %bitcast.121), calls=%async_computation.2 | async-start | bytes 2097152 | tf_op jit(solution)/shard_map/all_to_all | solution.py:571
  444.0 3.2 collective-permute-done.26
  448.4 5.3 add_bitcast_fusion
  453.7 3.0 dynamic-slice_convert_fusion
  457.1 1.6 collective-permute-start.22
  458.7 4.5 add_bitcast_fusion.1
  463.2 2.8 all-to-all-done.2
  466.1 2.7 gather_fusion.2
  470.4 6.4 %add_bitcast_fusion.3 = f32[1,1024,1024]{2,1,0:T(8,128)} fusion(bf16[1024,1024]{1,0:T(8,128)(2,1)} %collective-permute-done.27, bf16[1024,1024]{1,0:T(8,128)(2,1)} %get-tuple-element.110, bf16[512,1024]{1,0:T(8,128)(2,1)} %copy-done.18, bf16[512,1024]{1,0:T(8,128)(2,1)} %collective-permute-done.17), kind=kLoop, calls=%fused_computation.17 | loop fusion | flops 8388608 | bytes 10485760 | tf_op jit(solution)/shard_map/broadcast_in_dim | solution.py:682
  476.8 32.5 %collective-permute-done.24 = f32[64,1024]{1,0:T(8,128)S(1)} collective-permute-done((f32[64,1024]{1,0:T(8,128)S(1)}, f32[64,1024]{1,0:T(8,128)S(1)}, u32[]{:S(2)}, u32[]{:S(2)}) %collective-permute-start.24) | collective-permute-done | bytes 262176 | tf_op jit(solution)/shard_map/ppermute | solution.py:22
  510.0 1.5 convert_element_type.222
  513.1 5.7 %add_bitcast_fusion.2 = f32[1,1024,1024]{2,1,0:T(8,128)} fusion(bf16[1024,1024]{1,0:T(8,128)(2,1)} %collective-permute-done.28, bf16[1024,1024]{1,0:T(8,128)(2,1)S(1)} %copy-done.12, bf16[512,1024]{1,0:T(8,128)(2,1)} %collective-permute-done.22, bf16[512,1024]{1,0:T(8,128)(2,1)} %collective-permute-done.21), kind=kLoop, calls=%fused_computation.16 | loop fusion | flops 8388608 | bytes 10485760 | tf_op jit(solution)/shard_map/broadcast_in_dim | solution.py:684
  518.9 2.7 fusion.17
  523.2 9.6 %collective-permute-done.23 = bf16[64,1664]{0,1:T(8,128)(2,1)S(1)} collective-permute-done((bf16[64,1664]{0,1:T(8,128)(2,1)S(1)}, bf16[64,1664]{0,1:T(8,128)(2,1)S(1)}, u32[]{:S(2)}, u32[]{:S(2)}) %collective-permute-start.23) | collective-permute-done | bytes 213024 | tf_op jit(solution)/shard_map/ppermute | solution.py:22
  (246 shorter events, 43.4 us)
Async XLA Ops:
  7.2 77.5 %all-gather.3.cloned.1.call-start = ((), (), s32[]{:S(2)}) async-start(), calls=%async_computation.6 | async-start | bytes 3620864 | tf_op jit(solution)/shard_map/all_gather | solution.py:535
  9.8 26.4 %collective-permute-start = (bf16[512,1024]{1,0:T(8,128)(2,1)}, bf16[512,1024]{1,0:T(8,128)(2,1)S(1)}, u32[]{:S(2)}, u32[]{:S(2)}) collective-permute-start(bf16[512,1024]{1,0:T(8,128)(2,1)} %bitcast.113), channel_id=1, source_target_pairs={{0,16},{16,0},{1,17},{17,1},{2,18},{18,2},{3,19},{19,3},{4,20},{20... | collective-permute-start | bytes 3145736 | tf_op jit(solution)/shard_map/ppermute | solution.py:22
  36.2 49.9 %copy-start.4 = (bf16[512,1024]{1,0:T(8,128)(2,1)}, bf16[512,1024]{1,0:T(8,128)(2,1)S(1)}, u32[]{:S(2)}) copy-start(bf16[512,1024]{1,0:T(8,128)(2,1)S(1)} %collective-permute-done) | copy-start | bytes 3145732
  36.2 10.9 %copy-start.3 = (bf16[1,512,1024]{2,1,0:T(8,128)(2,1)S(1)}, bf16[1,512,1024]{2,1,0:T(8,128)(2,1)}, u32[]{:S(2)}) copy-start(bf16[1,512,1024]{2,1,0:T(8,128)(2,1)} %param.25) | copy-start | bytes 3145732
  36.2 47.1 %collective-permute-start.1 = (bf16[1024,1024]{1,0:T(8,128)(2,1)}, bf16[1024,1024]{1,0:T(8,128)(2,1)}, u32[]{:S(2)}, u32[]{:S(2)}) collective-permute-start(bf16[1024,1024]{1,0:T(8,128)(2,1)} %bitcast.158), channel_id=1, source_target_pairs={{0,16},{16,0},{1,17},{17,1},{2,18},{18,2},{3,19},{19,3},{4,20},{20... | collective-permute-start | bytes 6291464 | tf_op jit(solution)/shard_map/ppermute | solution.py:22
  40.3 44.5 %all-to-all-start = ((bf16[16,32,1024]{2,1,0:T(8,128)(2,1)}), bf16[16,32,1024]{2,1,0:T(8,128)(2,1)}, u32[]{:S(2)}, u32[]{:S(2)}) async-start(bf16[16,32,1024]{2,1,0:T(8,128)(2,1)} %bitcast.118), calls=%async_computation | async-start | bytes 2097152 | tf_op jit(solution)/shard_map/all_to_all | solution.py:571
  46.3 68.1 %all-gather.5.cloned.1.call-start = ((), (), s32[]{:S(2)}) async-start(), calls=%async_computation.7 | async-start | bytes 2228224 | tf_op jit(solution)/shard_map/all_gather | solution.py:541
  47.7 41.0 %copy-start.27 = (f32[1024]{0:T(1024)}, f32[1024]{0:T(1024)S(1)}, u32[]{:S(2)}) copy-start(f32[1024]{0:T(1024)S(1)} %broadcast_multiply_fusion) | copy-start | bytes 12292
  50.2 38.4 %copy-start.34 = (f32[1024]{0:T(1024)}, f32[1024]{0:T(1024)S(1)}, u32[]{:S(2)}) copy-start(f32[1024]{0:T(1024)S(1)} %add_rsqrt_fusion) | copy-start | bytes 12292
  83.3 68.3 %collective-permute-start.3 = (bf16[1024,1024]{1,0:T(8,128)(2,1)}, bf16[1024,1024]{1,0:T(8,128)(2,1)}, u32[]{:S(2)}, u32[]{:S(2)}) collective-permute-start(bf16[1024,1024]{1,0:T(8,128)(2,1)} %bitcast.9.refs_11_.refs_17_), channel_id=1, source_target_pairs={{0,16},{16,0},{1,17},{17,1},{2,18},{18,2},{3,19},{19,3},{4,20},{20... | collective-permute-start | bytes 6291464 | tf_op jit(solution)/shard_map/ppermute | solution.py:22
  112.8 27.9 %collective-permute-start.2 = (bf16[512,512]{1,0:T(8,128)(2,1)S(1)}, bf16[512,512]{1,0:T(8,128)(2,1)S(1)}, u32[]{:S(2)}, u32[]{:S(2)}) collective-permute-start(bf16[512,512]{1,0:T(8,128)(2,1)S(1)} %get-tuple-element.197), channel_id=1, source_target_pairs={{0,16},{16,0},{1,17},{17,1},{2,18},{18,2},{3,19},{19,3},{4,20},{20... | collective-permute-start | bytes 1572872 | tf_op jit(solution)/shard_map/ppermute | solution.py:22
  149.1 9.4 %copy-start.39 = (bf16[1,512]{1,0:T(2,128)(2,1)S(1)}, bf16[1,512]{1,0:T(2,128)(2,1)}, u32[]{:S(2)}) copy-start(bf16[1,512]{1,0:T(2,128)(2,1)} %param.32) | copy-start | bytes 3076
  149.1 9.4 %copy-start.40 = (bf16[1,512]{1,0:T(2,128)(2,1)S(1)}, bf16[1,512]{1,0:T(2,128)(2,1)}, u32[]{:S(2)}) copy-start(bf16[1,512]{1,0:T(2,128)(2,1)} %param.33) | copy-start | bytes 3076
  149.1 9.4 %copy-start.41 = (bf16[1,512]{1,0:T(2,128)(2,1)S(1)}, bf16[1,512]{1,0:T(2,128)(2,1)}, u32[]{:S(2)}) copy-start(bf16[1,512]{1,0:T(2,128)(2,1)} %param.37) | copy-start | bytes 3076
  149.1 9.4 %copy-start.42 = (bf16[1,512]{1,0:T(2,128)(2,1)S(1)}, bf16[1,512]{1,0:T(2,128)(2,1)}, u32[]{:S(2)}) copy-start(bf16[1,512]{1,0:T(2,128)(2,1)} %param.38) | copy-start | bytes 3076
  149.1 9.4 %copy-start.43 = (bf16[1,512]{1,0:T(2,128)(2,1)S(1)}, bf16[1,512]{1,0:T(2,128)(2,1)}, u32[]{:S(2)}) copy-start(bf16[1,512]{1,0:T(2,128)(2,1)} %param.39) | copy-start | bytes 3076
  149.1 9.4 %copy-start.44 = (bf16[1,512]{1,0:T(2,128)(2,1)S(1)}, bf16[1,512]{1,0:T(2,128)(2,1)}, u32[]{:S(2)}) copy-start(bf16[1,512]{1,0:T(2,128)(2,1)} %param.43) | copy-start | bytes 3076
  149.1 9.4 %copy-start.45 = (bf16[1,512]{1,0:T(2,128)(2,1)S(1)}, bf16[1,512]{1,0:T(2,128)(2,1)}, u32[]{:S(2)}) copy-start(bf16[1,512]{1,0:T(2,128)(2,1)} %param.44) | copy-start | bytes 3076
  149.1 9.4 %copy-start.30 = (bf16[1,2048]{1,0:T(2,128)(2,1)S(1)}, bf16[1,2048]{1,0:T(2,128)(2,1)}, u32[]{:S(2)}) copy-start(bf16[1,2048]{1,0:T(2,128)(2,1)} %param.41) | copy-start | bytes 12292
  149.1 9.4 %copy-start.31 = (bf16[1,2048]{1,0:T(2,128)(2,1)S(1)}, bf16[1,2048]{1,0:T(2,128)(2,1)}, u32[]{:S(2)}) copy-start(bf16[1,2048]{1,0:T(2,128)(2,1)} %param.35) | copy-start | bytes 12292
  151.6 28.7 %all-to-all-start.1 = ((bf16[16,32,1024]{2,1,0:T(8,128)(2,1)}), bf16[16,32,1024]{2,1,0:T(8,128)(2,1)S(1)}, u32[]{:S(2)}, u32[]{:S(2)}) async-start(bf16[16,32,1024]{2,1,0:T(8,128)(2,1)} %bitcast.10), calls=%async_computation.1 | async-start | bytes 2097152 | tf_op jit(solution)/shard_map/all_to_all | solution.py:571
  157.3 23.2 %collective-permute-start.5 = (bf16[1024,1024]{1,0:T(8,128)(2,1)}, bf16[1024,1024]{1,0:T(8,128)(2,1)}, u32[]{:S(2)}, u32[]{:S(2)}) collective-permute-start(bf16[1024,1024]{1,0:T(8,128)(2,1)} %bitcast.159), channel_id=1, source_target_pairs={{0,1},{1,0},{2,3},{3,2},{4,5},{5,4},{6,7},{7,6},{8,9},{9,8},{10,11... | collective-permute-start | bytes 6291464 | tf_op jit(solution)/shard_map/ppermute | solution.py:22
  157.7 25.1 %collective-permute-start.7 = (bf16[1024,1024]{1,0:T(8,128)(2,1)}, bf16[1024,1024]{1,0:T(8,128)(2,1)}, u32[]{:S(2)}, u32[]{:S(2)}) collective-permute-start(bf16[1024,1024]{1,0:T(8,128)(2,1)} %bitcast.9.refs_11_.refs_17_), channel_id=1, source_target_pairs={{0,1},{1,0},{2,3},{3,2},{4,5},{5,4},{6,7},{7,6},{8,9},{9,8},{10,11... | collective-permute-start | bytes 6291464 | tf_op jit(solution)/shard_map/ppermute | solution.py:22
  157.9 26.5 %collective-permute-start.6 = (bf16[1024,1024]{1,0:T(8,128)(2,1)}, bf16[1024,1024]{1,0:T(8,128)(2,1)}, u32[]{:S(2)}, u32[]{:S(2)}) collective-permute-start(bf16[1024,1024]{1,0:T(8,128)(2,1)} %collective-permute-done.1.refs_9_.refs_15_), channel_id=1, source_target_pairs={{0,1},{1,0},{2,3},{3,2},{4,5},{5,4},{6,7},{7,6},{8,9},{9,8},{10,11... | collective-permute-start | bytes 6291464 | tf_op jit(solution)/shard_map/ppermute | solution.py:22
  158.3 26.1 %collective-permute-start.8 = (bf16[1024,1024]{1,0:T(8,128)(2,1)}, bf16[1024,1024]{1,0:T(8,128)(2,1)}, u32[]{:S(2)}, u32[]{:S(2)}) collective-permute-start(bf16[1024,1024]{1,0:T(8,128)(2,1)} %collective-permute-done.3.refs_13_.refs_19_), channel_id=1, source_target_pairs={{0,1},{1,0},{2,3},{3,2},{4,5},{5,4},{6,7},{7,6},{8,9},{9,8},{10,11... | collective-permute-start | bytes 6291464 | tf_op jit(solution)/shard_map/ppermute | solution.py:22
  158.6 3.0 collective-permute-start.4
  161.6 47.9 %collective-permute-start.10 = (bf16[1024,1024]{1,0:T(8,128)(2,1)}, bf16[1024,1024]{1,0:T(8,128)(2,1)}, u32[]{:S(2)}, u32[]{:S(2)}) collective-permute-start(bf16[1024,1024]{1,0:T(8,128)(2,1)} %bitcast.153), channel_id=1, source_target_pairs={{0,1},{1,0},{2,3},{3,2},{4,5},{5,4},{6,7},{7,6},{8,9},{9,8},{10,11... | collective-permute-start | bytes 6291464 | tf_op jit(solution)/shard_map/ppermute | solution.py:22
  164.0 40.4 %copy-start.32 = (f32[1,1024]{1,0:T(1,128)}, f32[1,1024]{1,0:T(1,128)S(1)}, u32[]{:S(2)}) copy-start(f32[1,1024]{1,0:T(1,128)S(1)} %get-tuple-element.225.refs_12_) | copy-start | bytes 12292
  180.6 28.9 %collective-permute-start.9 = (bf16[1024,1024]{1,0:T(8,128)(2,1)}, bf16[1024,1024]{1,0:T(8,128)(2,1)}, u32[]{:S(2)}, u32[]{:S(2)}) collective-permute-start(bf16[1024,1024]{1,0:T(8,128)(2,1)} %bitcast.148), channel_id=1, source_target_pairs={{0,1},{1,0},{2,3},{3,2},{4,5},{5,4},{6,7},{7,6},{8,9},{9,8},{10,11... | collective-permute-start | bytes 6291464 | tf_op jit(solution)/shard_map/ppermute | solution.py:22
  182.8 21.6 %copy-start.19 = (bf16[512,1024]{1,0:T(8,128)(2,1)}, bf16[512,1024]{1,0:T(8,128)(2,1)S(1)}, u32[]{:S(2)}) copy-start(bf16[512,1024]{1,0:T(8,128)(2,1)S(1)} %fusion.19.grad_ref.refs_6_.refs_2_) | copy-start | bytes 3145732
  182.8 25.1 %collective-permute-start.11 = (bf16[512,1024]{1,0:T(8,128)(2,1)S(1)}, bf16[512,1024]{1,0:T(8,128)(2,1)S(1)}, u32[]{:S(2)}, u32[]{:S(2)}) collective-permute-start(bf16[512,1024]{1,0:T(8,128)(2,1)S(1)} %fusion.19.grad_ref.refs_6_.refs_2_), channel_id=1, source_target_pairs={{0,16},{16,0},{1,17},{17,1},{2,18},{18,2},{3,19},{19,3},{4,20},{20... | collective-permute-start | bytes 3145736 | tf_op jit(solution)/shard_map/ppermute | solution.py:22
  208.0 13.0 %copy-start.46 = (bf16[512,1024]{1,0:T(8,128)(2,1)}, bf16[512,1024]{1,0:T(8,128)(2,1)S(1)}, u32[]{:S(2)}) copy-start(bf16[512,1024]{1,0:T(8,128)(2,1)S(1)} %collective-permute-done.11.grad_ref.refs_7_) | copy-start | bytes 3145732
  208.0 24.4 %collective-permute-start.12 = (bf16[512,1024]{1,0:T(8,128)(2,1)}, bf16[512,1024]{1,0:T(8,128)(2,1)S(1)}, u32[]{:S(2)}, u32[]{:S(2)}) collective-permute-start(bf16[512,1024]{1,0:T(8,128)(2,1)} %get-tuple-element.79.normed_ref.refs_4_), channel_id=1, source_target_pairs={{0,16},{16,0},{1,17},{17,1},{2,18},{18,2},{3,19},{19,3},{4,20},{20... | collective-permute-start | bytes 3145736 | tf_op jit(solution)/shard_map/ppermute | solution.py:22
  244.5 28.6 %collective-permute-start.13 = (bf16[512,1024]{1,0:T(8,128)(2,1)}, bf16[512,1024]{1,0:T(8,128)(2,1)S(1)}, u32[]{:S(2)}, u32[]{:S(2)}) collective-permute-start(bf16[512,1024]{1,0:T(8,128)(2,1)} %get-tuple-element.80), channel_id=1, source_target_pairs={{0,16},{16,0},{1,17},{17,1},{2,18},{18,2},{3,19},{19,3},{4,20},{20... | collective-permute-start | bytes 3145736 | tf_op jit(solution)/shard_map/ppermute | solution.py:22
  256.4 34.3 %collective-permute-start.14 = (bf16[512,1024]{1,0:T(8,128)(2,1)}, bf16[512,1024]{1,0:T(8,128)(2,1)}, u32[]{:S(2)}, u32[]{:S(2)}) collective-permute-start(bf16[512,1024]{1,0:T(8,128)(2,1)} %get-tuple-element.84), channel_id=1, source_target_pairs={{0,16},{16,0},{1,17},{17,1},{2,18},{18,2},{3,19},{19,3},{4,20},{20... | collective-permute-start | bytes 3145736 | tf_op jit(solution)/shard_map/ppermute | solution.py:22
  257.0 16.1 %copy-start.16 = (f32[512,1024]{1,0:T(8,128)S(1)}, f32[512,1024]{1,0:T(8,128)}, u32[]{:S(2)}) copy-start(f32[512,1024]{1,0:T(8,128)} %get-tuple-element.76.refs_4_) | copy-start | bytes 6291460
  257.0 16.2 %copy-start.17 = (f32[512,1024]{1,0:T(8,128)S(1)}, f32[512,1024]{1,0:T(8,128)}, u32[]{:S(2)}) copy-start(f32[512,1024]{1,0:T(8,128)} %get-tuple-element.78) | copy-start | bytes 6291460
  326.1 8.3 %copy-start.38 = (s32[1,512]{1,0:T(1,128)S(1)}, s32[1,512]{1,0:T(1,128)}, u32[]{:S(2)}) copy-start(s32[1,512]{1,0:T(1,128)} %param.46) | copy-start | bytes 6148
  326.1 8.5 %collective-permute-start.15 = (bf16[1024,1024]{1,0:T(8,128)(2,1)}, bf16[1024,1024]{1,0:T(8,128)(2,1)}, u32[]{:S(2)}, u32[]{:S(2)}) collective-permute-start(bf16[1024,1024]{1,0:T(8,128)(2,1)} %get-tuple-element.96), channel_id=1, source_target_pairs={{0,1},{1,0},{2,3},{3,2},{4,5},{5,4},{6,7},{7,6},{8,9},{9,8},{10,11... | collective-permute-start | bytes 6291464 | tf_op jit(solution)/shard_map/ppermute | solution.py:22
  326.2 15.7 %collective-permute-start.16 = (bf16[1024,1024]{1,0:T(8,128)(2,1)}, bf16[1024,1024]{1,0:T(8,128)(2,1)}, u32[]{:S(2)}, u32[]{:S(2)}) collective-permute-start(bf16[1024,1024]{1,0:T(8,128)(2,1)} %get-tuple-element.98), channel_id=1, source_target_pairs={{0,1},{1,0},{2,3},{3,2},{4,5},{5,4},{6,7},{7,6},{8,9},{9,8},{10,11... | collective-permute-start | bytes 6291464 | tf_op jit(solution)/shard_map/ppermute | solution.py:22
  326.7 30.4 %all-to-all-start.3 = ((bf16[16,32,1024]{2,1,0:T(8,128)(2,1)}), bf16[16,32,1024]{2,1,0:T(8,128)(2,1)S(1)}, u32[]{:S(2)}, u32[]{:S(2)}) async-start(bf16[16,32,1024]{2,1,0:T(8,128)(2,1)} %bitcast.122), calls=%async_computation.3 | async-start | bytes 2097152 | tf_op jit(solution)/shard_map/all_to_all | solution.py:571
  334.1 134.7 %reduce-scatter.5.cloned.1.call-start = ((), (), s32[]{:S(2)}) async-start(), calls=%async_computation.8 | async-start | bytes 2228224 | tf_op jit(solution)/shard_map/reduce_scatter | solution.py:631
  334.7 7.2 %copy-start.33 = (f32[8,1,512]{2,1,0:T(1,128)S(1)}, f32[8,1,512]{2,1,0:T(1,128)}, u32[]{:S(2)}) copy-start(f32[8,1,512]{2,1,0:T(1,128)} %get-tuple-element.109) | copy-start | bytes 49156
  339.2 25.8 %collective-permute-start.17 = (bf16[512,1024]{1,0:T(8,128)(2,1)}, bf16[512,1024]{1,0:T(8,128)(2,1)}, u32[]{:S(2)}, u32[]{:S(2)}) collective-permute-start(bf16[512,1024]{1,0:T(8,128)(2,1)} %get-tuple-element.193), channel_id=1, source_target_pairs={{0,16},{16,0},{1,17},{17,1},{2,18},{18,2},{3,19},{19,3},{4,20},{20... | collective-permute-start | bytes 3145736 | tf_op jit(solution)/shard_map/ppermute | solution.py:22
  341.1 107.3 %collective-permute-start.30 = (bf16[1024,1024]{1,0:T(8,128)(2,1)}, bf16[1024,1024]{1,0:T(8,128)(2,1)}, u32[]{:S(2)}, u32[]{:S(2)}) collective-permute-start(bf16[1024,1024]{1,0:T(8,128)(2,1)} %get-tuple-element.117), channel_id=1, source_target_pairs={{0,1},{1,0},{2,3},{3,2},{4,5},{5,4},{6,7},{7,6},{8,9},{9,8},{10,11... | collective-permute-start | bytes 6291464 | tf_op jit(solution)/shard_map/ppermute | solution.py:22
  341.3 117.4 %collective-permute-start.29 = (bf16[1024,1024]{1,0:T(8,128)(2,1)}, bf16[1024,1024]{1,0:T(8,128)(2,1)}, u32[]{:S(2)}, u32[]{:S(2)}) collective-permute-start(bf16[1024,1024]{1,0:T(8,128)(2,1)} %get-tuple-element.115), channel_id=1, source_target_pairs={{0,1},{1,0},{2,3},{3,2},{4,5},{5,4},{6,7},{7,6},{8,9},{9,8},{10,11... | collective-permute-start | bytes 6291464 | tf_op jit(solution)/shard_map/ppermute | solution.py:22
  341.7 128.7 %collective-permute-start.27 = (bf16[1024,1024]{1,0:T(8,128)(2,1)}, bf16[1024,1024]{1,0:T(8,128)(2,1)}, u32[]{:S(2)}, u32[]{:S(2)}) collective-permute-start(bf16[1024,1024]{1,0:T(8,128)(2,1)} %get-tuple-element.111), channel_id=1, source_target_pairs={{0,1},{1,0},{2,3},{3,2},{4,5},{5,4},{6,7},{7,6},{8,9},{9,8},{10,11... | collective-permute-start | bytes 6291464 | tf_op jit(solution)/shard_map/ppermute | solution.py:22
  365.0 13.7 %collective-permute-start.18 = (bf16[512,512]{1,0:T(8,128)(2,1)}, bf16[512,512]{1,0:T(8,128)(2,1)S(1)}, u32[]{:S(2)}, u32[]{:S(2)}) collective-permute-start(bf16[512,512]{1,0:T(8,128)(2,1)} %get-tuple-element.100), channel_id=1, source_target_pairs={{0,16},{16,0},{1,17},{17,1},{2,18},{18,2},{3,19},{19,3},{4,20},{20... | collective-permute-start | bytes 1572872 | tf_op jit(solution)/shard_map/ppermute | solution.py:22
  369.4 152.2 %reduce-scatter.7.cloned.1.call-start = ((), (), s32[]{:S(2)}) async-start(), calls=%async_computation.9 | async-start | bytes 3620864
  378.7 26.9 %collective-permute-start.19 = (bf16[512,1024]{1,0:T(8,128)(2,1)}, bf16[512,1024]{1,0:T(8,128)(2,1)S(1)}, u32[]{:S(2)}, u32[]{:S(2)}) collective-permute-start(bf16[512,1024]{1,0:T(8,128)(2,1)} %get-tuple-element.102), channel_id=1, source_target_pairs={{0,16},{16,0},{1,17},{17,1},{2,18},{18,2},{3,19},{19,3},{4,20},{20... | collective-permute-start | bytes 3145736 | tf_op jit(solution)/shard_map/ppermute | solution.py:22
  381.6 24.0 %copy-start.20 = (bf16[512,1024]{1,0:T(8,128)(2,1)S(1)}, bf16[512,1024]{1,0:T(8,128)(2,1)}, u32[]{:S(2)}) copy-start(bf16[512,1024]{1,0:T(8,128)(2,1)} %get-tuple-element.104) | copy-start | bytes 3145732
  381.6 24.6 %copy-start.24 = (bf16[1024,1664]{1,0:T(8,128)(2,1)S(1)}, bf16[1024,1664]{1,0:T(8,128)(2,1)}, u32[]{:S(2)}) copy-start(bf16[1024,1664]{1,0:T(8,128)(2,1)} %all-gather.3.cloned.1.call-done) | copy-start | bytes 10223620
  405.6 23.7 %collective-permute-start.21 = (bf16[512,1024]{1,0:T(8,128)(2,1)S(1)}, bf16[512,1024]{1,0:T(8,128)(2,1)}, u32[]{:S(2)}, u32[]{:S(2)}) collective-permute-start(bf16[512,1024]{1,0:T(8,128)(2,1)S(1)} %copy-done.20), channel_id=1, source_target_pairs={{0,16},{16,0},{1,17},{17,1},{2,18},{18,2},{3,19},{19,3},{4,20},{20... | collective-permute-start | bytes 3145736 | tf_op jit(solution)/shard_map/ppermute | solution.py:22
  435.6 7.5 %collective-permute-start.25 = (f32[7680]{0:T(1024)S(1)}, f32[7680]{0:T(1024)S(1)}, u32[]{:S(2)}, u32[]{:S(2)}) collective-permute-start(f32[7680]{0:T(1024)S(1)} %pad_maximum_fusion.1), channel_id=1, source_target_pairs={{0,1},{1,0},{2,3},{3,2},{4,5},{5,4},{6,7},{7,6},{8,9},{9,8},{10,11... | collective-permute-start | bytes 92168 | tf_op jit(solution)/shard_map/ppermute | solution.py:22
  435.7 30.4 %all-to-all-start.2 = ((bf16[16,32,1024]{2,1,0:T(8,128)(2,1)}), bf16[16,32,1024]{2,1,0:T(8,128)(2,1)S(1)}, u32[]{:S(2)}, u32[]{:S(2)}) async-start(bf16[16,32,1024]{2,1,0:T(8,128)(2,1)} %bitcast.121), calls=%async_computation.2 | async-start | bytes 2097152 | tf_op jit(solution)/shard_map/all_to_all | solution.py:571
  443.2 4.0 collective-permute-start.26
  443.8 68.6 %collective-permute-start.28 = (bf16[1024,1024]{1,0:T(8,128)(2,1)}, bf16[1024,1024]{1,0:T(8,128)(2,1)}, u32[]{:S(2)}, u32[]{:S(2)}) collective-permute-start(bf16[1024,1024]{1,0:T(8,128)(2,1)} %get-tuple-element.113), channel_id=1, source_target_pairs={{0,1},{1,0},{2,3},{3,2},{4,5},{5,4},{6,7},{7,6},{8,9},{9,8},{10,11... | collective-permute-start | bytes 6291464 | tf_op jit(solution)/shard_map/ppermute | solution.py:22
  456.7 53.4 %collective-permute-start.20 = (bf16[512,1024]{1,0:T(8,128)(2,1)}, bf16[512,1024]{1,0:T(8,128)(2,1)}, u32[]{:S(2)}, u32[]{:S(2)}) collective-permute-start(bf16[512,1024]{1,0:T(8,128)(2,1)} %dynamic-slice_convert_fusion), channel_id=1, source_target_pairs={{0,16},{16,0},{1,17},{17,1},{2,18},{18,2},{3,19},{19,3},{4,20},{20... | collective-permute-start | bytes 3145736 | tf_op jit(solution)/shard_map/ppermute | solution.py:22
  457.1 54.4 %collective-permute-start.22 = (bf16[512,1024]{1,0:T(8,128)(2,1)}, bf16[512,1024]{1,0:T(8,128)(2,1)}, u32[]{:S(2)}, u32[]{:S(2)}) collective-permute-start(bf16[512,1024]{1,0:T(8,128)(2,1)} %get-tuple-element.105), channel_id=1, source_target_pairs={{0,16},{16,0},{1,17},{17,1},{2,18},{18,2},{3,19},{19,3},{4,20},{20... | collective-permute-start | bytes 3145736 | tf_op jit(solution)/shard_map/ppermute | solution.py:22
  469.7 39.6 %collective-permute-start.24 = (f32[64,1024]{1,0:T(8,128)S(1)}, f32[64,1024]{1,0:T(8,128)S(1)}, u32[]{:S(2)}, u32[]{:S(2)}) collective-permute-start(f32[64,1024]{1,0:T(8,128)S(1)} %convert_element_type.232), channel_id=1, source_target_pairs={{0,16},{16,0},{1,17},{17,1},{2,18},{18,2},{3,19},{19,3},{4,20},{20... | collective-permute-start | bytes 786440 | tf_op jit(solution)/shard_map/ppermute | solution.py:22
  470.4 38.9 %copy-start.21 = (bf16[64,1024]{1,0:T(8,128)(2,1)S(1)}, bf16[64,1024]{1,0:T(8,128)(2,1)}, u32[]{:S(2)}) copy-start(bf16[64,1024]{1,0:T(8,128)(2,1)} %reduce-scatter.5.cloned.1.call-done) | copy-start | bytes 393220
  470.4 41.2 %copy-start.10 = (f32[1024,1024]{1,0:T(8,128)S(1)}, f32[1024,1024]{1,0:T(8,128)}, u32[]{:S(2)}) copy-start(f32[1024,1024]{1,0:T(8,128)} %get-tuple-element.236) | copy-start | bytes 12582916
  476.8 34.8 %copy-start.26 = (f32[1024]{0:T(1024)S(1)}, f32[1024]{0:T(1024)}, u32[]{:S(2)}) copy-start(f32[1024]{0:T(1024)} %copy-done.25) | copy-start | bytes 12292
  522.7 10.1 %collective-permute-start.23 = (bf16[64,1664]{0,1:T(8,128)(2,1)S(1)}, bf16[64,1664]{0,1:T(8,128)(2,1)S(1)}, u32[]{:S(2)}, u32[]{:S(2)}) collective-permute-start(bf16[64,1664]{0,1:T(8,128)(2,1)S(1)} %copy.66), channel_id=1, source_target_pairs={{0,16},{16,0},{1,17},{17,1},{2,18},{18,2},{3,19},{19,3},{4,20},{20... | collective-permute-start | bytes 638984 | tf_op jit(solution)/shard_map/ppermute | solution.py:22
  (26 other events, 86.1 us)
Sparse Core Ops, SparseCore 0:
  10.9 63.0 all-gather.2
  76.1 38.1 all-gather.4
  369.5 62.0 reduce-scatter.4
  435.7 70.6 reduce-scatter.6

commit v3 on v2

--- a/solution.py
+++ b/solution.py
@@ -15,6 +15,7 @@
 BF16 = jnp.bfloat16
 F32 = jnp.float32
 VMEM_LIMIT = 56 * 1024 * 1024
+MESH = pl.DeviceIdType.MESH
 
 
 def swapped(value, axis):
@@ -49,6 +50,81 @@
     scaled = grad * gain
     inner = jnp.mean(scaled * xhat, axis=-1, keepdims=True)
     return rate * (scaled - jnp.mean(scaled, axis=-1, keepdims=True) - xhat * inner)
+
+
+def bits_of(peers):
+    return peers.bit_length() - 1
+
+
+def greet(partners):
+    barrier = pltpu.get_barrier_semaphore()
+    for device in partners:
+        pl.semaphore_signal(barrier, inc=1, device_id=device, device_id_type=MESH)
+    pl.semaphore_wait(barrier, len(partners))
+
+
+def remote(source, target, sends, recvs, device):
+    return pltpu.make_async_remote_copy(
+        src_ref=source,
+        dst_ref=target,
+        send_sem=sends,
+        recv_sem=recvs,
+        device_id=device,
+        device_id_type=MESH,
+    )
+
+
+class Halving:
+    def __init__(self, peers, held, landed, sends, recvs):
+        peer = lax.axis_index("fsdp")
+        self.stages = bits_of(peers)
+        self.bit = [lax.rem(peer // (1 << s), 2) for s in range(self.stages)]
+        self.partner = [
+            {"fsdp": peer + (1 - 2 * self.bit[s]) * (1 << s)} for s in range(self.stages)
+        ]
+        self.held, self.landed, self.sends, self.recvs = held, landed, sends, recvs
+
+    def copy(self, chunk, s):
+        return remote(
+            self.held[chunk][s].at[:, 1 - self.bit[s]],
+            self.landed[chunk][s],
+            self.sends.at[chunk, s],
+            self.recvs.at[chunk, s],
+            self.partner[s],
+        )
+
+    def start(self, chunk):
+        self.copy(chunk, 0).start()
+
+    def put(self, chunk, value):
+        self.held[chunk][0][...] = value.astype(BF16).reshape(self.held[chunk][0].shape)
+        self.start(chunk)
+
+    def finish(self, chunk, s):
+        self.copy(chunk, s).wait_recv()
+        total = self.held[chunk][s][:, self.bit[s]].astype(F32)
+        total = total + self.landed[chunk][s][...].astype(F32)
+        if s + 1 < self.stages:
+            held = self.held[chunk][s + 1]
+            held[...] = total.astype(BF16).reshape(held.shape)
+            self.copy(chunk, s + 1).start()
+        return total[0]
+
+    def drain(self, chunks):
+        for chunk in range(chunks):
+            for s in range(self.stages):
+                self.copy(chunk, s).wait_send()
+
+
+def halving_buffers(peers, rows, widths, first=True):
+    stages = bits_of(peers)
+    held = [
+        pltpu.VMEM((peers >> (s + 1), 2, rows, w), BF16)
+        for w in widths
+        for s in range(0 if first else 1, stages)
+    ]
+    landed = [pltpu.VMEM((peers >> (s + 1), rows, w), BF16) for w in widths for s in range(stages)]
+    return held + landed + [pltpu.SemaphoreType.DMA((len(widths), stages))] * 2
 
 
 def causal_mask(scores):
@@ -79,7 +155,25 @@
             log_ref[0, head : head + 1, start : start + BLOCK] = peak + jnp.log(total)
 
 
-def attention_backward_kernel(size, q_ref, k_ref, v_ref, g_ref, log_ref, d_ref, dk_sum, dv_sum):
+def attention_backward_kernel(peers, size, *refs):
+    q_ref, k_ref, v_ref, g_ref, log_ref, term_ref, d_ref, sum_ref, dk_sum, dv_sum = refs[:10]
+    stages = bits_of(peers)
+    held = [[term_ref, *refs[10 : 9 + stages]]]
+    landed = [refs[9 + stages : 9 + 2 * stages]]
+    reducer = Halving(peers, held, landed, *refs[9 + 2 * stages :])
+    step, steps = pl.program_id(0), 4
+
+    @pl.when(step == 0)
+    def _():
+        greet(reducer.partner)
+        reducer.start(0)
+
+    for s in range(stages - 1):
+
+        @pl.when(step == min(1 + s, steps - 1))
+        def _():
+            reducer.finish(0, s)
+
     length = q_ref.shape[0]
     scale = size**-0.5
     for head in range(q_ref.shape[1] // size):
@@ -114,6 +208,12 @@
         d_ref[2, :, lanes] = dv_sum[...].astype(BF16)
 
 
+    @pl.when(step == steps - 1)
+    def _():
+        sum_ref[...] = reducer.finish(0, stages - 1)
+        reducer.drain(1)
+
+
 def attention_specs(length, half):
     parts = half // 128
     column = lambda which: pl.BlockSpec((length, 128), lambda i: (0, which * parts + i))
@@ -141,29 +241,39 @@
     )(qkv, qkv, qkv)
 
 
-def attention_backward(qkv, grad, logs, size):
+def attention_backward(peers, qkv, grad, logs, terms, size):
     length, half = grad.shape
     parts, column = attention_specs(length, half)
     per = 128 // size
+    rows, width = terms.shape[0] // peers, terms.shape[1]
+    blocks = (peers // 2, 2, rows, width)
+    shape = jax.ShapeDtypeStruct
     return pl.pallas_call(
-        functools.partial(attention_backward_kernel, size),
+        functools.partial(attention_backward_kernel, peers, size),
         grid=(parts,),
-        out_shape=jax.ShapeDtypeStruct((3, length, half), BF16),
+        out_shape=(shape((3, length, half), BF16), shape((rows, width), F32)),
         in_specs=[
             column(0),
             column(1),
             column(2),
             column(0),
             pl.BlockSpec((1, per, length), lambda i: (i, 0, 0)),
+            pl.BlockSpec(blocks, lambda i: (0, 0, 0, 0)),
         ],
-        out_specs=pl.BlockSpec((3, length, 128), lambda i: (0, 0, i)),
-        scratch_shapes=[pltpu.VMEM((length, size), F32), pltpu.VMEM((length, size), F32)],
-        compiler_params=pltpu.CompilerParams(vmem_limit_bytes=VMEM_LIMIT),
+        out_specs=(
+            pl.BlockSpec((3, length, 128), lambda i: (0, 0, i)),
+            pl.BlockSpec((rows, width), lambda i: (0, 0)),
+        ),
+        scratch_shapes=[pltpu.VMEM((length, size), F32), pltpu.VMEM((length, size), F32)]
+        + halving_buffers(peers, rows, [width], first=False),
+        compiler_params=pltpu.CompilerParams(
+            vmem_limit_bytes=VMEM_LIMIT, collective_id=1, has_side_effects=True
+        ),
         cost_estimate=pl.CostEstimate(
             flops=20 * length * length * half, bytes_accessed=16 * length * half, transcendentals=0
         ),
         name="attention_backward",
-    )(qkv, qkv, qkv, grad, logs)
+    )(qkv, qkv, qkv, grad, logs, terms.reshape(blocks))
 
 
 def stream(step, steps, pairs, buffers, sems):
@@ -205,11 +315,11 @@
     return inner * cdf, slope
 
 
-def forward_first_kernel(ins, count, steps, *refs):
+def forward_first_kernel(steps, *refs):
     z_ref, gain_ref, shift_ref, out_bias_ref, gain_two, shift_two, bias_ref = refs[:7]
-    win, wout = refs[7 : 7 + ins], refs[7 + ins : 7 + count]
-    first_ref, normed_ref, active_ref, slope_ref, normed_two = refs[7 + count : 12 + count]
-    in_buf, out_buf, sems = refs[12 + count :]
+    win, wout = refs[7:11], refs[11:15]
+    first_ref, normed_ref, active_ref, slope_ref, normed_two = refs[15:20]
+    in_buf, out_buf, sems = refs[20:]
     step = pl.program_id(0)
 
     @pl.when(step == 0)
@@ -222,9 +332,12 @@
     slot = stream(step, steps, (win, wout), (in_buf, out_buf), sems)
     active, slope = gelu_parts(dot_last(normed_ref[...], in_buf[slot]) + bias_ref[0])
     low = active.astype(BF16)
-    active_ref[...] = low
     slope_ref[...] = slope.astype(BF16)
     first_ref[...] += dot(low, out_buf[slot])
+
+    @pl.when(step < steps // 2)
+    def _():
+        active_ref[...] = low
 
     @pl.when(step == steps - 1)
     def _():
@@ -294,16 +407,13 @@
             gwout[quarter][...] = grad_out
 
 
-def backward_first_kernel(ins, count, parts, steps, *refs):
-    own_ref, arrived_ref, grad_two_ref, z_ref, first_ref, cot_ref, score_ref = refs[:7]
-    normed_ref, active_ref, slope_ref, gain_ref, gain_two, centre_ref = refs[7:13]
-    win, wout = refs[13 : 13 + ins], refs[13 + ins : 13 + count]
-    sent_ref, vector_ref, bias_ref = refs[13 + count : 16 + count]
-    rest = refs[16 + count :]
-    gwin, gwout = rest[:parts], rest[parts : 2 * parts]
-    total, grad_in, grad_low, in_buf, out_buf, sems = rest[2 * parts :]
+def backward_first_kernel(steps, *refs):
+    own_ref, arrived_ref, grad_two_ref, z_ref, first_ref, cot_ref = refs[:6]
+    slope_ref, gain_ref, gain_two, centre_ref = refs[6:10]
+    win, wout = refs[10:14], refs[14:18]
+    back_ref, grad_low, vector_ref, inner_ref = refs[18:22]
+    total, in_buf, out_buf, sems = refs[22:]
     step = pl.program_id(0)
-    per = steps // parts
     down = lambda value: jnp.sum(value, axis=0, keepdims=True)
 
     @pl.when(step == 0)
@@ -313,7 +423,7 @@
         xhat, rate = normalised(z + first_ref[...])
         grad_normed = own_ref[...] + arrived_ref[...].astype(F32)
         grad_rows = norm_back(grad_normed, xhat, rate, gain_two[...])
-        grad_in[...] = grad_rows
+        back_ref[...] = grad_rows
         gate = jax.nn.sigmoid(jnp.sum(z * centre_ref[...], axis=-1, keepdims=True))
         low = (gate * cot_ref[...].astype(F32) + grad_rows).astype(BF16)
         grad_low[...] = low
@@ -321,22 +431,15 @@
         vector_ref[3:4] = down(grad_normed * xhat)
         vector_ref[4:5] = down(grad_normed)
         vector_ref[5:6] = down(grad_two_ref[...].astype(F32))
-        vector_ref[6:7] = down(score_ref[:, 0:1] * z)
-        vector_ref[7:8] = jnp.zeros_like(vector_ref[7:8])
+        vector_ref[6:8] = jnp.zeros_like(vector_ref[6:8])
 
     slot = stream(step, steps, (win, wout), (in_buf, out_buf), sems)
-    grad = grad_low[...]
-    inner = (slope_ref[...].astype(F32) * dot_last(grad, out_buf[slot])).astype(BF16)
-    bias_ref[0] = down(inner.astype(F32))
+    inner = (slope_ref[...].astype(F32) * dot_last(grad_low[...], out_buf[slot])).astype(BF16)
     total[...] += dot(inner, in_buf[slot])
-    low_out = dot_first(active_ref[...], grad).astype(BF16)
-    low_in = dot_first(inner, normed_ref[...]).astype(BF16)
-    for quarter in range(parts):
-
-        @pl.when(step // per == quarter)
-        def _():
-            gwin[quarter][...] = low_in
-            gwout[quarter][...] = low_out
+
+    @pl.when(step < steps // 2)
+    def _():
+        inner_ref[...] = inner
 
     @pl.when(step == steps - 1)
     def _():
@@ -344,9 +447,31 @@
         grad_normed = total[...]
         vector_ref[0:1] = down(grad_normed * xhat)
         vector_ref[1:2] = down(grad_normed)
-        grad_rows = norm_back(grad_normed, xhat, rate, gain_ref[...])
-        score = score_ref[:, 0:1]
-        sent_ref[...] = (grad_in[...] + grad_rows + score * centre_ref[...]).astype(BF16)
+        back_ref[...] += norm_back(grad_normed, xhat, rate, gain_ref[...])
+
+
+def weights_first_kernel(steps, *refs):
+    inner_ref, active_ref, normed_ref, grad_ref, normed_far, grad_far, in_bias = refs[:7]
+    win, wout = refs[7:9], refs[9:11]
+    bias_ref, gwin, gwout, in_buf, out_buf, sems = refs[11], refs[12:14], refs[14:16], *refs[16:]
+    step = pl.program_id(0)
+    slot = stream(step, steps, (win, wout), (in_buf, out_buf), sems)
+    active, slope = gelu_parts(dot_last(normed_far[...], in_buf[slot]) + in_bias[0])
+    inner = (slope * dot_last(grad_far[...], out_buf[slot])).astype(BF16)
+    own = inner_ref[...]
+    bias_ref[0] = jnp.sum(own.astype(F32), axis=0, keepdims=True) + jnp.sum(
+        inner.astype(F32), axis=0, keepdims=True
+    )
+    grad_in = (dot_first(own, normed_ref[...]) + dot_first(inner, normed_far[...])).astype(BF16)
+    grad_out = (
+        dot_first(active_ref[...], grad_ref[...]) + dot_first(active.astype(BF16), grad_far[...])
+    ).astype(BF16)
+    for quarter in range(2):
+
+        @pl.when(step // (steps // 2) == quarter)
+        def _():
+            gwin[quarter][...] = grad_in
+            gwout[quarter][...] = grad_out
 
 
 def expert_call(kernel, name, steps, inputs, weights, outs, scratch, flops):
@@ -404,18 +529,19 @@
         ]
 
     lines = [line(i) for i in range(7)]
-    counts = len(one[0]), len(one[0]) + len(one[1])
+    held = ((rows, CHUNK), lambda c: (0, jnp.minimum(c, near - 1)))
+    half_hidden = shape((rows, hidden // 2), BF16)
     wide_z, wide_cot = z.astype(F32), cot.astype(F32)
     gate = jax.nn.sigmoid(jnp.sum(wide_z * vectors[6], axis=-1, keepdims=True))
     grad_two = (gate * wide_cot).astype(BF16)
     grad_far = over(grad_two)
     first, normed_one, active_one, slope_one, normed_two = expert_call(
-        functools.partial(forward_first_kernel, *counts, steps),
+        functools.partial(forward_first_kernel, steps),
         "forward_first",
         steps,
         [flat(z)] + lines[:5] + [(chunked[0], *thin)],
         one[0] + one[1],
-        [wide_rows, low_rows] + [(shape((rows, hidden), BF16), *wide)] * 2 + [low_rows],
+        [wide_rows, low_rows, (half_hidden, *held), (shape((rows, hidden), BF16), *wide), low_rows],
         [],
         2 * matmul,
     )
@@ -448,7 +574,9 @@
 
     own_part, active_own, slope_own = forward_second(normed_two, F32)
     far_part, active_far, slope_far = forward_second(normed_far, BF16)
+    normed_one_far = over(after(normed_one, normed_far))
     grad_far_part, inner_far = backward_second(grad_far, slope_far, BF16)
+    grad_far_part = after(grad_far_part, normed_one_far)
     grad_own_part, inner_own = backward_second(grad_two, slope_own, F32)
     outs = expert_call(
         functools.partial(weights_second_kernel, 2, near),
@@ -463,32 +591,164 @@
     )
     bias_two, gwin_two, gwout_two = outs[0].reshape(hidden // 2), outs[1:3], outs[3:5]
 
-    branch = first + (own_part + over(far_part).astype(F32) + vectors[5])
+    grad_arrived = over(grad_far_part)
+    far_arrived = over(after(far_part, grad_arrived))
+    back, grad_one, sums, inner_one = expert_call(
+        functools.partial(backward_first_kernel, steps),
+        "backward_first",
+        steps,
+        [
+            flat(a)
+            for a in (grad_own_part, after(grad_arrived, bias_two), grad_two, z, first, cot)
+        ]
+        + [(slope_one, *wide), line(0), line(3), line(6)],
+        one[0] + one[1],
+        [wide_rows, low_rows, flat(shape((8, features), F32)), (half_hidden, *held)],
+        [pltpu.VMEM((rows, features), F32)],
+        2 * matmul,
+    )
+    grad_one_far = over(grad_one)
+    branch = first + (own_part + far_arrived.astype(F32) + vectors[5])
     gated = (gate * branch).astype(BF16)
     grad_gate = jnp.sum(wide_cot * branch, axis=-1, keepdims=True)
-    score = jnp.broadcast_to(grad_gate * gate * (1.0 - gate), (rows, 128))
-
-    grad_arrived = after(over(grad_far_part), outs[0])
+    score = grad_gate * gate * (1.0 - gate)
+    grad_sent = (back + score * vectors[6]).astype(BF16)
+    grad_centre = jnp.sum(score * wide_z, axis=0, keepdims=True)
     outs = expert_call(
-        functools.partial(backward_first_kernel, *counts, 4, steps),
-        "backward_first",
-        steps,
-        [flat(a) for a in (grad_own_part, grad_arrived, grad_two, z, first, cot, score)]
-        + [flat(normed_one), (active_one, *wide), (slope_one, *wide)]
-        + [line(0), line(3), line(6)],
-        one[0] + one[1],
-        [low_rows, flat(shape((8, features), F32)), (shape((steps, 1, CHUNK), F32), *thin)]
-        + quarter_outs(4, steps)
-        + quarter_outs(4, steps),
-        [
-            pltpu.VMEM((rows, features), F32),
-            pltpu.VMEM((rows, features), F32),
-            pltpu.VMEM((rows, features), BF16),
+        functools.partial(weights_first_kernel, near),
+        "weights_first",
+        near,
+        [(inner_one, *wide), (active_one, *wide)]
+        + [flat(a) for a in (normed_one, grad_one, normed_one_far, grad_one_far)]
+        + [(chunked[0, :near], *thin)],
+        one[0][:2] + one[1][:2],
+        [(shape((near, 1, CHUNK), F32), *thin)] + quarter_outs(2, near) + quarter_outs(2, near),
+        [],
+        3 * matmul,
+    )
+    bias_one = outs[0].reshape(hidden // 2)
+    sums = jnp.concatenate([sums[:6], grad_centre], axis=0)
+    grads = [(outs[1], outs[2]), (outs[3], outs[4]), gwin_two, gwout_two]
+    return gated, grad_sent, sums, jnp.stack([bias_one, bias_two]), grads
+
+
+def project_back_kernel(peers, *refs):
+    stages = bits_of(peers)
+    d_ref, w_ref, normed_ref, seq_hbm, middle_hbm, gain_ref = refs[:6]
+    grad_refs, tail_ref, out_ref = refs[6:9], refs[9], refs[10]
+    refs = refs[11:]
+    held = [refs[i * stages : (i + 1) * stages] for i in range(4)]
+    landed = [refs[i * stages : (i + 1) * stages] for i in range(4, 8)]
+    reducer = Halving(peers, held, landed, *refs[8 * stages : 8 * stages + 2])
+    refs = refs[8 * stages + 2 :]
+    rows_send, rows_recv, rows_own, shard_send, shard_recv, tail_send, tail_recv = refs[:7]
+    turned, seq_ref, middle_ref, far_send, far_recv, local = refs[7:]
+    seq = lax.axis_index("seq")
+    tokens, features = middle_ref.shape
+    half = d_ref.shape[2]
+    across = {"seq": 1 - seq}
+    seq_copy = pltpu.make_async_copy(seq_hbm, seq_ref, local.at[0])
+    middle_copy = pltpu.make_async_copy(middle_hbm, middle_ref, local.at[1])
+    seq_copy.start()
+    middle_copy.start()
+    greet(reducer.partner + [across])
+    block = lambda which: pl.ds(pl.multiple_of(which * tokens, tokens), tokens)
+
+    def grad_rows(which):
+        total = dot_last(d_ref[0, block(which), :], w_ref[:, :half])
+        total += dot_last(d_ref[1, block(which), :], w_ref[:, half : 2 * half])
+        return total + dot_last(d_ref[2, block(which), :], w_ref[:, 2 * half : 3 * half])
+
+    def norm_sums(which, grad):
+        xhat, _ = normalised(seq_ref[block(which), :].astype(F32))
+        return jnp.sum(grad * xhat, axis=0, keepdims=True), jnp.sum(grad, axis=0, keepdims=True)
+
+    far = grad_rows(1 - seq)
+    rows_send[...] = far.astype(BF16)
+    rows_copy = remote(rows_send, rows_recv, far_send.at[0], far_recv.at[0], across)
+    rows_copy.start()
+    turned[...] = normed_ref[...].T
+    for chunk in range(3):
+        reducer.put(chunk, dot(turned[...], d_ref[chunk]))
+    reducer.finish(0, 0)
+    seq_copy.wait()
+    far_one, far_two = norm_sums(1 - seq, far)
+    reducer.finish(1, 0)
+    own = grad_rows(seq)
+    rows_own[...] = own
+    own_one, own_two = norm_sums(seq, own)
+    line = lambda value: jnp.broadcast_to(value, (64, features))
+    lines = jnp.concatenate([line(far_one + own_one), line(far_two + own_two)], axis=0)
+    reducer.put(3, lines.T)
+    reducer.finish(2, 0)
+    results = [None] * 4
+    for time in range(1, stages + 3):
+        for chunk in range(4):
+            s = time - chunk if chunk < 3 else time - 2
+            if (1 if chunk < 3 else 0) <= s < stages:
+                results[chunk] = reducer.finish(chunk, s)
+    for chunk in range(3):
+        shard_send[chunk] = results[chunk].astype(BF16)
+    tail_send[...] = results[3]
+    shard_copy = remote(shard_send, shard_recv, far_send.at[1], far_recv.at[1], across)
+    tail_copy = remote(tail_send, tail_recv, far_send.at[2], far_recv.at[2], across)
+    shard_copy.start()
+    tail_copy.start()
+    rows_copy.wait_recv()
+    middle_copy.wait()
+    xhat, rate = normalised(seq_ref[block(seq), :].astype(F32))
+    grad = rows_own[...] + rows_recv[...].astype(F32)
+    out_ref[...] = middle_ref[...] + norm_back(grad, xhat, rate, gain_ref[...])
+    columns = lambda which: pl.ds(pl.multiple_of(which * half, half), half)
+    shard_copy.wait_recv()
+    tail_copy.wait_recv()
+    for chunk in range(3):
+        grad_refs[chunk][:, columns(seq)] = shard_send[chunk].astype(F32)
+        grad_refs[chunk][:, columns(1 - seq)] = shard_recv[chunk].astype(F32)
+    tail_ref[...] = tail_send[...] + tail_recv[...]
+    rows_copy.wait_send()
+    shard_copy.wait_send()
+    tail_copy.wait_send()
+    reducer.drain(4)
+
+
+def project_back(peers, grads, weight, normed, sequence, grad_middle, gain):
+    tokens, features = grad_middle.shape
+    half = grads.shape[2]
+    rows = features // peers
+    shape = jax.ShapeDtypeStruct
+    return pl.pallas_call(
+        functools.partial(project_back_kernel, peers),
+        out_shape=[shape((rows, features), F32)] * 3
+        + [shape((rows, 128), F32), shape((tokens, features), F32)],
+        in_specs=[pl.BlockSpec(memory_space=pltpu.VMEM)] * 3
+        + [pl.BlockSpec(memory_space=pl.ANY)] * 2
+        + [pl.BlockSpec(memory_space=pltpu.VMEM)],
+        out_specs=[pl.BlockSpec(memory_space=pltpu.VMEM)] * 5,
+        scratch_shapes=halving_buffers(peers, rows, [half, half, half, 128])
+        + [
+            pltpu.VMEM((tokens, features), BF16),
+            pltpu.VMEM((tokens, features), BF16),
+            pltpu.VMEM((tokens, features), F32),
+            pltpu.VMEM((3, rows, half), BF16),
+            pltpu.VMEM((3, rows, half), BF16),
+            pltpu.VMEM((rows, 128), F32),
+            pltpu.VMEM((rows, 128), F32),
+            pltpu.VMEM(normed.shape[::-1], BF16),
+            pltpu.VMEM(sequence.shape, BF16),
+            pltpu.VMEM((tokens, features), F32),
+            pltpu.SemaphoreType.DMA((3,)),
+            pltpu.SemaphoreType.DMA((3,)),
+            pltpu.SemaphoreType.DMA((2,)),
         ],
-        4 * matmul,
-    )
-    grad_sent, sums, bias_one = outs[0], outs[1], outs[2].reshape(hidden)
-    return gated, grad_sent, sums[:7], bias_one, bias_two, (outs[3:7], outs[7:11]), (gwin_two, gwout_two)
+        compiler_params=pltpu.CompilerParams(
+            vmem_limit_bytes=VMEM_LIMIT, collective_id=0, has_side_effects=True
+        ),
+        cost_estimate=pl.CostEstimate(
+            flops=60 * 10**9, bytes_accessed=40 * 10**6, transcendentals=0
+        ),
+        name="project_back",
+    )(grads, weight, normed, sequence, grad_middle, gain)
 
 
 def body(
@@ -579,9 +839,9 @@
 
     gathered = after(gathered, cot_slots)
 
-    sequence = ordered(left, rows, other_rows, 0).astype(F32)
+    sequence = ordered(left, rows, other_rows, 0)
     gain, shift = gathered[:, 3 * half].astype(F32), gathered[:, 3 * half + 1].astype(F32)
-    xhat, rate = normalised(sequence)
+    xhat, _ = normalised(sequence.astype(F32))
     normed = (xhat * gain + shift).astype(BF16)
     qkv_weight = gathered[:, : 3 * half]
     qkv = dot(normed, qkv_weight).astype(BF16)
@@ -593,30 +853,23 @@
     middle = rows.astype(F32) + dot(mixed, output_full)
 
     z = exchange(after(jnp.take(middle.astype(BF16), order[0], axis=0), far_out))
-    gated, grad_sent, vector_grads, bias_one, bias_two, grads_one, grads_two = expert(
+    gated, grad_sent, vector_grads, bias_grads, weight_grads = expert(
         z, cot_slots, vectors, biases, one, two, over
     )
-    home = jnp.take(exchange(gated), inverse[0], axis=0)
+    returned = exchange(grad_sent)
+    home = jnp.take(exchange(after(gated, returned)), inverse[0], axis=0)
     layer_out = (middle + home.astype(F32)).astype(BF16)
     add = lambda *values: sum(value.astype(F32) for value in values)
-    cut = quarter // 2
-    far_sums = []
-    for _, _, far, cross in grads_one:
-        near = beside(cross)
-        far_sums += [add(far[at : at + cut], near[at : at + cut]).astype(BF16) for at in (0, cut)]
-    coming = jnp.take(after(exchange(grad_sent), *far_sums), inverse[0], axis=0)
-    grads_far = [over(far_sums[0])]
+    coming = jnp.take(returned, inverse[0], axis=0)
     grad_middle = cot.astype(F32) + coming.astype(F32)
 
-    grad_win_two, grad_wout_two = [
-        mine.astype(F32) + beside(near).astype(F32) for mine, near in grads_two
+    grad_win_one, grad_wout_one, grad_win_two, grad_wout_two = [
+        add(mine, beside(near)) for mine, near in weight_grads
     ]
 
     own_half = lambda table, which: lax.dynamic_slice_in_dim(table, which * half, half, 1)
     core = lax.rem(peer, 2)
-    bias_quarters = jnp.stack(
-        [bias_one, jnp.concatenate([bias_two, jnp.zeros_like(bias_two)])]
-    ).reshape(2, 4, quarter)
+    bias_quarters = jnp.pad(bias_grads, ((0, 0), (0, 2 * quarter))).reshape(2, 4, quarter)
     bias_rows = lambda first: ordered(left, bias_quarters[:, first], bias_quarters[:, first + 2], 1)
     flat = lambda table, bias: jnp.concatenate([table.reshape(-1), bias.reshape(-1)])
     small = flat(own_half(vector_grads, core), bias_rows(0)) + beside(
@@ -628,54 +881,24 @@
     bias_out = small[count * half :].reshape(2, 1, 2 * quarter)
 
     grad_attn = grad_middle.astype(BF16)
-    grad_wo = lax.psum_scatter(
-        dot_first(mixed, grad_attn).astype(BF16), "fsdp", scatter_dimension=0, tiled=True
-    ).astype(F32)
-    grad_wo = grad_wo + over(grad_wo)
+    output_terms = dot_first(mixed, grad_attn).astype(BF16)
     grad_mixed = dot_last(grad_attn, output_full).astype(BF16)
     part_of = lambda value, which: lax.dynamic_slice_in_dim(value, which * half, half, 1)
-    other_grad = over(after(part_of(grad_mixed, 1 - seq), grads_far[0]))
+    other_grad = over(part_of(grad_mixed, 1 - seq))
     grad_heads = ordered(left, part_of(grad_mixed, seq), other_grad, 0)
-    for value in far_sums[1:]:
-        grads_far.append(over(after(value, other_grad, grads_far[-1])))
-    grad_win_one, grad_wout_one = [
-        add(g[0], beside(g[1]), jnp.concatenate(grads_far[i : i + 2], axis=0))
-        for g, i in zip(grads_one, (0, 2))
-    ]
-    parts = after(attention_backward(qkv, grad_heads, logs, size), grads_far[1])
-    grad_normed = dot_last(parts[0], qkv_weight[:, :half])
-    grad_normed = grad_normed + dot_last(parts[1], qkv_weight[:, half : 2 * half])
-    grad_normed = grad_normed + dot_last(parts[2], qkv_weight[:, 2 * half :])
-    norm_sums = jnp.stack([jnp.sum(grad_normed * xhat, axis=0), jnp.sum(grad_normed, axis=0)], axis=1)
-    packed = jnp.concatenate(
-        [dot_first(normed, parts[i]).astype(BF16) for i in range(3)]
-        + [jnp.pad(norm_sums, ((0, 0), (0, 126))).astype(BF16)],
-        axis=1,
-    )
-    packed = after(packed, grads_far[2])
-    shard = lax.psum_scatter(packed, "fsdp", scatter_dimension=0, tiled=True)
-    other_shard = over(shard)
-    join = lambda which: ordered(
-        left,
-        shard[:, which * half : (which + 1) * half],
-        other_shard[:, which * half : (which + 1) * half],
-        1,
-    ).astype(F32)
-    norm_grads = shard[:, 3 * half : 3 * half + 2].astype(F32)
-    norm_grads = norm_grads + other_shard[:, 3 * half : 3 * half + 2].astype(F32)
-    arrived = over(block_of(grad_normed, 1 - seq).astype(BF16)).astype(F32)
-    arrived = after(arrived, grads_far[3])
-    grad_own = block_of(grad_normed, seq) + arrived
-    own_xhat, own_rate = normalised(rows.astype(F32))
-    grad_inputs = grad_middle + norm_back(grad_own, own_xhat, own_rate, gain)
+    parts, grad_wo = attention_backward(peers, qkv, grad_heads, logs, output_terms, size)
+    grad_wo = grad_wo + over(grad_wo)
+    grad_q, grad_k, grad_v, norm_grads, grad_inputs = project_back(
+        peers, parts, gathered, normed, sequence, grad_middle, gain[None]
+    )
     return (
         layer_out[None],
         grad_inputs[None],
         norm_grads[:, 0],
-        norm_grads[:, 1],
-        join(0),
-        join(1),
-        join(2),
+        norm_grads[:, 64],
+        grad_q,
+        grad_k,
+        grad_v,
         grad_wo,
         vector_out[0],
         vector_out[1],

time: 553 us -> 518 us (0.937)
  Pallas kernels: 154 us -> 226 us
  waiting for transfers between devices: 195 us -> 139 us
  other arithmetic: 61.9 us -> 41.9 us
  matrix products: 29.3 us -> 13.5 us
  local copies, waits for them, and re-layouts: 35.8 us -> 25.5 us
    pallas_call x1 -> x2, Pallas kernels: 24 us -> 86.7 us  [the longest x1 48.4 us: project_back(): pl.pallas_call(functools.partial(project_back_kernel, peers), out_shape=[...]
    ppermute x31 -> x25, waiting for transfers between devices: 164 us -> 117 us  [swapped(): return lax.ppermute(value, axis, pairs)]
    dot_general x4 -> x1, matrix products: 13 us -> 1.28 us  [dot_last(): lax.dot_general(left, right, (((1,), (1,)), ((), ())), preferred_element_...]
    convert_element_type x7 -> x1, other arithmetic: 11.6 us -> 1.21 us  [expert(): grad_sent = (back + score * vectors[6]).astype(BF16)]
    all_to_all x4, waiting for transfers between devices: 29.7 us -> 19.6 us  [body(): lax.all_to_all(value.reshape(peers, tokens // peers, features), 'fsdp', s...]
    pallas_call x7 -> x8, Pallas kernels: 114 us -> 124 us  [expert_call(): pl.pallas_call(kernel, grid=(steps,), out_shape=tuple((s for s, _, _ in o...]
    unnamed x116 -> x104, local copies, waits for them, and re-layouts: 14.3 us -> 8.71 us
    ppermute x31 -> x25, starting transfers between devices: 24.8 us -> 21.7 us  [swapped(): return lax.ppermute(value, axis, pairs)]
  transfers between devices with their start and end apart: 39 -> 31, of which waited for: 17 -> 11; matrix products, arithmetic and copies ran while one was open for 21% -> 13% of each run, Pallas kernels for 20% -> 37%
where the time goes in v3:
time: 518 us; the launch traced here: 508 us
  Pallas kernels  226 us (44%)
  waiting for transfers between devices  139 us (27%)
  starting transfers between devices  46.9 us (9%)
  other arithmetic  41.9 us (8%)
  local copies, waits for them, and re-layouts  25.5 us (5%)
  between operations  15.4 us (3%)
  matrix products  13.5 us (3%)
    pallas_call x8, Pallas kernels, expert_call(): pl.pallas_call(kernel, grid=(steps,), out_shape=tuple((s for s, _, _ in o...  124 us
    ppermute x25, waiting for transfers between devices, swapped(): return lax.ppermute(value, axis, pairs)  117 us
    pallas_call x1, Pallas kernels, project_back(): pl.pallas_call(functools.partial(project_back_kernel, peers), out_shape=[...  48.4 us
    pallas_call x1, Pallas kernels, attention_backward(): pl.pallas_call(functools.partial(attention_backward_kernel, peers, size),...  38.3 us
    all_to_all x4, starting transfers between devices, body(): lax.all_to_all(value.reshape(peers, tokens // peers, features), 'fsdp', s...  25 us
    ppermute x25, starting transfers between devices, swapped(): return lax.ppermute(value, axis, pairs)  21.7 us
    all_to_all x4, waiting for transfers between devices, body(): lax.all_to_all(value.reshape(peers, tokens // peers, features), 'fsdp', s...  19.6 us
    pallas_call x1, Pallas kernels, attention_forward(): pl.pallas_call(functools.partial(attention_forward_kernel, size), grid=(p...  15.9 us
  transfers between devices with their start and end apart: 31, of which 11 were waited for; matrix products, arithmetic and copies ran while one was open for 13% of the time, Pallas kernels for 37%

profile of v3, /device:TPU:0, one launch (start us, length us, event | category | flops | bytes accessed | tf_op | source)
XLA Modules:
  0.0 508.1 jit_solution(7794579457660771862)
XLA Ops:
  8.2 0.9 constant_dynamic-slice_fusion.11
  9.0 0.8 constant_dynamic-slice_fusion.12
  10.6 3.0 collective-permute-start
  14.3 2.1 gather_fusion
  16.4 20.6 %collective-permute-done = bf16[512,1024]{1,0:T(8,128)(2,1)S(1)} collective-permute-done((bf16[512,1024]{1,0:T(8,128)(2,1)}, bf16[512,1024]{1,0:T(8,128)(2,1)S(1)}, u32[]{:S(2)}, u32[]{:S(2)}) %collective-permute-start) | collective-permute-done | bytes 1048608 | tf_op jit(solution)/shard_map/ppermute | solution.py:23
  37.0 1.7 collective-permute-start.1
  38.7 1.1 broadcast_select_fusion.1
  39.9 5.9 %all-to-all-start = ((bf16[16,32,1024]{2,1,0:T(8,128)(2,1)}), bf16[16,32,1024]{2,1,0:T(8,128)(2,1)S(1)}, u32[]{:S(2)}, u32[]{:S(2)}) async-start(bf16[16,32,1024]{2,1,0:T(8,128)(2,1)} %bitcast.5), calls=%async_computation | async-start | bytes 2097152 | tf_op jit(solution)/shard_map/all_to_all | solution.py:831
  46.6 2.6 convert_reduce_fusion
  49.9 34.2 %collective-permute-done.1.refs_9_.refs_12_ = bf16[1024,1024]{1,0:T(8,128)(2,1)} collective-permute-done((bf16[1024,1024]{1,0:T(8,128)(2,1)}, bf16[1024,1024]{1,0:T(8,128)(2,1)}, u32[]{:S(2)}, u32[]{:S(2)}) %collective-permute-start.1) | collective-permute-done | bytes 2097184 | tf_op jit(solution)/shard_map/ppermute | solution.py:23
  84.1 1.4 collective-permute-start.3
  85.5 1.7 convert_reduce_fusion.2
  87.3 0.8 fusion.5.refs_2_
  88.1 1.3 copy-done.9
  89.6 4.8 convolution_convert_fusion.q_ref.k_ref.v_ref.refs_0_.refs_1_.refs_2_
  94.4 15.9 %attention_forward.1 = (bf16[1024,512]{1,0:T(8,128)(2,1)}, f32[4,2,1024]{2,1,0:T(2,128)}) custom-call(bf16[1024,1536]{1,0:T(8,128)(2,1)} %convolution_convert_fusion.q_ref.k_ref.v_ref.refs_0_.refs_1_.refs_2_, bf16[1024,1536]{1,0:T(8,128)(2,1)} %convolution_convert_fusion.q_ref.k_ref.v_ref.refs_0_.refs_1_.refs_2_, ...), custom_call_target="tpu_custom_call" | custom-call | flops 4294967296 | bytes 5242880 | tf_op jit(solution)/shard_map/attention_forward/pallas_call | solution.py:227
  110.3 2.1 constant_dynamic-slice_fusion.9
  113.1 2.0 all-gather.5.cloned.1.call-done
  115.1 26.4 %collective-permute-done.2 = bf16[512,512]{1,0:T(8,128)(2,1)S(1)} collective-permute-done((bf16[512,512]{1,0:T(8,128)(2,1)S(1)}, bf16[512,512]{1,0:T(8,128)(2,1)S(1)}, u32[]{:S(2)}, u32[]{:S(2)}) %collective-permute-start.2) | collective-permute-done | bytes 524320 | tf_op jit(solution)/shard_map/ppermute | solution.py:23
  141.5 0.8 copy-done.46
  142.2 4.8 fusion.30
  147.1 2.0 gather_fusion.1
  149.2 1.1 broadcast_select_fusion
  150.4 5.8 %all-to-all-start.1 = ((bf16[16,32,1024]{2,1,0:T(8,128)(2,1)}), bf16[16,32,1024]{2,1,0:T(8,128)(2,1)S(1)}, u32[]{:S(2)}, u32[]{:S(2)}) async-start(bf16[16,32,1024]{2,1,0:T(8,128)(2,1)} %bitcast.86), calls=%async_computation.1 | async-start | bytes 2097152 | tf_op jit(solution)/shard_map/all_to_all | solution.py:831
  158.1 2.4 collective-permute-done.4
  162.3 16.8 %all-to-all-done.1 = bf16[16,32,1024]{2,1,0:T(8,128)(2,1)S(1)} async-done(((bf16[16,32,1024]{2,1,0:T(8,128)(2,1)}), bf16[16,32,1024]{2,1,0:T(8,128)(2,1)S(1)}, u32[]{:S(2)}, u32[]{:S(2)}) %all-to-all-start.1) | async-done | bytes 1048608 | tf_op jit(solution)/shard_map/all_to_all | solution.py:831
  180.4 1.5 collective-permute-start.11
  181.9 19.6 %forward_first.1 = (f32[512,1024]{1,0:T(8,128)}, bf16[512,1024]{1,0:T(8,128)(2,1)}, bf16[512,2048]{1,0:T(8,128)(2,1)}, bf16[512,4096]{1,0:T(8,128)(2,1)}, bf16[512,1024]{1,0:T(8,128)(2,1)}) custom-call(bf16[512,1024]{1,0:T(8,128)(2,1)} %bitcast.83, f32[1,1024]{1,0:T(1,128)} %get-tuple-element.151.refs_1_.refs_7_, f32[1,1024]{1,0:T(1,128)} %get-tuple-element.150.refs_2_, ...), custom_call_target="tpu_custom_call" | custom-call | flops 17179869184 | bytes 28348416 | tf_op jit(solution)/shard_map/forward_first/pallas_call | solution.py:488
  201.6 4.0 collective-permute-done.11.grad_ref.refs_7_
  205.6 1.5 collective-permute-start.12
  207.8 22.3 %collective-permute-done.12.normed_ref.refs_5_ = bf16[512,1024]{1,0:T(8,128)(2,1)S(1)} collective-permute-done((bf16[512,1024]{1,0:T(8,128)(2,1)}, bf16[512,1024]{1,0:T(8,128)(2,1)S(1)}, u32[]{:S(2)}, u32[]{:S(2)}) %collective-permute-start.12) | collective-permute-done | bytes 1048608 | tf_op jit(solution)/shard_map/ppermute | solution.py:23
  230.1 1.5 collective-permute-start.13
  231.6 11.1 %forward_second.3 = (bf16[512,1024]{1,0:T(8,128)(2,1)}, bf16[512,2048]{1,0:T(8,128)(2,1)}, bf16[512,2048]{1,0:T(8,128)(2,1)}) custom-call(bf16[512,1024]{1,0:T(8,128)(2,1)} %copy-done.43, f32[4,1,512]{2,1,0:T(1,128)} %get-tuple-element.145.bias_ref, bf16[1024,1024]{1,0:T(8,128)(2,1)} %bitcast.118, bf16[1024,1024]{1,0:T(8,128)(2,1)} %collective-permute-done.9.refs_1_, ...), custom_call_target="tpu_custom_call" | custom-call | flops 8589934592 | bytes 14688256 | tf_op jit(solution)/shard_map/forward_second/pallas_call | solution.py:488
  242.7 10.3 %backward_second.2 = (bf16[512,1024]{1,0:T(8,128)(2,1)}, bf16[512,2048]{1,0:T(8,128)(2,1)}) custom-call(bf16[512,1024]{1,0:T(8,128)(2,1)} %copy-done.41, bf16[512,2048]{1,0:T(8,128)(2,1)} %get-tuple-element.81.slope_ref, bf16[1024,1024]{1,0:T(8,128)(2,1)} %bitcast.119, bf16[1024,1024]{1,0:T(8,128)(2,1)} %collective-permute-done.9.refs_1_, ...), custom_call_target="tpu_custom_call" | custom-call | flops 8589934592 | bytes 14680064 | tf_op jit(solution)/shard_map/backward_second/pallas_call | solution.py:488
  253.7 1.5 collective-permute-start.14
  255.2 11.5 %forward_second.2 = (f32[512,1024]{1,0:T(8,128)}, bf16[512,2048]{1,0:T(8,128)(2,1)}, bf16[512,2048]{1,0:T(8,128)(2,1)}) custom-call(bf16[512,1024]{1,0:T(8,128)(2,1)} %get-tuple-element.79.normed_ref.refs_4_, f32[4,1,512]{2,1,0:T(1,128)} %get-tuple-element.145.bias_ref, bf16[1024,1024]{1,0:T(8,128)(2,1)} %bitcast.120, ...), custom_call_target="tpu_custom_call" | custom-call | flops 8589934592 | bytes 15736832 | tf_op jit(solution)/shard_map/forward_second/pallas_call | solution.py:488
  266.7 10.8 %backward_second.3 = (f32[512,1024]{1,0:T(8,128)}, bf16[512,2048]{1,0:T(8,128)(2,1)}) custom-call(bf16[512,1024]{1,0:T(8,128)(2,1)} %copy-done.17, bf16[512,2048]{1,0:T(8,128)(2,1)} %get-tuple-element.87.slope_ref, bf16[1024,1024]{1,0:T(8,128)(2,1)} %bitcast.121, bf16[1024,1024]{1,0:T(8,128)(2,1)} %collective-permute-done.9.refs_1_, ...), custom_call_target="tpu_custom_call" | custom-call | flops 8589934592 | bytes 15728640 | tf_op jit(solution)/shard_map/backward_second/pallas_call | solution.py:488
  278.5 22.6 %backward_first.1 = (f32[512,1024]{1,0:T(8,128)}, bf16[512,1024]{1,0:T(8,128)(2,1)}, f32[8,1024]{1,0:T(8,128)}, bf16[512,2048]{1,0:T(8,128)(2,1)}) custom-call(f32[512,1024]{1,0:T(8,128)} %get-tuple-element.88.refs_0_, bf16[512,1024]{1,0:T(8,128)(2,1)} %copy-done.45, bf16[512,1024]{1,0:T(8,128)(2,1)} %copy-done.17, bf16[512,1024]{1,0:T(8,128)(2,1)} %bitcast.84, ...), custom_call_target="tpu_custom_call" | custom-call | flops 17179869184 | bytes 34648064 | tf_op jit(solution)/shard_map/backward_first/pallas_call | solution.py:488
  301.2 1.2 collective-permute-start.18
  302.4 15.7 %weights_second.1 = (f32[4,1,512]{2,1,0:T(1,128)}, bf16[1024,1024]{1,0:T(8,128)(2,1)}, bf16[1024,1024]{1,0:T(8,128)(2,1)}, bf16[1024,1024]{1,0:T(8,128)(2,1)}, bf16[1024,1024]{1,0:T(8,128)(2,1)}) custom-call(bf16[512,2048]{1,0:T(8,128)(2,1)} %get-tuple-element.105.refs_0_, bf16[512,2048]{1,0:T(8,128)(2,1)} %get-tuple-element.106.refs_1_, ...), custom_call_target="tpu_custom_call" | custom-call | flops 17179869184 | bytes 20979712 | tf_op jit(solution)/shard_map/weights_second/pallas_call | solution.py:488
  318.6 1.6 fusion.10
  320.2 1.2 add_convert_fusion.1
  321.4 7.3 %all-to-all-start.2 = ((bf16[16,32,1024]{2,1,0:T(8,128)(2,1)}), bf16[16,32,1024]{2,1,0:T(8,128)(2,1)S(1)}, u32[]{:S(2)}, u32[]{:S(2)}) async-start(bf16[16,32,1024]{2,1,0:T(8,128)(2,1)} %bitcast.18), calls=%async_computation.2 | async-start | bytes 2097152 | tf_op jit(solution)/shard_map/all_to_all | solution.py:831
  328.7 22.0 %weights_first.1 = (f32[4,1,512]{2,1,0:T(1,128)}, bf16[1024,1024]{1,0:T(8,128)(2,1)}, bf16[1024,1024]{1,0:T(8,128)(2,1)}, bf16[1024,1024]{1,0:T(8,128)(2,1)}, bf16[1024,1024]{1,0:T(8,128)(2,1)}) custom-call(bf16[512,2048]{1,0:T(8,128)(2,1)} %get-tuple-element.101.refs_0_, bf16[512,2048]{1,0:T(8,128)(2,1)} %get-tuple-element.102.refs_1_, ...), custom_call_target="tpu_custom_call" | custom-call | flops 25769803776 | bytes 25182208 | tf_op jit(solution)/shard_map/weights_first/pallas_call | solution.py:488
  352.7 6.1 %all-to-all-start.3 = ((bf16[16,32,1024]{2,1,0:T(8,128)(2,1)}), bf16[16,32,1024]{2,1,0:T(8,128)(2,1)S(1)}, u32[]{:S(2)}, u32[]{:S(2)}) async-start(bf16[16,32,1024]{2,1,0:T(8,128)(2,1)} %bitcast.20), calls=%async_computation.3 | async-start | bytes 2097152 | tf_op jit(solution)/shard_map/all_to_all | solution.py:831
  358.8 5.1 %add_bitcast_fusion.1 = f32[1,1024,1024]{2,1,0:T(8,128)} fusion(bf16[1024,1024]{1,0:T(8,128)(2,1)} %collective-permute-done.23, bf16[1024,1024]{1,0:T(8,128)(2,1)} %get-tuple-element.114), kind=kLoop, calls=%fused_computation.13 | loop fusion | flops 3145728 | bytes 8388608 | tf_op jit(solution)/shard_map/broadcast_in_dim | solution.py:911
  364.4 1.0 collective-permute-start.20
  365.4 5.1 %add_bitcast_fusion = f32[1,1024,1024]{2,1,0:T(8,128)} fusion(bf16[1024,1024]{1,0:T(8,128)(2,1)} %collective-permute-done.24, bf16[1024,1024]{1,0:T(8,128)(2,1)} %get-tuple-element.116), kind=kLoop, calls=%fused_computation.12 | loop fusion | flops 3145728 | bytes 8388608 | tf_op jit(solution)/shard_map/broadcast_in_dim | solution.py:913
  371.7 2.0 gather_fusion.3
  373.8 5.1 %add_bitcast_fusion.3 = f32[1,1024,1024]{2,1,0:T(8,128)} fusion(bf16[1024,1024]{1,0:T(8,128)(2,1)} %collective-permute-done.21, bf16[1024,1024]{1,0:T(8,128)(2,1)} %get-tuple-element.110), kind=kLoop, calls=%fused_computation.15 | loop fusion | flops 3145728 | bytes 8388608 | tf_op jit(solution)/shard_map/broadcast_in_dim | solution.py:905
  378.9 2.8 all-to-all-done.3
  381.8 2.8 gather_fusion.2
  384.5 3.6 convert_add_fusion
  388.1 1.3 convolution_convert_fusion.2
  389.5 1.0 collective-permute-start.16
  391.0 4.6 add_bitcast_fusion.2
  395.6 2.6 convolution_convert_fusion.1
  398.2 5.8 %collective-permute-done.16 = bf16[512,512]{1,0:T(8,128)(2,1)S(1)} collective-permute-done((bf16[512,512]{1,0:T(8,128)(2,1)S(1)}, bf16[512,512]{1,0:T(8,128)(2,1)S(1)}, u32[]{:S(2)}, u32[]{:S(2)}) %collective-permute-start.16) | collective-permute-done | bytes 524320 | tf_op jit(solution)/shard_map/ppermute | solution.py:23
  404.0 1.4 maximum_select_fusion.2.refs_3_
  405.4 38.3 %attention_backward.1 = (bf16[3,1024,512]{2,1,0:T(8,128)(2,1)}, f32[64,1024]{1,0:T(8,128)}) custom-call(bf16[1024,1536]{1,0:T(8,128)(2,1)} %convolution_convert_fusion.q_ref.k_ref.v_ref.refs_0_.refs_1_.refs_2_, bf16[1024,1536]{1,0:T(8,128)(2,1)} %convolution_convert_fusion.q_ref.k_ref.v_ref.refs_0_.refs_1_.refs_2_, ...), custom_call_target="tpu_custom_call" | custom-call | flops 10737418240 | bytes 8388608 | tf_op jit(solution)/shard_map/attention_backward/pallas_call | solution.py:251
  443.7 1.0 collective-permute-start.17
  444.7 48.4 %project_back.1 = (f32[64,1024]{1,0:T(8,128)}, f32[64,1024]{1,0:T(8,128)}, f32[64,1024]{1,0:T(8,128)}, f32[64,128]{1,0:T(8,128)}, f32[512,1024]{1,0:T(8,128)}) custom-call(bf16[3,1024,512]{2,1,0:T(8,128)(2,1)} %get-tuple-element.93.refs_0_, bf16[1024,1664]{1,0:T(8,128)(2,1)} %all-gather.3.cloned.1.call-done.refs_1_, bf16[1024,1024]{1,0:T(8,128)(2,1)} %copy-done.9, ...), custom_call_target="tpu_custom_call" | custom-call | flops 60000002048 | bytes 40000000 | tf_op jit(solution)/shard_map/project_back/pallas_call | solution.py:720
  493.1 1.5 slice_reduce_fusion
  495.4 3.2 copy.68
  (195 shorter events, 19.7 us)
Async XLA Ops:
  7.2 7.1 %copy-start.2 = (bf16[1,512,1024]{2,1,0:T(8,128)(2,1)S(1)}, bf16[1,512,1024]{2,1,0:T(8,128)(2,1)}, u32[]{:S(2)}) copy-start(bf16[1,512,1024]{2,1,0:T(8,128)(2,1)} %param.47) | copy-start | bytes 3145732
  7.2 78.3 %all-gather.3.cloned.1.call-start = ((), (), s32[]{:S(2)}) async-start(), calls=%async_computation.4 | async-start | bytes 3620864 | tf_op jit(solution)/shard_map/all_gather | solution.py:795
  10.6 26.4 %collective-permute-start = (bf16[512,1024]{1,0:T(8,128)(2,1)}, bf16[512,1024]{1,0:T(8,128)(2,1)S(1)}, u32[]{:S(2)}, u32[]{:S(2)}) collective-permute-start(bf16[512,1024]{1,0:T(8,128)(2,1)} %bitcast.88), channel_id=1, source_target_pairs={{0,16},{16,0},{1,17},{17,1},{2,18},{18,2},{3,19},{19,3},{4,20},{20... | collective-permute-start | bytes 3145736 | tf_op jit(solution)/shard_map/ppermute | solution.py:23
  37.0 47.1 %collective-permute-start.1 = (bf16[1024,1024]{1,0:T(8,128)(2,1)}, bf16[1024,1024]{1,0:T(8,128)(2,1)}, u32[]{:S(2)}, u32[]{:S(2)}) collective-permute-start(bf16[1024,1024]{1,0:T(8,128)(2,1)} %bitcast.122), channel_id=1, source_target_pairs={{0,16},{16,0},{1,17},{17,1},{2,18},{18,2},{3,19},{19,3},{4,20},{20... | collective-permute-start | bytes 6291464 | tf_op jit(solution)/shard_map/ppermute | solution.py:23
  39.9 45.7 %all-to-all-start = ((bf16[16,32,1024]{2,1,0:T(8,128)(2,1)}), bf16[16,32,1024]{2,1,0:T(8,128)(2,1)S(1)}, u32[]{:S(2)}, u32[]{:S(2)}) async-start(bf16[16,32,1024]{2,1,0:T(8,128)(2,1)} %bitcast.5), calls=%async_computation | async-start | bytes 2097152 | tf_op jit(solution)/shard_map/all_to_all | solution.py:831
  45.8 69.2 %all-gather.5.cloned.1.call-start = ((), (), s32[]{:S(2)}) async-start(), calls=%async_computation.5 | async-start | bytes 2228224 | tf_op jit(solution)/shard_map/all_gather | solution.py:801
  49.2 38.9 %copy-start.4 = (bf16[1024,1024]{1,0:T(8,128)(2,1)}, bf16[1024,1024]{1,0:T(8,128)(2,1)S(1)}, u32[]{:S(2)}) copy-start(bf16[1024,1024]{1,0:T(8,128)(2,1)S(1)} %get-tuple-element.123.refs_3_) | copy-start | bytes 6291460
  84.1 66.3 %collective-permute-start.3 = (bf16[1024,1024]{1,0:T(8,128)(2,1)}, bf16[1024,1024]{1,0:T(8,128)(2,1)}, u32[]{:S(2)}, u32[]{:S(2)}) collective-permute-start(bf16[1024,1024]{1,0:T(8,128)(2,1)} %bitcast.9.refs_11_.refs_14_.refs_9_), channel_id=1, source_target_pairs={{0,16},{16,0},{1,17},{17,1},{2,18},{18,2},{3,19},{19,3},{4,20},{20... | collective-permute-start | bytes 6291464 | tf_op jit(solution)/shard_map/ppermute | solution.py:23
  85.5 93.9 %copy-start.7 = (bf16[16,32,1024]{2,1,0:T(8,128)(2,1)}, bf16[16,32,1024]{2,1,0:T(8,128)(2,1)S(1)}, u32[]{:S(2)}) copy-start(bf16[16,32,1024]{2,1,0:T(8,128)(2,1)S(1)} %all-to-all-done) | copy-start | bytes 3145732
  110.3 32.0 %copy-start.15 = (bf16[1,512,1024]{2,1,0:T(8,128)(2,1)S(1)}, bf16[1,512,1024]{2,1,0:T(8,128)(2,1)}, u32[]{:S(2)}) copy-start(bf16[1,512,1024]{2,1,0:T(8,128)(2,1)} %param.25) | copy-start | bytes 3145732
  112.4 29.0 %collective-permute-start.2 = (bf16[512,512]{1,0:T(8,128)(2,1)S(1)}, bf16[512,512]{1,0:T(8,128)(2,1)S(1)}, u32[]{:S(2)}, u32[]{:S(2)}) collective-permute-start(bf16[512,512]{1,0:T(8,128)(2,1)S(1)} %get-tuple-element.129), channel_id=1, source_target_pairs={{0,16},{16,0},{1,17},{17,1},{2,18},{18,2},{3,19},{19,3},{4,20},{20... | collective-permute-start | bytes 1572872 | tf_op jit(solution)/shard_map/ppermute | solution.py:23
  149.1 8.2 %copy-start.26 = (bf16[1,2048]{1,0:T(2,128)(2,1)S(1)}, bf16[1,2048]{1,0:T(2,128)(2,1)}, u32[]{:S(2)}) copy-start(bf16[1,2048]{1,0:T(2,128)(2,1)} %param.41) | copy-start | bytes 12292
  149.1 8.2 %copy-start.27 = (bf16[1,2048]{1,0:T(2,128)(2,1)S(1)}, bf16[1,2048]{1,0:T(2,128)(2,1)}, u32[]{:S(2)}) copy-start(bf16[1,2048]{1,0:T(2,128)(2,1)} %param.35) | copy-start | bytes 12292
  149.1 8.2 %copy-start.33 = (bf16[1,512]{1,0:T(2,128)(2,1)S(1)}, bf16[1,512]{1,0:T(2,128)(2,1)}, u32[]{:S(2)}) copy-start(bf16[1,512]{1,0:T(2,128)(2,1)} %param.32) | copy-start | bytes 3076
  149.2 8.2 %copy-start.34 = (bf16[1,512]{1,0:T(2,128)(2,1)S(1)}, bf16[1,512]{1,0:T(2,128)(2,1)}, u32[]{:S(2)}) copy-start(bf16[1,512]{1,0:T(2,128)(2,1)} %param.33) | copy-start | bytes 3076
  149.2 8.2 %copy-start.35 = (bf16[1,512]{1,0:T(2,128)(2,1)S(1)}, bf16[1,512]{1,0:T(2,128)(2,1)}, u32[]{:S(2)}) copy-start(bf16[1,512]{1,0:T(2,128)(2,1)} %param.37) | copy-start | bytes 3076
  149.2 8.2 %copy-start.36 = (bf16[1,512]{1,0:T(2,128)(2,1)S(1)}, bf16[1,512]{1,0:T(2,128)(2,1)}, u32[]{:S(2)}) copy-start(bf16[1,512]{1,0:T(2,128)(2,1)} %param.38) | copy-start | bytes 3076
  149.2 8.2 %copy-start.37 = (bf16[1,512]{1,0:T(2,128)(2,1)S(1)}, bf16[1,512]{1,0:T(2,128)(2,1)}, u32[]{:S(2)}) copy-start(bf16[1,512]{1,0:T(2,128)(2,1)} %param.39) | copy-start | bytes 3076
  149.2 8.2 %copy-start.38 = (bf16[1,512]{1,0:T(2,128)(2,1)S(1)}, bf16[1,512]{1,0:T(2,128)(2,1)}, u32[]{:S(2)}) copy-start(bf16[1,512]{1,0:T(2,128)(2,1)} %param.43) | copy-start | bytes 3076
  149.2 8.2 %copy-start.39 = (bf16[1,512]{1,0:T(2,128)(2,1)S(1)}, bf16[1,512]{1,0:T(2,128)(2,1)}, u32[]{:S(2)}) copy-start(bf16[1,512]{1,0:T(2,128)(2,1)} %param.44) | copy-start | bytes 3076
  150.4 28.7 %all-to-all-start.1 = ((bf16[16,32,1024]{2,1,0:T(8,128)(2,1)}), bf16[16,32,1024]{2,1,0:T(8,128)(2,1)S(1)}, u32[]{:S(2)}, u32[]{:S(2)}) async-start(bf16[16,32,1024]{2,1,0:T(8,128)(2,1)} %bitcast.86), calls=%async_computation.1 | async-start | bytes 2097152 | tf_op jit(solution)/shard_map/all_to_all | solution.py:831
  156.1 23.6 %collective-permute-start.5 = (bf16[1024,1024]{1,0:T(8,128)(2,1)}, bf16[1024,1024]{1,0:T(8,128)(2,1)}, u32[]{:S(2)}, u32[]{:S(2)}) collective-permute-start(bf16[1024,1024]{1,0:T(8,128)(2,1)} %bitcast.123), channel_id=1, source_target_pairs={{0,1},{1,0},{2,3},{3,2},{4,5},{5,4},{6,7},{7,6},{8,9},{9,8},{10,11... | collective-permute-start | bytes 6291464 | tf_op jit(solution)/shard_map/ppermute | solution.py:23
  156.7 23.7 %collective-permute-start.7 = (bf16[1024,1024]{1,0:T(8,128)(2,1)}, bf16[1024,1024]{1,0:T(8,128)(2,1)}, u32[]{:S(2)}, u32[]{:S(2)}) collective-permute-start(bf16[1024,1024]{1,0:T(8,128)(2,1)} %bitcast.9.refs_11_.refs_14_.refs_9_), channel_id=1, source_target_pairs={{0,1},{1,0},{2,3},{3,2},{4,5},{5,4},{6,7},{7,6},{8,9},{9,8},{10,11... | collective-permute-start | bytes 6291464 | tf_op jit(solution)/shard_map/ppermute | solution.py:23
  156.8 25.1 %collective-permute-start.6 = (bf16[1024,1024]{1,0:T(8,128)(2,1)}, bf16[1024,1024]{1,0:T(8,128)(2,1)}, u32[]{:S(2)}, u32[]{:S(2)}) collective-permute-start(bf16[1024,1024]{1,0:T(8,128)(2,1)} %collective-permute-done.1.refs_9_.refs_12_), channel_id=1, source_target_pairs={{0,1},{1,0},{2,3},{3,2},{4,5},{5,4},{6,7},{7,6},{8,9},{9,8},{10,11... | collective-permute-start | bytes 6291464 | tf_op jit(solution)/shard_map/ppermute | solution.py:23
  157.2 24.7 %collective-permute-start.8 = (bf16[1024,1024]{1,0:T(8,128)(2,1)}, bf16[1024,1024]{1,0:T(8,128)(2,1)}, u32[]{:S(2)}, u32[]{:S(2)}) collective-permute-start(bf16[1024,1024]{1,0:T(8,128)(2,1)} %collective-permute-done.3.refs_13_.refs_16_), channel_id=1, source_target_pairs={{0,1},{1,0},{2,3},{3,2},{4,5},{5,4},{6,7},{7,6},{8,9},{9,8},{10,11... | collective-permute-start | bytes 6291464 | tf_op jit(solution)/shard_map/ppermute | solution.py:23
  157.5 3.0 collective-permute-start.4
  160.5 71.0 %collective-permute-start.9 = (bf16[1024,1024]{1,0:T(8,128)(2,1)}, bf16[1024,1024]{1,0:T(8,128)(2,1)}, u32[]{:S(2)}, u32[]{:S(2)}) collective-permute-start(bf16[1024,1024]{1,0:T(8,128)(2,1)} %bitcast.117), channel_id=1, source_target_pairs={{0,1},{1,0},{2,3},{3,2},{4,5},{5,4},{6,7},{7,6},{8,9},{9,8},{10,11... | collective-permute-start | bytes 6291464 | tf_op jit(solution)/shard_map/ppermute | solution.py:23
  162.3 39.3 %copy-start.24 = (f32[1,1024]{1,0:T(1,128)}, f32[1,1024]{1,0:T(1,128)S(1)}, u32[]{:S(2)}) copy-start(f32[1,1024]{1,0:T(1,128)S(1)} %get-tuple-element.152.refs_9_) | copy-start | bytes 12292
  179.7 21.8 %copy-start.17 = (bf16[512,1024]{1,0:T(8,128)(2,1)}, bf16[512,1024]{1,0:T(8,128)(2,1)S(1)}, u32[]{:S(2)}) copy-start(bf16[512,1024]{1,0:T(8,128)(2,1)S(1)} %fusion.9.grad_ref.refs_2_.refs_6_) | copy-start | bytes 3145732
  179.7 51.9 %collective-permute-start.10 = (bf16[1024,1024]{1,0:T(8,128)(2,1)}, bf16[1024,1024]{1,0:T(8,128)(2,1)}, u32[]{:S(2)}, u32[]{:S(2)}) collective-permute-start(bf16[1024,1024]{1,0:T(8,128)(2,1)} %bitcast.16.refs_2_), channel_id=1, source_target_pairs={{0,1},{1,0},{2,3},{3,2},{4,5},{5,4},{6,7},{7,6},{8,9},{9,8},{10,11... | collective-permute-start | bytes 6291464 | tf_op jit(solution)/shard_map/ppermute | solution.py:23
  180.4 25.2 %collective-permute-start.11 = (bf16[512,1024]{1,0:T(8,128)(2,1)S(1)}, bf16[512,1024]{1,0:T(8,128)(2,1)S(1)}, u32[]{:S(2)}, u32[]{:S(2)}) collective-permute-start(bf16[512,1024]{1,0:T(8,128)(2,1)S(1)} %fusion.9.grad_ref.refs_2_.refs_6_), channel_id=1, source_target_pairs={{0,16},{16,0},{1,17},{17,1},{2,18},{18,2},{3,19},{19,3},{4,20},{20... | collective-permute-start | bytes 3145736 | tf_op jit(solution)/shard_map/ppermute | solution.py:23
  181.9 25.2 %copy-start.31 = (s32[1,512]{1,0:T(1,128)S(1)}, s32[1,512]{1,0:T(1,128)}, u32[]{:S(2)}) copy-start(s32[1,512]{1,0:T(1,128)} %param.46) | copy-start | bytes 6148
  205.6 37.1 %copy-start.41 = (bf16[512,1024]{1,0:T(8,128)(2,1)}, bf16[512,1024]{1,0:T(8,128)(2,1)S(1)}, u32[]{:S(2)}) copy-start(bf16[512,1024]{1,0:T(8,128)(2,1)S(1)} %collective-permute-done.11.grad_ref.refs_7_) | copy-start | bytes 3145732
  205.6 24.5 %collective-permute-start.12 = (bf16[512,1024]{1,0:T(8,128)(2,1)}, bf16[512,1024]{1,0:T(8,128)(2,1)S(1)}, u32[]{:S(2)}, u32[]{:S(2)}) collective-permute-start(bf16[512,1024]{1,0:T(8,128)(2,1)} %get-tuple-element.79.normed_ref.refs_4_), channel_id=1, source_target_pairs={{0,16},{16,0},{1,17},{17,1},{2,18},{18,2},{3,19},{19,3},{4,20},{20... | collective-permute-start | bytes 3145736 | tf_op jit(solution)/shard_map/ppermute | solution.py:23
  230.1 23.6 %collective-permute-start.13 = (bf16[512,1024]{1,0:T(8,128)(2,1)}, bf16[512,1024]{1,0:T(8,128)(2,1)S(1)}, u32[]{:S(2)}, u32[]{:S(2)}) collective-permute-start(bf16[512,1024]{1,0:T(8,128)(2,1)} %get-tuple-element.84.refs_2_), channel_id=1, source_target_pairs={{0,16},{16,0},{1,17},{17,1},{2,18},{18,2},{3,19},{19,3},{4,20},{20... | collective-permute-start | bytes 3145736 | tf_op jit(solution)/shard_map/ppermute | solution.py:23
  253.7 13.0 %copy-start.42 = (bf16[512,1024]{1,0:T(8,128)(2,1)}, bf16[512,1024]{1,0:T(8,128)(2,1)S(1)}, u32[]{:S(2)}) copy-start(bf16[512,1024]{1,0:T(8,128)(2,1)S(1)} %collective-permute-done.13.refs_4_) | copy-start | bytes 3145732
  253.7 23.8 %collective-permute-start.14 = (bf16[512,1024]{1,0:T(8,128)(2,1)}, bf16[512,1024]{1,0:T(8,128)(2,1)S(1)}, u32[]{:S(2)}, u32[]{:S(2)}) collective-permute-start(bf16[512,1024]{1,0:T(8,128)(2,1)} %get-tuple-element.85), channel_id=1, source_target_pairs={{0,16},{16,0},{1,17},{17,1},{2,18},{18,2},{3,19},{19,3},{4,20},{20... | collective-permute-start | bytes 3145736 | tf_op jit(solution)/shard_map/ppermute | solution.py:23
  266.7 10.9 %copy-start.44 = (bf16[512,1024]{1,0:T(8,128)(2,1)S(1)}, bf16[512,1024]{1,0:T(8,128)(2,1)}, u32[]{:S(2)}) copy-start(bf16[512,1024]{1,0:T(8,128)(2,1)} %get-tuple-element.86) | copy-start | bytes 3145732
  277.6 41.0 %collective-permute-start.15 = (bf16[512,1024]{1,0:T(8,128)(2,1)S(1)}, bf16[512,1024]{1,0:T(8,128)(2,1)S(1)}, u32[]{:S(2)}, u32[]{:S(2)}) collective-permute-start(bf16[512,1024]{1,0:T(8,128)(2,1)S(1)} %copy-done.44), channel_id=1, source_target_pairs={{0,16},{16,0},{1,17},{17,1},{2,18},{18,2},{3,19},{19,3},{4,20},{20... | collective-permute-start | bytes 3145736 | tf_op jit(solution)/shard_map/ppermute | solution.py:23
  301.2 27.5 %collective-permute-start.18 = (bf16[512,1024]{1,0:T(8,128)(2,1)}, bf16[512,1024]{1,0:T(8,128)(2,1)}, u32[]{:S(2)}, u32[]{:S(2)}) collective-permute-start(bf16[512,1024]{1,0:T(8,128)(2,1)} %get-tuple-element.103.refs_3_), channel_id=1, source_target_pairs={{0,16},{16,0},{1,17},{17,1},{2,18},{18,2},{3,19},{19,3},{4,20},{20... | collective-permute-start | bytes 3145736 | tf_op jit(solution)/shard_map/ppermute | solution.py:23
  302.4 16.2 %copy-start.8 = (bf16[16,32,1024]{2,1,0:T(8,128)(2,1)S(1)}, bf16[16,32,1024]{2,1,0:T(8,128)(2,1)}, u32[]{:S(2)}) copy-start(bf16[16,32,1024]{2,1,0:T(8,128)(2,1)} %copy-done.7) | copy-start | bytes 3145732
  302.4 16.2 %copy-start.12 = (f32[512,1024]{1,0:T(8,128)S(1)}, f32[512,1024]{1,0:T(8,128)}, u32[]{:S(2)}) copy-start(f32[512,1024]{1,0:T(8,128)} %get-tuple-element.76.refs_4_) | copy-start | bytes 6291460
  302.4 16.2 %copy-start.13 = (f32[512,1024]{1,0:T(8,128)S(1)}, f32[512,1024]{1,0:T(8,128)}, u32[]{:S(2)}) copy-start(f32[512,1024]{1,0:T(8,128)} %get-tuple-element.78) | copy-start | bytes 6291460
  318.1 40.8 %collective-permute-start.23 = (bf16[1024,1024]{1,0:T(8,128)(2,1)}, bf16[1024,1024]{1,0:T(8,128)(2,1)}, u32[]{:S(2)}, u32[]{:S(2)}) collective-permute-start(bf16[1024,1024]{1,0:T(8,128)(2,1)} %get-tuple-element.115), channel_id=1, source_target_pairs={{0,1},{1,0},{2,3},{3,2},{4,5},{5,4},{6,7},{7,6},{8,9},{9,8},{10,11... | collective-permute-start | bytes 6291464 | tf_op jit(solution)/shard_map/ppermute | solution.py:23
  318.1 47.3 %collective-permute-start.24 = (bf16[1024,1024]{1,0:T(8,128)(2,1)}, bf16[1024,1024]{1,0:T(8,128)(2,1)}, u32[]{:S(2)}, u32[]{:S(2)}) collective-permute-start(bf16[1024,1024]{1,0:T(8,128)(2,1)} %get-tuple-element.117), channel_id=1, source_target_pairs={{0,1},{1,0},{2,3},{3,2},{4,5},{5,4},{6,7},{7,6},{8,9},{9,8},{10,11... | collective-permute-start | bytes 6291464 | tf_op jit(solution)/shard_map/ppermute | solution.py:23
  321.4 31.3 %all-to-all-start.2 = ((bf16[16,32,1024]{2,1,0:T(8,128)(2,1)}), bf16[16,32,1024]{2,1,0:T(8,128)(2,1)S(1)}, u32[]{:S(2)}, u32[]{:S(2)}) async-start(bf16[16,32,1024]{2,1,0:T(8,128)(2,1)} %bitcast.18), calls=%async_computation.2 | async-start | bytes 2097152 | tf_op jit(solution)/shard_map/all_to_all | solution.py:831
  328.7 22.1 %copy-start.32 = (f32[4,1,512]{2,1,0:T(1,128)S(1)}, f32[4,1,512]{2,1,0:T(1,128)}, u32[]{:S(2)}) copy-start(f32[4,1,512]{2,1,0:T(1,128)} %get-tuple-element.109) | copy-start | bytes 24580
  328.7 23.5 %copy-start.6 = (bf16[16,32,1024]{2,1,0:T(8,128)(2,1)S(1)}, bf16[16,32,1024]{2,1,0:T(8,128)(2,1)}, u32[]{:S(2)}) copy-start(bf16[16,32,1024]{2,1,0:T(8,128)(2,1)} %copy-done.5) | copy-start | bytes 3145732
  328.7 23.8 %copy-start.28 = (f32[8,1024]{1,0:T(8,128)S(1)}, f32[8,1024]{1,0:T(8,128)}, u32[]{:S(2)}) copy-start(f32[8,1024]{1,0:T(8,128)} %get-tuple-element.100) | copy-start | bytes 98308
  351.6 22.1 %collective-permute-start.21 = (bf16[1024,1024]{1,0:T(8,128)(2,1)}, bf16[1024,1024]{1,0:T(8,128)(2,1)}, u32[]{:S(2)}, u32[]{:S(2)}) collective-permute-start(bf16[1024,1024]{1,0:T(8,128)(2,1)} %get-tuple-element.111), channel_id=1, source_target_pairs={{0,1},{1,0},{2,3},{3,2},{4,5},{5,4},{6,7},{7,6},{8,9},{9,8},{10,11... | collective-permute-start | bytes 6291464 | tf_op jit(solution)/shard_map/ppermute | solution.py:23
  352.6 11.8 %collective-permute-start.19 = (f32[7680]{0:T(1024)S(1)}, f32[7680]{0:T(1024)S(1)}, u32[]{:S(2)}, u32[]{:S(2)}) collective-permute-start(f32[7680]{0:T(1024)S(1)} %pad_maximum_fusion), channel_id=1, source_target_pairs={{0,1},{1,0},{2,3},{3,2},{4,5},{5,4},{6,7},{7,6},{8,9},{9,8},{10,11... | collective-permute-start | bytes 92168 | tf_op jit(solution)/shard_map/ppermute | solution.py:23
  352.7 29.0 %all-to-all-start.3 = ((bf16[16,32,1024]{2,1,0:T(8,128)(2,1)}), bf16[16,32,1024]{2,1,0:T(8,128)(2,1)S(1)}, u32[]{:S(2)}, u32[]{:S(2)}) async-start(bf16[16,32,1024]{2,1,0:T(8,128)(2,1)} %bitcast.20), calls=%async_computation.3 | async-start | bytes 2097152 | tf_op jit(solution)/shard_map/all_to_all | solution.py:831
  364.0 26.5 %collective-permute-start.22 = (bf16[1024,1024]{1,0:T(8,128)(2,1)}, bf16[1024,1024]{1,0:T(8,128)(2,1)}, u32[]{:S(2)}, u32[]{:S(2)}) collective-permute-start(bf16[1024,1024]{1,0:T(8,128)(2,1)} %get-tuple-element.113), channel_id=1, source_target_pairs={{0,1},{1,0},{2,3},{3,2},{4,5},{5,4},{6,7},{7,6},{8,9},{9,8},{10,11... | collective-permute-start | bytes 6291464 | tf_op jit(solution)/shard_map/ppermute | solution.py:23
  364.4 6.1 %collective-permute-start.20 = (f32[7680]{0:T(1024)S(1)}, f32[7680]{0:T(1024)S(1)}, u32[]{:S(2)}, u32[]{:S(2)}) collective-permute-start(f32[7680]{0:T(1024)S(1)} %maximum_add_fusion), channel_id=1, source_target_pairs={{0,16},{16,0},{1,17},{17,1},{2,18},{18,2},{3,19},{19,3},{4,20},{20... | collective-permute-start | bytes 92168 | tf_op jit(solution)/shard_map/ppermute | solution.py:23
  384.5 3.6 copy-start.40
  388.1 7.5 %copy-start.14 = (f32[512,1024]{1,0:T(8,128)}, f32[512,1024]{1,0:T(8,128)S(1)}, u32[]{:S(2)}) copy-start(f32[512,1024]{1,0:T(8,128)S(1)} %get-tuple-element.157.refs_4_) | copy-start | bytes 6291460
  389.5 14.5 %collective-permute-start.16 = (bf16[512,512]{1,0:T(8,128)(2,1)S(1)}, bf16[512,512]{1,0:T(8,128)(2,1)S(1)}, u32[]{:S(2)}, u32[]{:S(2)}) collective-permute-start(bf16[512,512]{1,0:T(8,128)(2,1)S(1)} %get-tuple-element.127), channel_id=1, source_target_pairs={{0,16},{16,0},{1,17},{17,1},{2,18},{18,2},{3,19},{19,3},{4,20},{20... | collective-permute-start | bytes 1572872 | tf_op jit(solution)/shard_map/ppermute | solution.py:23
  391.0 4.6 copy-start.18
  391.0 4.6 copy-start.47
  443.7 51.0 %collective-permute-start.17 = (f32[64,1024]{1,0:T(8,128)}, f32[64,1024]{1,0:T(8,128)S(1)}, u32[]{:S(2)}, u32[]{:S(2)}) collective-permute-start(f32[64,1024]{1,0:T(8,128)} %get-tuple-element.99), channel_id=1, source_target_pairs={{0,16},{16,0},{1,17},{17,1},{2,18},{18,2},{3,19},{19,3},{4,20},{20... | collective-permute-start | bytes 786440 | tf_op jit(solution)/shard_map/ppermute | solution.py:23
  444.7 50.0 %copy-start.19 = (f32[64,1024]{1,0:T(8,128)S(1)}, f32[64,1024]{1,0:T(8,128)}, u32[]{:S(2)}) copy-start(f32[64,1024]{1,0:T(8,128)} %get-tuple-element.99) | copy-start | bytes 786436
  495.4 5.4 %copy-start.1 = (bf16[64,1024]{1,0:T(8,128)(2,1)S(1)}, bf16[64,1024]{1,0:T(8,128)(2,1)}, u32[]{:S(2)}) copy-start(bf16[64,1024]{1,0:T(8,128)(2,1)} %param.30) | copy-start | bytes 393220
  495.4 4.0 copy-start.21
  495.4 4.7 copy-start.20
  (15 other events, 27.4 us)
Sparse Core Ops, SparseCore 0:
  10.9 62.5 all-gather.2
  75.7 39.3 all-gather.4
